TPU v7x, 512 devices: a whole 4x4x16 slice. The times are simulated.
512 devices in a mesh: seq: 32 (over z, core), img: 16 (over y, x).
Axes of the slice: x: 4, y: 4, z: 16, core: 2. Of those that a mesh axis runs over, the one named last changes fastest.
Arguments:
- tokens: bfloat16 [16, 96, 128, 2240], P('img', 'seq'), may hold values from -8 to 8
- norm_gain: bfloat16 [2240], replicated, may hold values from 0.099609375 to 1.8984375
- caption: bfloat16 [16, 2240], P('img'), may hold values from -6 to 6
- null_caption: bfloat16 [2240], replicated, may hold values from -6 to 6
- keep: int32 [16], P('img'), may hold values from 0 to 1, as said below
- bucket_rows: int32 [16], P('img'), may hold values from 25 to 96, as said below
- w_qkv: bfloat16 [2240, 3456], P('img', 'seq'), may hold values from -0.125 to 0.125
Outputs:
- attended: bfloat16 [16, 96, 128, 1152], P('img', 'seq')
Inputs may be any that keep to these rules, and one draw needn't show every extreme that they name: `keep`: 1 keeps the image's caption, 0 drops it; some image keeps and some drops. `bucket_rows`: rows in use are the first ones of an image's grid; some image uses all 96 rows.
All inputs are finite; a program needn't handle non-finite values.
Results may differ from a plain program's by a relative error of at most 0.0017.
Values may be sent and summed in bfloat16 or wider, within the bound.
No kernel may reach another device: no remote copies, remote signals or barrier semaphores. Data moves between devices by JAX's collectives and lax.ppermute only.
A program may use at most 128 MiB of HBM per device.

v0:
```python
import jax
import jax.numpy as jnp
from jax import lax
from jax.sharding import PartitionSpec as P

HDIM = 32


norm_eps = 1e-06
attn_eps = 1e-06


def body(tokens, norm_gain, caption, null_caption, keep, bucket_rows, w_qkv):
    grid_rows = tokens.shape[1]
    grid_cols = tokens.shape[2]
    features_count = tokens.shape[3]
    token_count = grid_rows * grid_cols
    features = tokens.reshape(token_count, features_count).astype(jnp.float32)
    mean_square = jnp.mean(features * features, axis=1, keepdims=True)
    condition = jnp.where(keep[0] > 0, caption[0], null_caption).astype(jnp.float32)
    hidden = (
        features * lax.rsqrt(mean_square + norm_eps) * norm_gain.astype(jnp.float32) + condition
    ).astype(jnp.bfloat16)
    rows_whole = lax.all_gather(w_qkv, "img", axis=0, tiled=True)
    projected = jnp.dot(
        hidden,
        lax.all_gather(rows_whole, "seq", axis=1, tiled=True),
        preferred_element_type=jnp.float32,
    )
    inner_width = projected.shape[1] // 3
    head_count = inner_width // HDIM
    grid_row = (
        lax.axis_index("seq") * grid_rows + jnp.arange(token_count, dtype=jnp.int32) // grid_cols
    )
    live_mask = (grid_row < bucket_rows[0]).astype(jnp.float32)
    queries = jax.nn.relu(projected[:, :inner_width]).reshape(token_count, head_count, HDIM)
    keys_relu = jax.nn.relu(projected[:, inner_width : 2 * inner_width]).reshape(
        token_count, head_count, HDIM
    )
    keys_relu = keys_relu * live_mask[:, None, None]
    values = projected[:, 2 * inner_width :].reshape(token_count, head_count, HDIM)
    state_outer = jnp.einsum("thd,the->hde", keys_relu, values, precision=lax.Precision.HIGHEST)
    key_total = jnp.sum(keys_relu, axis=0)
    state_outer, key_total = lax.psum((state_outer, key_total), "seq")
    numerator = jnp.einsum("thd,hde->the", queries, state_outer, precision=lax.Precision.HIGHEST)
    denominator = jnp.einsum("thd,hd->th", queries, key_total, precision=lax.Precision.HIGHEST)
    result = numerator / (denominator[:, :, None] + attn_eps) * live_mask[:, None, None]
    return result.reshape(1, grid_rows, grid_cols, inner_width).astype(jnp.bfloat16)


def solution(mesh):
    in_specs = (
        P("img", "seq", None, None),
        P(),
        P("img", None),
        P(),
        P("img"),
        P("img"),
        P("img", "seq"),
    )
    out_specs = P("img", "seq", None, None)
    return jax.shard_map(body, mesh=mesh, in_specs=in_specs, out_specs=out_specs, check_vma=False)
```

profile of v0, /device:TPU:1, one launch (start us, length us, event | category | flops | bytes accessed | tf_op | source)
XLA Modules:
  0.0 392.8 jit_solution(5974640022013583326)
XLA Ops:
  6.5 20.1 %all-gather = bf16[16,140,108]{2,1,0:T(8,128)(2,1)S(1)} all-gather(bf16[1,140,108]{2,1,0:T(8,128)(2,1)} %bitcast.47), channel_id=1, replica_groups=mesh['seq'=32,'img'=16] {'img'}, dimensions={0}, use_global_device_ids=true | all-gather | bytes 514080 | tf_op jit(solution)/shard_map/all_gather | solution.py:24
  26.6 0.2 reshape.71
  26.8 1.1 copy.18
  28.6 2.6 copy.17
  31.9 0.7 convert_element_type.42
  32.6 1.3 reduce.2
  33.9 1.8 multiply_reduce_fusion
  35.7 0.7 select_convert_fusion
  36.4 1.7 fusion.2
  38.2 103.2 %all-gather.4.cloned.1.call-done = bf16[32,108,2240]{2,1,0:T(8,128)(2,1)} async-done(((bf16[1,108,2240]{2,1,0:T(8,128)(2,1)}), bf16[32,108,2240]{2,1,0:T(8,128)(2,1)}) %all-gather.4.cloned.1.call-update) | async-done | bytes 15482896 | tf_op jit(solution)/shard_map/all_gather | solution.py:27
  141.3 19.5 %reshape.73 = bf16[3456,2240]{1,0:T(8,128)(2,1)} reshape(bf16[32,108,2240]{2,1,0:T(8,128)(2,1)} %all-gather.4.cloned.1.call-done) | data formatting | bytes 30965760
  160.8 10.4 %fusion.17 = f32[384,3456]{1,0:T(8,128)S(1)} fusion(bf16[384,2240]{1,0:T(8,128)(2,1)S(1)} %copy-done, bf16[3456,2240]{1,0:T(8,128)(2,1)} %reshape.73), kind=kOutput, calls=%fused_computation.30 | convolution fusion | flops 5945425920 | bytes 22511616 | tf_op jit(solution)/shard_map/dot_general | solution.py:25
  171.2 2.2 multiply_reduce_fusion.1
  173.4 1.2 copy.19
  174.5 2.2 copy.20
  176.7 3.0 fusion.5
  179.8 2.2 copy.21
  182.0 0.1 reduce_sum.22
  182.0 88.2 %psum.15 = f32[36,32]{1,0:T(8,128)S(1)} all-reduce(f32[36,32]{1,0:T(8,128)S(1)} %reduce_sum.22), channel_id=1, replica_groups=mesh['seq'=32,'img'=16] {'seq'}, use_global_device_ids=true, to_apply=%region_3.4 | all-reduce | flops 1152 | bytes 9216 | tf_op jit(solution)/shard_map/psum | solution.py:44
  270.3 1.1 fusion.9
  271.4 109.5 %all-reduce.2.cloned.1.call-done = f32[36,32,32]{2,1,0:T(8,128)} async-done(((f32[36,32,32]{2,1,0:T(8,128)}), f32[36,32,32]{2,1,0:T(8,128)}) %all-reduce.2.cloned.1.call-update) | async-done | bytes 147472 | tf_op jit(solution)/shard_map/psum | solution.py:44
  380.9 2.8 fusion.4
  383.7 0.3 convert_element_type.47
  384.0 1.9 copy.23
  (9 shorter events, 0.1 us)
Async XLA Ops:
  6.5 134.8 %all-gather.4.cloned.1.call-start = ((), (), s32[]{:S(2)}) async-start(), calls=%async_computation.1 | async-start | bytes 17031168 | tf_op jit(solution)/shard_map/all_gather | solution.py:27
  27.9 353.0 %all-reduce.2.cloned.1.call-start = ((), (), s32[]{:S(2)}) async-start(), calls=%async_computation | async-start | bytes 1179648 | tf_op jit(solution)/shard_map/psum | solution.py:44
  38.2 122.7 %copy-start = (bf16[384,2240]{1,0:T(8,128)(2,1)S(1)}, bf16[384,2240]{1,0:T(8,128)(2,1)}, u32[]{:S(2)}) copy-start(bf16[384,2240]{1,0:T(8,128)(2,1)} %fusion.2) | copy-start | bytes 5160964
Sparse Core Ops, SparseCore 0:
  28.0 113.2 all-gather.3
  179.9 200.9 all-reduce.1
where the time goes:
time: 394 us; the launch traced here: 393 us
  waiting for transfers between devices  213 us (54%)
  blocking collectives  108 us (27%)
  local copies, waits for them, and re-layouts  31.2 us (8%)
  matrix products  17.3 us (4%)
  between operations  14.8 us (4%)
  other arithmetic  8.47 us (2%)
    psum x1, waiting for transfers between devices, body(): state_outer, key_total = lax.psum((state_outer, key_total), 'seq')  109 us
    all_gather x1, waiting for transfers between devices, body(): lax.all_gather(rows_whole, 'seq', axis=1, tiled=True)  103 us
    psum x1, blocking collectives, body(): state_outer, key_total = lax.psum((state_outer, key_total), 'seq')  88.2 us
    unnamed x5, local copies, waits for them, and re-layouts  20.8 us
    all_gather x1, blocking collectives, body(): rows_whole = lax.all_gather(w_qkv, 'img', axis=0, tiled=True)  20.1 us
    dot_general x1, matrix products, body(): jnp.dot(hidden, lax.all_gather(rows_whole, 'seq', axis=1, tiled=True), pr...  10.4 us
  transfers between devices with their start and end apart: 2, of which 2 were waited for; matrix products, arithmetic and copies ran while one was open for 3% of the time, Pallas kernels for 0%

commit v1 on v0

v1 whole, which is shorter than its diff:
```python
import functools

import jax
import jax.numpy as jnp
from jax import lax
from jax.experimental import pallas as pl
from jax.experimental.pallas import tpu as pltpu
from jax.sharding import PartitionSpec as P

HDIM = 32
LANES = 128
GROUP = LANES // HDIM

norm_eps = 1e-06
attn_eps = 1e-06
HIGHEST = lax.Precision.HIGHEST


def block_mask():
    row = lax.broadcasted_iota(jnp.int32, (LANES, LANES), 0) // HDIM
    col = lax.broadcasted_iota(jnp.int32, (LANES, LANES), 1) // HDIM
    return row == col


def live_rows(live_ref, tokens_per_core):
    token = lax.broadcasted_iota(jnp.int32, (2 * tokens_per_core, LANES), 0)
    limit = jnp.where(
        token < tokens_per_core, live_ref[0], live_ref[1] + tokens_per_core
    )
    return (token < limit).astype(jnp.float32)


def state_kernel(live_ref, mine_ref, other_ref, w_ref, out_ref, proj_ref):
    step = pl.program_id(0)
    tokens_per_core = mine_ref.shape[0]
    width = w_ref.shape[2]
    weights = w_ref[...].reshape(-1, width)
    at = pl.multiple_of(step * width, LANES)
    proj_ref[:tokens_per_core, pl.ds(at, width)] = jnp.dot(
        mine_ref[...], weights, preferred_element_type=jnp.float32
    )
    proj_ref[tokens_per_core:, pl.ds(at, width)] = jnp.dot(
        other_ref[...], weights, preferred_element_type=jnp.float32
    )

    @pl.when(step == pl.num_programs(0) - 1)
    def _():
        live = live_rows(live_ref, tokens_per_core)
        same_head = block_mask()
        full = proj_ref.shape[1] // LANES // 2
        chunks = out_ref.shape[0]
        rows = HDIM // chunks
        tiles = full + 1
        out_ref[...] = jnp.zeros_like(out_ref)
        for tile in range(tiles):
            if tile < full:
                keys = proj_ref[:, tile * LANES : (tile + 1) * LANES]
                values = proj_ref[:, (full + tile) * LANES : (full + tile + 1) * LANES]
                keep = same_head
            else:
                keys = proj_ref[:, 2 * full * LANES :]
                values = pltpu.roll(keys, LANES // 2, 1)
                half = lax.broadcasted_iota(jnp.int32, (LANES, LANES), 1) < LANES // 2
                keep = jnp.logical_and(same_head, half)
            keys = jnp.maximum(keys, 0.0) * live
            outer = lax.dot_general(
                keys,
                values,
                (((0,), (0,)), ((), ())),
                precision=HIGHEST,
                preferred_element_type=jnp.float32,
            )
            outer = jnp.where(keep, outer, 0.0)
            packed = outer[:HDIM]
            for head in range(1, GROUP):
                packed = packed + outer[head * HDIM : (head + 1) * HDIM]
            total = jnp.sum(keys, axis=0, keepdims=True)
            for chunk in range(chunks):
                for row in range(rows):
                    source = chunk * rows + row
                    target = row * tiles + tile
                    out_ref[chunk, target : target + 1, :] = packed[source : source + 1]
                target = rows * tiles + tile
                out_ref[chunk, target : target + 1, :] = total


def attend_kernel(live_ref, mine_ref, other_ref, w_ref, state_ref, own_ref, far_ref):
    tokens_per_core = mine_ref.shape[0]
    width = w_ref.shape[2]
    tiles = width // LANES
    chunks = state_ref.shape[0]
    rows = HDIM // chunks
    weights = w_ref[...].reshape(-1, width)
    live = live_rows(live_ref, tokens_per_core)
    same_head = block_mask()
    ones = same_head.astype(jnp.float32)
    for hidden_ref, result_ref, first in (
        (mine_ref, own_ref, 0),
        (other_ref, far_ref, tokens_per_core),
    ):
        queries = jnp.maximum(
            jnp.dot(hidden_ref[...], weights, preferred_element_type=jnp.float32), 0.0
        )
        for tile in range(tiles):
            query = queries[:, tile * LANES : (tile + 1) * LANES]
            packed = jnp.concatenate(
                [
                    state_ref[chunk, row * tiles + tile : row * tiles + tile + 1, :]
                    for chunk in range(chunks)
                    for row in range(rows)
                ],
                axis=0,
            )
            state = jnp.where(same_head, jnp.concatenate([packed] * GROUP, axis=0), 0.0)
            total = state_ref[0, rows * tiles + tile : rows * tiles + tile + 1, :]
            numerator = jnp.dot(
                query, state, precision=HIGHEST, preferred_element_type=jnp.float32
            )
            denominator = jnp.dot(
                query * total, ones, precision=HIGHEST, preferred_element_type=jnp.float32
            )
            result = numerator / (denominator + attn_eps)
            result = result * live[first : first + tokens_per_core]
            result_ref[:, tile * LANES : (tile + 1) * LANES] = result.astype(jnp.bfloat16)


def compute_state(live, mine, other, weights, chunks):
    images, depth, width = weights.shape
    tokens_per_core, contraction = mine.shape
    steps = 3
    block = width // steps
    tiles = width // LANES // 2 + 1
    slots = -(-(HDIM // chunks + 1) * tiles // 8) * 8
    whole = pl.BlockSpec((tokens_per_core, contraction), lambda i: (0, 0))
    return pl.pallas_call(
        state_kernel,
        grid=(steps,),
        in_specs=[
            pl.BlockSpec(memory_space=pltpu.SMEM),
            whole,
            whole,
            pl.BlockSpec((images, depth, block), lambda i: (0, 0, i)),
        ],
        out_specs=pl.BlockSpec((chunks, slots, LANES), lambda i: (0, 0, 0)),
        out_shape=jax.ShapeDtypeStruct((chunks, slots, LANES), jnp.float32),
        scratch_shapes=[pltpu.VMEM((2 * tokens_per_core, width), jnp.float32)],
        compiler_params=pltpu.CompilerParams(vmem_limit_bytes=48 * 1024 * 1024),
        name="state",
    )(live, mine, other, weights)


def compute_output(live, mine, other, weights, state):
    tokens_per_core = mine.shape[0]
    width = weights.shape[2]
    result = jax.ShapeDtypeStruct((tokens_per_core, width), jnp.bfloat16)
    vmem = pl.BlockSpec(memory_space=pltpu.VMEM)
    return pl.pallas_call(
        attend_kernel,
        in_specs=[pl.BlockSpec(memory_space=pltpu.SMEM), vmem, vmem, vmem, vmem],
        out_specs=[vmem, vmem],
        out_shape=[result, result],
        compiler_params=pltpu.CompilerParams(vmem_limit_bytes=48 * 1024 * 1024),
        name="attend",
    )(live, mine, other, weights, state)


def body(tokens, norm_gain, caption, null_caption, keep, bucket_rows, w_qkv):
    grid_rows, grid_cols, features_count = tokens.shape[1:]
    token_count = grid_rows * grid_cols
    seq_size = lax.axis_size("seq")
    img_size = lax.axis_size("img")
    chips = seq_size // 2
    seq_at = lax.axis_index("seq")
    core = seq_at % 2
    swap = [(s, s ^ 1) for s in range(seq_size)]
    same_core = [[2 * z + c for z in range(chips)] for c in range(2)]
    depth = features_count // img_size
    padded = -(-depth // 16) * 16
    columns = w_qkv.shape[1] * seq_size
    inner = columns // 3
    half = inner // 2
    main = half // LANES * LANES
    rest = half - main

    gathered = lax.all_gather(w_qkv, "seq", axis=0)
    rows = jnp.transpose(gathered, (1, 0, 2)).reshape(depth, columns)
    rows = jnp.pad(rows, ((0, padded - depth), (0, 0)))

    def pick(part):
        low = rows[:, part * inner : part * inner + half]
        high = rows[:, part * inner + half : (part + 1) * inner]
        return jnp.where(core == 0, low, high)

    query_cols, key_cols, value_cols = pick(0), pick(1), pick(2)
    pair = jnp.concatenate(
        [key_cols[:, :main], value_cols[:, :main], key_cols[:, main:], value_cols[:, main:]],
        axis=1,
    )
    query_cols = jnp.pad(query_cols, ((0, 0), (0, LANES - rest)))
    pair_weights = lax.all_gather(pair, "img", axis=0)
    query_weights = lax.all_gather(query_cols, "img", axis=0)

    features = jnp.transpose(tokens[0], (0, 2, 1)).astype(jnp.float32)
    mean_square = jnp.mean(features * features, axis=1, keepdims=True)
    condition = jnp.where(keep[0] > 0, caption[0], null_caption).astype(jnp.float32)
    hidden = (
        features * lax.rsqrt(mean_square + norm_eps) * norm_gain.astype(jnp.float32)[None, :, None]
        + condition[None, :, None]
    ).astype(jnp.bfloat16)
    hidden = hidden.reshape(grid_rows, img_size, depth, grid_cols)
    hidden = jnp.pad(hidden, ((0, 0), (0, 0), (0, padded - depth), (0, 0)))
    hidden = hidden.reshape(grid_rows, img_size * padded, grid_cols)
    mine = jnp.transpose(hidden, (0, 2, 1)).reshape(token_count, img_size * padded)
    other = lax.ppermute(mine, "seq", swap)

    first_row = jnp.stack([seq_at, seq_at ^ 1]) * grid_rows
    live = jnp.clip(bucket_rows[0] - first_row, 0, grid_rows) * grid_cols

    part = compute_state(live, mine, other, pair_weights, chips)
    part = lax.all_to_all(part, "seq", 0, 0, axis_index_groups=same_core)
    part = jnp.sum(part, axis=0)
    part = jnp.broadcast_to(part[None], (chips,) + part.shape)
    state = lax.all_to_all(part, "seq", 0, 0, axis_index_groups=same_core)

    own, far = compute_output(live, mine, other, query_weights, state)
    back = lax.ppermute(far, "seq", swap)
    own, back = own[:, :half], back[:, :half]
    result = jnp.where(
        core == 0,
        jnp.concatenate([own, back], axis=1),
        jnp.concatenate([back, own], axis=1),
    )
    return result.reshape(1, grid_rows, grid_cols, inner)


def solution(mesh):
    in_specs = (
        P("img", "seq", None, None),
        P(),
        P("img", None),
        P(),
        P("img"),
        P("img"),
        P("img", "seq"),
    )
    out_specs = P("img", "seq", None, None)
    return jax.shard_map(body, mesh=mesh, in_specs=in_specs, out_specs=out_specs, check_vma=False)
```

time: 394 us -> 205 us (0.52)
  waiting for transfers between devices: 213 us -> 85.2 us
  blocking collectives: 108 us -> 64.9 us
  local copies, waits for them, and re-layouts: 31.2 us -> 6.46 us
  matrix products: 17.3 us -> 0 us
  Pallas kernels: 0 us -> 17.3 us
  starting transfers between devices: 0.04 us -> 11.4 us
    psum x1 -> x0, waiting for transfers between devices: 109 us -> none  [body(): state_outer, key_total = lax.psum((state_outer, key_total), 'seq')]
    psum x1 -> x0, blocking collectives: 88.2 us -> none  [body(): state_outer, key_total = lax.psum((state_outer, key_total), 'seq')]
    all_to_all x0 -> x1, blocking collectives: none -> 23.9 us  [body(): part = lax.all_to_all(part, 'seq', 0, 0, axis_index_groups=same_core)]
    all_gather x1 -> x2, waiting for transfers between devices: 103 us -> 80.9 us  [the longest x1 57 us: body(): pair_weights = lax.all_gather(pair, 'img', axis=0)]
    all_gather x1, blocking collectives: 20.1 us -> 41 us  [body(): gathered = lax.all_gather(w_qkv, 'seq', axis=0)]
    unnamed x5 -> x8, local copies, waits for them, and re-layouts: 20.8 us -> 0.02 us
    pallas_call x0 -> x2, Pallas kernels: none -> 17.3 us  [the longest x1 9.4 us: compute_state(): pl.pallas_call(state_kernel, grid=(steps,), in_specs=[pl.BlockSpec(memory...]
    dot_general x4 -> x0, matrix products: 17.3 us -> none  [the longest x1 10.4 us: body(): jnp.dot(hidden, lax.all_gather(rows_whole, 'seq', axis=1, tiled=True), pr...]
  transfers between devices with their start and end apart: 2 -> 5, of which waited for: 2 -> 4; matrix products, arithmetic and copies ran while one was open for 3% -> 3% of each run, Pallas kernels for 0% -> 5%
where the time goes in v1:
time: 205 us
  waiting for transfers between devices  85.2 us (42%)
  blocking collectives  64.9 us (32%)
  Pallas kernels  17.3 us (8%)
  between operations  14.9 us (7%)
  starting transfers between devices  11.4 us (6%)
  local copies, waits for them, and re-layouts  6.46 us (3%)
  other arithmetic  4.57 us (2%)
    all_gather x1, waiting for transfers between devices, body(): pair_weights = lax.all_gather(pair, 'img', axis=0)  57 us
    all_gather x1, blocking collectives, body(): gathered = lax.all_gather(w_qkv, 'seq', axis=0)  41 us
    all_to_all x1, blocking collectives, body(): part = lax.all_to_all(part, 'seq', 0, 0, axis_index_groups=same_core)  23.9 us
    all_gather x1, waiting for transfers between devices, body(): query_weights = lax.all_gather(query_cols, 'img', axis=0)  23.9 us
    pallas_call x1, Pallas kernels, compute_state(): pl.pallas_call(state_kernel, grid=(steps,), in_specs=[pl.BlockSpec(memory...  9.4 us
    pallas_call x1, Pallas kernels, compute_output(): pl.pallas_call(attend_kernel, in_specs=[pl.BlockSpec(memory_space=pltpu.S...  7.94 us
    all_to_all x1, starting transfers between devices, body(): state = lax.all_to_all(part, 'seq', 0, 0, axis_index_groups=same_core)  6.03 us
  transfers between devices with their start and end apart: 5, of which 4 were waited for; matrix products, arithmetic and copies ran while one was open for 3% of the time, Pallas kernels for 5%

profile of v1, /device:TPU:1, one launch (start us, length us, event | category | flops | bytes accessed | tf_op | source)
XLA Modules:
  0.0 204.7 jit_solution(5381291726040236468)
XLA Ops:
  6.5 41.0 %all-gather.3 = bf16[32,140,108]{2,1,0:T(8,128)(2,1)S(1)} all-gather(bf16[1,140,108]{2,1,0:T(8,128)(2,1)} %bitcast.32), channel_id=2, replica_groups=mesh['seq'=32,'img'=16] {'seq'}, dimensions={0}, use_global_device_ids=true | all-gather | bytes 997920 | tf_op jit(solution)/shard_map/all_gather | solution.py:185
  47.5 0.3 copy.12
  47.8 2.5 %reshape.86 = bf16[140,3456]{1,0:T(8,128)(2,1)S(1)} reshape(bf16[140,32,108]{2,1,0:T(8,128)(2,1)S(1)} %copy.12) | data formatting | bytes 1935360 | tf_op jit(solution)/shard_map/reshape | solution.py:186
  50.4 0.3 fusion.7
  50.8 0.8 concatenate.27
  51.7 0.7 pad.14
  53.1 0.3 fusion
  53.5 1.3 fusion.4
  54.8 0.4 reshape.83
  55.2 0.1 pad.12
  55.4 0.9 copy.11
  56.3 2.1 %collective-permute-start = (bf16[384,2304]{1,0:T(8,128)(2,1)S(1)}, bf16[384,2304]{1,0:T(8,128)(2,1)S(1)}, u32[]{:S(2)}, u32[]{:S(2)}) collective-permute-start(bf16[384,2304]{1,0:T(8,128)(2,1)S(1)} %bitcast.23), channel_id=1, source_target_pairs={{0,16},{16,0},{32,48},{48,32},{64,80},{80,64},{96,112},{112,96},{1... | collective-permute-start | bytes 5308424 | tf_op jit(solution)/shard_map/ppermute | solution.py:214
  59.1 2.8 %collective-permute-done.other_ref = bf16[384,2304]{1,0:T(8,128)(2,1)S(1)} collective-permute-done((bf16[384,2304]{1,0:T(8,128)(2,1)S(1)}, bf16[384,2304]{1,0:T(8,128)(2,1)S(1)}, u32[]{:S(2)}, u32[]{:S(2)}) %collective-permute-start) | collective-permute-done | bytes 1769504 | tf_op jit(solution)/shard_map/ppermute | solution.py:214
  61.8 57.0 %all-gather.9.cloned.1.call-done = bf16[2304,1152]{1,0:T(8,128)(2,1)} async-done(((bf16[144,1152]{1,0:T(8,128)(2,1)}), bf16[2304,1152]{1,0:T(8,128)(2,1)}) %all-gather.9.cloned.1.call-update) | async-done | bytes 5308432 | tf_op jit(solution)/shard_map/all_gather | solution.py:200
  118.9 9.4 %state.1 = f32[16,16,128]{2,1,0:T(8,128)S(1)} custom-call(s32[2]{0:T(128)S(1)} %clamp_multiply_fusion.live_ref, bf16[384,2304]{1,0:T(8,128)(2,1)S(1)} %bitcast.24, bf16[384,2304]{1,0:T(8,128)(2,1)S(1)} %collective-permute-done.other_ref, bf16[16,144,1152]{2,1,0:T(8,128)(2,1)} %bitcast.28), custom_call_target="tpu_custom_call" | custom-call | tf_op jit(solution)/shard_map/state/pallas_call | solution.py:135
  128.3 23.9 %all_to_all.10 = f32[16,16,128]{2,1,0:T(8,128)} all-to-all(f32[16,16,128]{2,1,0:T(8,128)S(1)} %state.1), channel_id=1, replica_groups={{0,32,64,96,128,160,192,224,256,288,320,352,384,416,448,480},{16,48,80,..., dimensions={0} | all-to-all | bytes 262144 | tf_op jit(solution)/shard_map/all_to_all | solution.py:220
  152.2 0.9 reduce_sum.19
  153.1 0.7 broadcast_in_dim.2
  153.8 6.0 %all-to-all-start.1 = ((f32[16,16,128]{2,1,0:T(8,128)}), f32[16,16,128]{2,1,0:T(8,128)}, u32[]{:S(2)}, u32[]{:S(2)}) async-start(f32[16,16,128]{2,1,0:T(8,128)} %broadcast_in_dim.2), calls=%async_computation.1 | async-start | bytes 262144 | tf_op jit(solution)/shard_map/all_to_all | solution.py:223
  159.8 23.9 %all-gather.7.cloned.1.call-done = bf16[2304,640]{1,0:T(8,128)(2,1)} async-done(((bf16[144,640]{1,0:T(8,128)(2,1)}), bf16[2304,640]{1,0:T(8,128)(2,1)}) %all-gather.7.cloned.1.call-update) | async-done | bytes 2949136 | tf_op jit(solution)/shard_map/all_gather | solution.py:201
  183.7 7.9 %attend.1 = (bf16[384,640]{1,0:T(8,128)(2,1)S(1)}, bf16[384,640]{1,0:T(8,128)(2,1)S(1)}) custom-call(s32[2]{0:T(128)S(1)} %clamp_multiply_fusion.live_ref, bf16[384,2304]{1,0:T(8,128)(2,1)S(1)} %bitcast.25, bf16[384,2304]{1,0:T(8,128)(2,1)S(1)} %collective-permute-done.other_ref, bf16[16,144,640]{2,1,0:T(8,128)(2,1)} %bitcast.30, ...), custom_call_target="tpu_custom_call" | custom-call | tf_op jit(solution)/shard_map/attend/pallas_call | solution.py:157
  191.6 3.2 %collective-permute-start.1 = (bf16[384,640]{1,0:T(8,128)(2,1)S(1)}, bf16[384,640]{1,0:T(8,128)(2,1)S(1)}, u32[]{:S(2)}, u32[]{:S(2)}) collective-permute-start(bf16[384,640]{1,0:T(8,128)(2,1)S(1)} %get-tuple-element.8), channel_id=1, source_target_pairs={{0,16},{16,0},{32,48},{48,32},{64,80},{80,64},{96,112},{112,96},{1... | collective-permute-start | bytes 1474568 | tf_op jit(solution)/shard_map/ppermute | solution.py:226
  194.9 1.5 collective-permute-done.1
  196.3 1.5 maximum_select_fusion
  (22 shorter events, 0.3 us)
Async XLA Ops:
  6.5 112.4 %all-gather.9.cloned.1.call-start = ((), (), s32[]{:S(2)}) async-start(), calls=%async_computation.3 | async-start | bytes 5640192 | tf_op jit(solution)/shard_map/all_gather | solution.py:200
  50.4 2.7 %copy-start.2 = (bf16[2240]{0:T(1024)(128)(2,1)S(1)}, bf16[2240]{0:T(1024)(128)(2,1)}, u32[]{:S(2)}) copy-start(bf16[2240]{0:T(1024)(128)(2,1)} %param.8) | copy-start | bytes 13444
  50.4 2.7 %copy-start.1 = (bf16[1,2240]{1,0:T(2,128)(2,1)S(1)}, bf16[1,2240]{1,0:T(2,128)(2,1)}, u32[]{:S(2)}) copy-start(bf16[1,2240]{1,0:T(2,128)(2,1)} %param.9) | copy-start | bytes 13444
  50.4 2.7 %copy-start = (bf16[1,3,128,2240]{2,3,1,0:T(8,128)(2,1)S(1)}, bf16[1,3,128,2240]{2,3,1,0:T(8,128)(2,1)}, u32[]{:S(2)}) copy-start(bf16[1,3,128,2240]{2,3,1,0:T(8,128)(2,1)} %param.7) | copy-start | bytes 5160964
  50.7 2.8 %copy-start.3 = (bf16[2240]{0:T(1024)(128)(2,1)S(1)}, bf16[2240]{0:T(1024)(128)(2,1)}, u32[]{:S(2)}) copy-start(bf16[2240]{0:T(1024)(128)(2,1)} %param.10) | copy-start | bytes 13444
  51.6 132.1 %all-gather.7.cloned.1.call-start = ((), (), s32[]{:S(2)}) async-start(), calls=%async_computation.2 | async-start | bytes 3133440 | tf_op jit(solution)/shard_map/all_gather | solution.py:201
  56.3 5.6 %collective-permute-start = (bf16[384,2304]{1,0:T(8,128)(2,1)S(1)}, bf16[384,2304]{1,0:T(8,128)(2,1)S(1)}, u32[]{:S(2)}, u32[]{:S(2)}) collective-permute-start(bf16[384,2304]{1,0:T(8,128)(2,1)S(1)} %bitcast.23), channel_id=1, source_target_pairs={{0,16},{16,0},{32,48},{48,32},{64,80},{80,64},{96,112},{112,96},{1... | collective-permute-start | bytes 5308424 | tf_op jit(solution)/shard_map/ppermute | solution.py:214
  153.8 29.9 %all-to-all-start.1 = ((f32[16,16,128]{2,1,0:T(8,128)}), f32[16,16,128]{2,1,0:T(8,128)}, u32[]{:S(2)}, u32[]{:S(2)}) async-start(f32[16,16,128]{2,1,0:T(8,128)} %broadcast_in_dim.2), calls=%async_computation.1 | async-start | bytes 262144 | tf_op jit(solution)/shard_map/all_to_all | solution.py:223
  191.6 4.7 %collective-permute-start.1 = (bf16[384,640]{1,0:T(8,128)(2,1)S(1)}, bf16[384,640]{1,0:T(8,128)(2,1)S(1)}, u32[]{:S(2)}, u32[]{:S(2)}) collective-permute-start(bf16[384,640]{1,0:T(8,128)(2,1)S(1)} %get-tuple-element.8), channel_id=1, source_target_pairs={{0,16},{16,0},{32,48},{48,32},{64,80},{80,64},{96,112},{112,96},{1... | collective-permute-start | bytes 1474568 | tf_op jit(solution)/shard_map/ppermute | solution.py:226
Sparse Core Ops, SparseCore 0:
  51.7 67.1 all-gather.8
  121.9 61.7 all-gather.6

commit v2 on v0

v2 whole, which is shorter than its diff:
```python
import jax
import jax.numpy as jnp
import numpy as np
from jax import lax
from jax.experimental import pallas as pl
from jax.experimental.pallas import tpu as pltpu
from jax.sharding import PartitionSpec as P


HDIM = 32
LANES = 128
GROUP = LANES // HDIM
TEAM = 4

norm_eps = 1e-06
attn_eps = 1e-06
HIGHEST = lax.Precision.HIGHEST

VMEM = pl.BlockSpec(memory_space=pltpu.VMEM)
SMEM = pl.BlockSpec(memory_space=pltpu.SMEM)
HBM = pl.BlockSpec(memory_space=pltpu.HBM)
PARAMS = pltpu.CompilerParams(vmem_limit_bytes=58 * 1024 * 1024)

FAR_MASKS = np.array([0] * 4 + [1] * 4 + [3] * 4 + [2] * 4)
NEAR_SLOTS = np.array([0, 1, 2, 3] * 3 + [0, 1] + [2, 3])


def block_mask():
    row = lax.broadcasted_iota(jnp.int32, (LANES, LANES), 0) // HDIM
    col = lax.broadcasted_iota(jnp.int32, (LANES, LANES), 1) // HDIM
    return row == col


def live_rows(limit, tokens):
    token = lax.broadcasted_iota(jnp.int32, (tokens, LANES), 0)
    return (token < limit).astype(jnp.float32)


def load_blocks(place_ref, base, pieces, start, into_ref, sems):
    depth, width = pieces[0].shape[1], into_ref.shape[1]
    copies = []
    for piece in pieces:
        for at in range(piece.shape[0]):
            count = len(copies)
            row = pl.multiple_of(place_ref[base + count] * depth, 16)
            copies.append(
                pltpu.make_async_copy(
                    piece.at[at, :, pl.ds(start, width)],
                    into_ref.at[pl.ds(row, depth), :],
                    sems.at[count],
                )
            )
    for copy in copies:
        copy.start()
    return copies


def load_hidden(hidden, into_ref, sems):
    copies = [
        pltpu.make_async_copy(ref, into_ref.at[at], sems.at[at])
        for at, ref in enumerate(hidden)
    ]
    for copy in copies:
        copy.start()
    return copies


def state_kernel(place_ref, live_ref, *refs):
    hidden, refs = refs[:TEAM], refs[TEAM:]
    first, second, refs = refs[:5], refs[5:10], refs[10:]
    out_ref, keys_ref, values_ref, pair_w, mixed_w, hidden_ref, pair_s, mixed_s, hidden_s = refs
    tokens = hidden_ref.shape[1]
    full = values_ref.shape[1] // LANES
    pair_copies = load_blocks(place_ref, 0, first, 0, pair_w, pair_s)
    hidden_copies = load_hidden(hidden, hidden_ref, hidden_s)
    mixed_copies = load_blocks(place_ref, 16, second, full * LANES, mixed_w, mixed_s)
    for copy in pair_copies:
        copy.wait()
    wide = full * LANES
    for at in range(TEAM):
        hidden_copies[at].wait()
        rows = slice(at * tokens, (at + 1) * tokens)
        block = hidden_ref[at]
        live = live_rows(live_ref[at], tokens)
        keys = jnp.dot(block, pair_w[:, :wide], preferred_element_type=jnp.float32)
        for tile in range(full):
            lanes = slice(tile * LANES, (tile + 1) * LANES)
            keys_ref[rows, lanes] = jnp.maximum(keys[:, lanes], 0.0) * live
        values_ref[rows, :] = jnp.dot(
            block, pair_w[:, wide:], preferred_element_type=jnp.float32
        )
        if at == 0:
            for copy in mixed_copies:
                copy.wait()
        keys_ref[rows, wide:] = jnp.dot(
            block, mixed_w[...], preferred_element_type=jnp.float32
        )
    same_head = block_mask()
    column = lax.broadcasted_iota(jnp.int32, (LANES, LANES), 1)
    chunks = out_ref.shape[0]
    rows = HDIM // chunks
    tiles = full + 1
    out_ref[...] = jnp.zeros_like(out_ref)
    for tile in range(tiles):
        keys = keys_ref[:, tile * LANES : (tile + 1) * LANES]
        if tile < full:
            values = values_ref[:, tile * LANES : (tile + 1) * LANES]
            keep = same_head
        else:
            values = pltpu.roll(keys, LANES - HDIM, 1)
            live = jnp.concatenate(
                [live_rows(live_ref[at], tokens) for at in range(TEAM)], axis=0
            )
            keys = jnp.maximum(keys, 0.0) * live
            keep = jnp.logical_and(same_head, column < HDIM)
        outer = lax.dot_general(
            keys,
            values,
            (((0,), (0,)), ((), ())),
            precision=HIGHEST,
            preferred_element_type=jnp.float32,
        )
        outer = jnp.where(keep, outer, 0.0)
        packed = outer[:HDIM]
        for head in range(1, GROUP):
            packed = packed + outer[head * HDIM : (head + 1) * HDIM]
        total = jnp.sum(keys, axis=0, keepdims=True)
        for chunk in range(chunks):
            for row in range(rows):
                source = chunk * rows + row
                target = row * tiles + tile
                out_ref[chunk, target : target + 1, :] = packed[source : source + 1]
            target = rows * tiles + tile
            out_ref[chunk, target : target + 1, :] = total


def query_kernel(place_ref, *refs):
    hidden, refs = refs[:TEAM], refs[TEAM:]
    second, refs = refs[:5], refs[5:]
    out_ref, weights_ref, hidden_ref, sems, hidden_s = refs
    tokens = hidden_ref.shape[1]
    copies = load_blocks(place_ref, 16, second, 0, weights_ref, sems)
    hidden_copies = load_hidden(hidden, hidden_ref, hidden_s)
    for copy in copies:
        copy.wait()
    for at in range(TEAM):
        hidden_copies[at].wait()
        rows = slice(at * tokens, (at + 1) * tokens)
        queries = jnp.dot(
            hidden_ref[at], weights_ref[...], preferred_element_type=jnp.float32
        )
        edge = out_ref.shape[1] - LANES
        out_ref[rows, :edge] = jnp.maximum(queries[:, :edge], 0.0)
        out_ref[rows, edge:] = jnp.maximum(
            pltpu.roll(queries[:, edge:], LANES - 2 * HDIM, 1), 0.0
        )


def attend_kernel(slot_ref, live_ref, query_ref, state_ref, out_ref):
    tokens = query_ref.shape[0]
    tiles = query_ref.shape[1] // LANES
    chunks = state_ref.shape[0]
    rows = HDIM // chunks
    live = live_rows(live_ref[pl.program_id(0)], tokens)
    same_head = block_mask()
    ones = same_head.astype(jnp.float32)
    for tile in range(tiles):
        query = query_ref[:, tile * LANES : (tile + 1) * LANES]
        packed = jnp.concatenate(
            [
                state_ref[chunk, row * tiles + tile : row * tiles + tile + 1, :]
                for chunk in range(chunks)
                for row in range(rows)
            ],
            axis=0,
        )
        state = jnp.where(same_head, jnp.concatenate([packed] * GROUP, axis=0), 0.0)
        total = state_ref[0, rows * tiles + tile : rows * tiles + tile + 1, :]
        numerator = jnp.dot(
            query, state, precision=HIGHEST, preferred_element_type=jnp.float32
        )
        denominator = jnp.dot(
            query * total, ones, precision=HIGHEST, preferred_element_type=jnp.float32
        )
        result = numerator / (denominator + attn_eps) * live
        out_ref[0, :, tile * LANES : (tile + 1) * LANES] = result.astype(jnp.bfloat16)


def compute_state(place, live, hidden, first, second, chunks):
    tokens, contraction = hidden[0].shape
    wide = first[0].shape[2] // 2
    tiles = wide // LANES + 1
    slots = -(-(HDIM // chunks + 1) * tiles // 8) * 8
    return pl.pallas_call(
        state_kernel,
        in_specs=[SMEM, SMEM] + [HBM] * (TEAM + len(first) + len(second)),
        out_specs=VMEM,
        out_shape=jax.ShapeDtypeStruct((chunks, slots, LANES), jnp.float32),
        scratch_shapes=[
            pltpu.VMEM((TEAM * tokens, wide + LANES), jnp.float32),
            pltpu.VMEM((TEAM * tokens, wide), jnp.float32),
            pltpu.VMEM((contraction, 2 * wide), jnp.bfloat16),
            pltpu.VMEM((contraction, LANES), jnp.bfloat16),
            pltpu.VMEM((TEAM, tokens, contraction), jnp.bfloat16),
            pltpu.SemaphoreType.DMA((16,)),
            pltpu.SemaphoreType.DMA((16,)),
            pltpu.SemaphoreType.DMA((TEAM,)),
        ],
        compiler_params=PARAMS,
        name="state",
    )(place, live, *hidden, *first, *second)


def compute_queries(place, hidden, second):
    tokens, contraction = hidden[0].shape
    width = second[0].shape[2]
    return pl.pallas_call(
        query_kernel,
        in_specs=[SMEM] + [HBM] * (TEAM + len(second)),
        out_specs=VMEM,
        out_shape=jax.ShapeDtypeStruct((TEAM * tokens, width), jnp.float32),
        scratch_shapes=[
            pltpu.VMEM((contraction, width), jnp.bfloat16),
            pltpu.VMEM((TEAM, tokens, contraction), jnp.bfloat16),
            pltpu.SemaphoreType.DMA((16,)),
            pltpu.SemaphoreType.DMA((TEAM,)),
        ],
        compiler_params=PARAMS,
        cost_estimate=pl.CostEstimate(
            flops=2 * TEAM * tokens * contraction * width,
            bytes_accessed=4 * TEAM * tokens * width + 2 * contraction * (width + TEAM * tokens),
            transcendentals=0,
        ),
        name="queries",
    )(place, *hidden, *second)


def compute_output(slots, live, queries, state):
    tokens, width = queries.shape[0] // TEAM, queries.shape[1]
    return pl.pallas_call(
        attend_kernel,
        grid_spec=pltpu.PrefetchScalarGridSpec(
            num_scalar_prefetch=2,
            grid=(TEAM,),
            in_specs=[
                pl.BlockSpec((tokens, width), lambda i, slots, live: (i, 0)),
                pl.BlockSpec(state.shape, lambda i, slots, live: (0, 0, 0)),
            ],
            out_specs=pl.BlockSpec((1, tokens, width), lambda i, slots, live: (slots[i], 0, 0)),
        ),
        out_shape=jax.ShapeDtypeStruct((TEAM, tokens, width), jnp.bfloat16),
        compiler_params=PARAMS,
        name="attend",
    )(slots, live, queries, state)


def spread(block, count, axis, groups):
    copies = jnp.broadcast_to(block[None], (count,) + block.shape)
    return lax.all_to_all(copies, axis, 0, 0, axis_index_groups=groups)


def exchange(block, mask, axis, count):
    return lax.ppermute(block, axis, [(i, i ^ mask) for i in range(count)])


def far_stage(held, one, two, count):
    middle = held.shape[0] // 2
    from_one = exchange(held, one, "img", count)
    from_two = exchange(held, two, "img", count)
    low = exchange(from_one[:middle], two, "img", count)
    high = exchange(from_two[middle:], one, "img", count)
    return [held, from_one, from_two, low, high]


def body(tokens, norm_gain, caption, null_caption, keep, bucket_rows, w_qkv):
    grid_rows, grid_cols, features_count = tokens.shape[1:]
    token_count = grid_rows * grid_cols
    seq_size = lax.axis_size("seq")
    img_size = lax.axis_size("img")
    side = 4
    teams = seq_size // TEAM
    seq_at = lax.axis_index("seq")
    img_at = lax.axis_index("img")
    rank = seq_at % TEAM
    same_rank = [[TEAM * j + r for j in range(teams)] for r in range(TEAM)]
    team = [[TEAM * j + r for r in range(TEAM)] for j in range(teams)]
    x_groups = [[y * side + x for x in range(side)] for y in range(side)]
    y_groups = [[y * side + x for y in range(side)] for x in range(side)]
    depth = features_count // img_size
    padded = -(-depth // 16) * 16
    columns = w_qkv.shape[1] * seq_size
    inner = columns // 3
    share = inner // TEAM
    main = share // LANES * LANES
    rest = share - main

    gathered = lax.all_gather(w_qkv, "seq", axis=0)
    rows = jnp.transpose(gathered, (1, 0, 2)).reshape(depth, columns)
    rows = jnp.pad(rows, ((0, padded - depth), (0, 0)))

    def pick(part):
        chosen = rows[:, part * inner : part * inner + share]
        for r in range(1, TEAM):
            start = part * inner + r * share
            chosen = jnp.where(rank == r, rows[:, start : start + share], chosen)
        return chosen

    query_cols, key_cols, value_cols = pick(0), pick(1), pick(2)
    first = jnp.concatenate([key_cols[:, :main], value_cols[:, :main]], axis=1)
    second = jnp.concatenate(
        [
            query_cols[:, :main],
            key_cols[:, main:],
            value_cols[:, main:],
            query_cols[:, main:],
            jnp.zeros((padded, LANES - 3 * rest), jnp.bfloat16),
        ],
        axis=1,
    )
    first_near = spread(first, side, "img", x_groups)
    second, tokens, first_near = lax.optimization_barrier((second, tokens, first_near))
    second_near = spread(second, side, "img", y_groups)
    first_pieces = far_stage(first_near, side, 3 * side, img_size)
    second_pieces = far_stage(second_near, 1, 3, img_size)
    y_at, x_at = img_at // side, img_at % side
    place = jnp.concatenate(
        [
            jnp.bitwise_xor(y_at, FAR_MASKS) * side + NEAR_SLOTS,
            NEAR_SLOTS * side + jnp.bitwise_xor(x_at, FAR_MASKS),
        ]
    ).astype(jnp.int32)

    features = jnp.transpose(tokens[0], (0, 2, 1)).astype(jnp.float32)
    mean_square = jnp.mean(features * features, axis=1, keepdims=True)
    condition = jnp.where(keep[0] > 0, caption[0], null_caption).astype(jnp.float32)
    hidden = (
        features * lax.rsqrt(mean_square + norm_eps) * norm_gain.astype(jnp.float32)[None, :, None]
        + condition[None, :, None]
    ).astype(jnp.bfloat16)
    hidden = hidden.reshape(grid_rows, img_size, depth, grid_cols)
    hidden = jnp.pad(hidden, ((0, 0), (0, 0), (0, padded - depth), (0, 0)))
    hidden = hidden.reshape(grid_rows, img_size * padded, grid_cols)
    mine = jnp.transpose(hidden, (0, 2, 1)).reshape(token_count, img_size * padded)
    beside = exchange(mine, 2, "seq", seq_size)
    late, _ = lax.optimization_barrier((beside, first_pieces[1:3] + second_pieces[1:3]))
    across = exchange(late, 1, "seq", seq_size)
    hidden = (mine, exchange(mine, 1, "seq", seq_size), beside, across)

    slots = jnp.bitwise_xor(rank, jnp.arange(TEAM, dtype=jnp.int32))
    first_row = (seq_at - rank + slots) * grid_rows
    live = jnp.clip(bucket_rows[0] - first_row, 0, grid_rows) * grid_cols

    part = compute_state(place, live, hidden, first_pieces, second_pieces, teams)
    part = lax.all_to_all(part, "seq", 0, 0, axis_index_groups=same_rank)
    state = spread(jnp.sum(part, axis=0), teams, "seq", same_rank)
    queries = compute_queries(place, hidden, second_pieces)

    result = compute_output(slots, live, queries, state)
    result = lax.all_to_all(result, "seq", 0, 0, axis_index_groups=team)
    result = jnp.transpose(result[:, :, :share], (1, 0, 2))
    return result.reshape(1, grid_rows, grid_cols, inner)


def solution(mesh):
    in_specs = (
        P("img", "seq", None, None),
        P(),
        P("img", None),
        P(),
        P("img"),
        P("img"),
        P("img", "seq"),
    )
    out_specs = P("img", "seq", None, None)

    return jax.shard_map(
        body, mesh=mesh, in_specs=in_specs, out_specs=out_specs, check_vma=False
    )
```

time: 394 us -> 218 us (0.55)
  waiting for transfers between devices: 213 us -> 45.1 us
  starting transfers between devices: 0.04 us -> 50.6 us
  blocking collectives: 108 us -> 63.6 us
  Pallas kernels: 0 us -> 32.2 us
  matrix products: 17.3 us -> 0 us
  local copies, waits for them, and re-layouts: 31.2 us -> 18.1 us
  between operations: 14.8 us -> 1.76 us
    psum x1 -> x0, waiting for transfers between devices: 109 us -> none  [body(): state_outer, key_total = lax.psum((state_outer, key_total), 'seq')]
    all_gather x1 -> x0, waiting for transfers between devices: 103 us -> none  [body(): lax.all_gather(rows_whole, 'seq', axis=1, tiled=True)]
    psum x1 -> x0, blocking collectives: 88.2 us -> none  [body(): state_outer, key_total = lax.psum((state_outer, key_total), 'seq')]
    ppermute x0 -> x11, starting transfers between devices: none -> 32.7 us  [exchange(): return lax.ppermute(block, axis, [(i, i ^ mask) for i in range(count)])]
    pallas_call x0 -> x3, Pallas kernels: none -> 32.2 us  [the longest x1 15.2 us: compute_state(): pl.pallas_call(state_kernel, in_specs=[SMEM, SMEM] + [HBM] * (TEAM + len(...]
    all_to_all x0 -> x1, blocking collectives: none -> 22.6 us  [body(): result = lax.all_to_all(result, 'seq', 0, 0, axis_index_groups=team)]
    all_to_all x0 -> x4, waiting for transfers between devices: none -> 22.6 us  [the longest x1 11.7 us: body(): part = lax.all_to_all(part, 'seq', 0, 0, axis_index_groups=same_rank)]
    ppermute x0 -> x11, waiting for transfers between devices: none -> 22.5 us  [exchange(): return lax.ppermute(block, axis, [(i, i ^ mask) for i in range(count)])]
  transfers between devices with their start and end apart: 2 -> 15, of which waited for: 2 -> 8; matrix products, arithmetic and copies ran while one was open for 3% -> 5% of each run, Pallas kernels for 0% -> 5%
where the time goes in v2:
time: 218 us; the launch traced here: 217 us
  blocking collectives  63.6 us (29%)
  starting transfers between devices  50.6 us (23%)
  waiting for transfers between devices  45.1 us (21%)
  Pallas kernels  32.2 us (15%)
  local copies, waits for them, and re-layouts  18.1 us (8%)
  other arithmetic  5.28 us (2%)
    all_gather x1, blocking collectives, body(): gathered = lax.all_gather(w_qkv, 'seq', axis=0)  41 us
    ppermute x11, starting transfers between devices, exchange(): return lax.ppermute(block, axis, [(i, i ^ mask) for i in range(count)])  32.7 us
    all_to_all x1, blocking collectives, body(): result = lax.all_to_all(result, 'seq', 0, 0, axis_index_groups=team)  22.6 us
    ppermute x11, waiting for transfers between devices, exchange(): return lax.ppermute(block, axis, [(i, i ^ mask) for i in range(count)])  22.5 us
    pallas_call x1, Pallas kernels, compute_state(): pl.pallas_call(state_kernel, in_specs=[SMEM, SMEM] + [HBM] * (TEAM + len(...  15.2 us
    all_to_all x1, waiting for transfers between devices, body(): part = lax.all_to_all(part, 'seq', 0, 0, axis_index_groups=same_rank)  11.7 us
    all_to_all x3, starting transfers between devices, spread(): return lax.all_to_all(copies, axis, 0, 0, axis_index_groups=groups)  11.5 us
    all_to_all x3, waiting for transfers between devices, spread(): return lax.all_to_all(copies, axis, 0, 0, axis_index_groups=groups)  10.9 us
  transfers between devices with their start and end apart: 15, of which 8 were waited for; matrix products, arithmetic and copies ran while one was open for 5% of the time, Pallas kernels for 5%

profile of v2, /device:TPU:1, one launch (start us, length us, event | category | flops | bytes accessed | tf_op | source)
XLA Modules:
  0.0 216.6 jit_solution(15096110281221340762)
XLA Ops:
  0.0 41.0 %all-gather.1 = bf16[32,140,108]{2,1,0:T(8,128)(2,1)S(1)} all-gather(bf16[1,140,108]{2,1,0:T(8,128)(2,1)} %bitcast.23), channel_id=2, replica_groups=mesh['seq'=32,'img'=16] {'seq'}, dimensions={0}, use_global_device_ids=true | all-gather | bytes 997920 | tf_op jit(solution)/shard_map/all_gather | solution.py:297
  41.3 2.5 %reshape.32 = bf16[140,3456]{1,0:T(8,128)(2,1)S(1)} reshape(bf16[140,32,108]{2,1,0:T(8,128)(2,1)S(1)} %copy.15) | data formatting | bytes 1935360 | tf_op jit(solution)/shard_map/reshape | solution.py:298
  45.5 4.0 %all-to-all-start = ((bf16[4,144,512]{2,1,0:T(8,128)(2,1)}), bf16[4,144,512]{2,1,0:T(8,128)(2,1)S(1)}, u32[]{:S(2)}, u32[]{:S(2)}) async-start(bf16[4,144,512]{2,1,0:T(8,128)(2,1)} %broadcast_in_dim.9), calls=%async_computation | async-start | bytes 1179648 | tf_op jit(solution)/shard_map/all_to_all | solution.py:259
  51.0 8.3 %all-to-all-done.refs_4_ = bf16[4,144,512]{2,1,0:T(8,128)(2,1)S(1)} async-done(((bf16[4,144,512]{2,1,0:T(8,128)(2,1)}), bf16[4,144,512]{2,1,0:T(8,128)(2,1)S(1)}, u32[]{:S(2)}, u32[]{:S(2)}) %all-to-all-start) | async-done | bytes 589856 | tf_op jit(solution)/shard_map/all_to_all | solution.py:259
  66.7 4.2 %all-to-all-start.1 = ((bf16[4,144,384]{2,1,0:T(8,128)(2,1)}), bf16[4,144,384]{2,1,0:T(8,128)(2,1)}, u32[]{:S(2)}, u32[]{:S(2)}) async-start(bf16[4,144,384]{2,1,0:T(8,128)(2,1)} %broadcast_in_dim.10), calls=%async_computation.1 | async-start | bytes 884736 | tf_op jit(solution)/shard_map/all_to_all | solution.py:259
  70.9 4.6 %collective-permute-start.3 = (bf16[4,144,512]{2,1,0:T(8,128)(2,1)}, bf16[4,144,512]{2,1,0:T(8,128)(2,1)}, u32[]{:S(2)}, u32[]{:S(2)}) collective-permute-start(bf16[4,144,512]{2,1,0:T(8,128)(2,1)} %copy-done.5), channel_id=1, source_target_pairs={{0,12},{1,13},{2,14},{3,15},{4,8},{5,9},{6,10},{7,11},{8,4},{9,5},... | collective-permute-start | bytes 1769480 | tf_op jit(solution)/shard_map/ppermute | solution.py:263
  77.8 2.8 %collective-permute-start.5 = (bf16[4,144,384]{2,1,0:T(8,128)(2,1)}, bf16[4,144,384]{2,1,0:T(8,128)(2,1)S(1)}, u32[]{:S(2)}, u32[]{:S(2)}) collective-permute-start(bf16[4,144,384]{2,1,0:T(8,128)(2,1)} %all-to-all-done.1.refs_4_.refs_9_), channel_id=1, source_target_pairs={{0,3},{1,2},{2,1},{3,0},{4,7},{5,6},{6,5},{7,4},{8,11},{9,10},{10,... | collective-permute-start | bytes 1327112 | tf_op jit(solution)/shard_map/ppermute | solution.py:263
  82.5 9.1 %collective-permute-done.3.refs_6_ = bf16[4,144,512]{2,1,0:T(8,128)(2,1)} collective-permute-done((bf16[4,144,512]{2,1,0:T(8,128)(2,1)}, bf16[4,144,512]{2,1,0:T(8,128)(2,1)}, u32[]{:S(2)}, u32[]{:S(2)}) %collective-permute-start.3) | collective-permute-done | bytes 589856 | tf_op jit(solution)/shard_map/ppermute | solution.py:263
  91.6 3.5 %collective-permute-start = (bf16[384,2304]{1,0:T(8,128)(2,1)S(1)}, bf16[384,2304]{1,0:T(8,128)(2,1)}, u32[]{:S(2)}, u32[]{:S(2)}) collective-permute-start(bf16[384,2304]{1,0:T(8,128)(2,1)S(1)} %bitcast.18), channel_id=1, source_target_pairs={{0,16},{16,0},{32,48},{48,32},{64,80},{80,64},{96,112},{112,96},{1... | collective-permute-start | bytes 5308424 | tf_op jit(solution)/shard_map/ppermute | solution.py:263
  95.1 8.7 %collective-permute-done.1.refs_2_ = bf16[384,2304]{1,0:T(8,128)(2,1)S(1)} collective-permute-done((bf16[384,2304]{1,0:T(8,128)(2,1)S(1)}, bf16[384,2304]{1,0:T(8,128)(2,1)S(1)}, u32[]{:S(2)}, u32[]{:S(2)}) %collective-permute-start.1) | collective-permute-done | bytes 1769504 | tf_op jit(solution)/shard_map/ppermute | solution.py:263
  103.8 4.1 %collective-permute-start.6 = (bf16[384,2304]{1,0:T(8,128)(2,1)S(1)}, bf16[384,2304]{1,0:T(8,128)(2,1)}, u32[]{:S(2)}, u32[]{:S(2)}) collective-permute-start(bf16[384,2304]{1,0:T(8,128)(2,1)S(1)} %collective-permute-done.1.refs_2_), channel_id=1, source_target_pairs={{0,16},{16,0},{32,48},{48,32},{64,80},{80,64},{96,112},{112,96},{1... | collective-permute-start | bytes 5308424 | tf_op jit(solution)/shard_map/ppermute | solution.py:263
  109.6 3.2 %collective-permute-start.10 = (bf16[2,144,512]{2,1,0:T(8,128)(2,1)}, bf16[2,144,512]{2,1,0:T(8,128)(2,1)}, u32[]{:S(2)}, u32[]{:S(2)}) collective-permute-start(bf16[2,144,512]{2,1,0:T(8,128)(2,1)} %slice.101), channel_id=1, source_target_pairs={{0,4},{1,5},{2,6},{3,7},{4,0},{5,1},{6,2},{7,3},{8,12},{9,13},{10,... | collective-permute-start | bytes 884744 | tf_op jit(solution)/shard_map/ppermute | solution.py:263
  114.5 3.8 %collective-permute-start.9 = (bf16[2,144,512]{2,1,0:T(8,128)(2,1)}, bf16[2,144,512]{2,1,0:T(8,128)(2,1)}, u32[]{:S(2)}, u32[]{:S(2)}) collective-permute-start(bf16[2,144,512]{2,1,0:T(8,128)(2,1)} %slice.100), channel_id=1, source_target_pairs={{0,12},{1,13},{2,14},{3,15},{4,8},{5,9},{6,10},{7,11},{8,4},{9,5},... | collective-permute-start | bytes 884744 | tf_op jit(solution)/shard_map/ppermute | solution.py:263
  120.5 2.2 %collective-permute-start.8 = (bf16[2,144,384]{2,1,0:T(8,128)(2,1)S(1)}, bf16[2,144,384]{2,1,0:T(8,128)(2,1)S(1)}, u32[]{:S(2)}, u32[]{:S(2)}) collective-permute-start(bf16[2,144,384]{2,1,0:T(8,128)(2,1)S(1)} %slice.99), channel_id=1, source_target_pairs={{0,1},{1,0},{2,3},{3,2},{4,5},{5,4},{6,7},{7,6},{8,9},{9,8},{10,11... | collective-permute-start | bytes 663560 | tf_op jit(solution)/shard_map/ppermute | solution.py:263
  123.6 2.7 %collective-permute-start.7 = (bf16[2,144,384]{2,1,0:T(8,128)(2,1)S(1)}, bf16[2,144,384]{2,1,0:T(8,128)(2,1)S(1)}, u32[]{:S(2)}, u32[]{:S(2)}) collective-permute-start(bf16[2,144,384]{2,1,0:T(8,128)(2,1)S(1)} %slice.98), channel_id=1, source_target_pairs={{0,3},{1,2},{2,1},{3,0},{4,7},{5,6},{6,5},{7,4},{8,11},{9,10},{10,... | collective-permute-start | bytes 663560 | tf_op jit(solution)/shard_map/ppermute | solution.py:263
  128.8 4.1 %collective-permute-done.7.refs_7_.refs_12_ = bf16[2,144,384]{2,1,0:T(8,128)(2,1)S(1)} collective-permute-done((bf16[2,144,384]{2,1,0:T(8,128)(2,1)S(1)}, bf16[2,144,384]{2,1,0:T(8,128)(2,1)S(1)}, u32[]{:S(2)}, u32[]{:S(2)}) %collective-permute-start.7) | collective-permute-done | bytes 221216 | tf_op jit(solution)/shard_map/ppermute | solution.py:263
  133.6 15.2 %state.1 = f32[8,16,128]{2,1,0:T(8,128)} custom-call(s32[32]{0:T(128)} %pad_add_fusion.place_ref, s32[4]{0:T(128)} %clamp_multiply_fusion.live_ref, bf16[384,2304]{1,0:T(8,128)(2,1)} %bitcast.19, bf16[384,2304]{1,0:T(8,128)(2,1)} %collective-permute-done.refs_1_, bf16[384,2304]{1,0:T(8,128)(2,1)} %copy-done.1, ...), custom_call_target="tpu_custom_call" | custom-call | tf_op jit(solution)/shard_map/state/pallas_call | solution.py:194
  148.8 6.4 %all-to-all-start.2 = ((f32[8,16,128]{2,1,0:T(8,128)}), f32[8,16,128]{2,1,0:T(8,128)S(1)}, u32[]{:S(2)}, u32[]{:S(2)}) async-start(f32[8,16,128]{2,1,0:T(8,128)} %state.1), calls=%async_computation.2 | async-start | bytes 131072 | tf_op jit(solution)/shard_map/all_to_all | solution.py:354
  155.7 11.7 %all-to-all-done.2 = f32[8,16,128]{2,1,0:T(8,128)S(1)} async-done(((f32[8,16,128]{2,1,0:T(8,128)}), f32[8,16,128]{2,1,0:T(8,128)S(1)}, u32[]{:S(2)}, u32[]{:S(2)}) %all-to-all-start.2) | async-done | bytes 65568 | tf_op jit(solution)/shard_map/all_to_all | solution.py:354
  168.1 3.4 %all-to-all-start.3 = ((f32[8,16,128]{2,1,0:T(8,128)}), f32[8,16,128]{2,1,0:T(8,128)S(1)}, u32[]{:S(2)}, u32[]{:S(2)}) async-start(f32[8,16,128]{2,1,0:T(8,128)} %broadcast_in_dim.11), calls=%async_computation.3 | async-start | bytes 131072 | tf_op jit(solution)/shard_map/all_to_all | solution.py:259
  171.4 9.9 %queries.1.query_ref = f32[1536,384]{1,0:T(8,128)} custom-call(s32[32]{0:T(128)} %pad_add_fusion.place_ref, bf16[384,2304]{1,0:T(8,128)(2,1)} %bitcast.20, bf16[384,2304]{1,0:T(8,128)(2,1)} %collective-permute-done.refs_1_, bf16[384,2304]{1,0:T(8,128)(2,1)} %copy-done.1, bf16[384,2304]{1,0:T(8,128)(2,1)} %collective-permute-done.6.refs_3_, ...), custom_call_target="tpu_custom_call" | custom-call | flops 2717908992 | bytes 11206656 | tf_op jit(solution)/shard_map/queries/pallas_call | solution.py:217
  181.4 2.2 %all-to-all-done.3.state_ref = f32[8,16,128]{2,1,0:T(8,128)S(1)} async-done(((f32[8,16,128]{2,1,0:T(8,128)}), f32[8,16,128]{2,1,0:T(8,128)S(1)}, u32[]{:S(2)}, u32[]{:S(2)}) %all-to-all-start.3) | async-done | bytes 65568 | tf_op jit(solution)/shard_map/all_to_all | solution.py:259
  184.2 7.1 %attend.1 = bf16[4,384,384]{2,1,0:T(8,128)(2,1)} custom-call(s32[4]{0:T(128)} %iota_xor_fusion.slot_ref, s32[4]{0:T(128)} %clamp_multiply_fusion.live_ref, f32[1536,384]{1,0:T(8,128)} %queries.1.query_ref, f32[8,16,128]{2,1,0:T(8,128)} %copy-done.8), custom_call_target="tpu_custom_call" | custom-call | tf_op jit(solution)/shard_map/attend/pallas_call | solution.py:240
  191.3 22.6 %all_to_all.25 = bf16[4,384,384]{2,1,0:T(8,128)(2,1)S(1)} all-to-all(bf16[4,384,384]{2,1,0:T(8,128)(2,1)} %attend.1), channel_id=1, replica_groups={{0,16,32,48},{64,80,96,112},{128,144,160,176},{192,208,224,240},{256,27..., dimensions={0} | all-to-all | bytes 2359296 | tf_op jit(solution)/shard_map/all_to_all | solution.py:359
  (77 shorter events, 27.8 us)
Async XLA Ops:
  44.5 6.5 %copy-start.11 = (bf16[2240]{0:T(1024)(128)(2,1)S(1)}, bf16[2240]{0:T(1024)(128)(2,1)}, u32[]{:S(2)}) copy-start(bf16[2240]{0:T(1024)(128)(2,1)} %param.13) | copy-start | bytes 13444
  44.5 14.8 %copy-start.2 = (bf16[1,3,128,2240]{2,3,1,0:T(8,128)(2,1)S(1)}, bf16[1,3,128,2240]{2,3,1,0:T(8,128)(2,1)}, u32[]{:S(2)}) copy-start(bf16[1,3,128,2240]{2,3,1,0:T(8,128)(2,1)} %param.10) | copy-start | bytes 5160964
  45.5 13.8 %all-to-all-start = ((bf16[4,144,512]{2,1,0:T(8,128)(2,1)}), bf16[4,144,512]{2,1,0:T(8,128)(2,1)S(1)}, u32[]{:S(2)}, u32[]{:S(2)}) async-start(bf16[4,144,512]{2,1,0:T(8,128)(2,1)} %broadcast_in_dim.9), calls=%async_computation | async-start | bytes 1179648 | tf_op jit(solution)/shard_map/all_to_all | solution.py:259
  62.8 60.8 %copy-start = (bf16[3,128,2304]{2,1,0:T(8,128)(2,1)}, bf16[3,128,2304]{2,1,0:T(8,128)(2,1)S(1)}, u32[]{:S(2)}) copy-start(bf16[3,128,2304]{2,1,0:T(8,128)(2,1)S(1)} %copy.16) | copy-start | bytes 5308420
  62.9 55.4 %copy-start.12 = (s32[16]{0:T(128)S(1)}, s32[16]{0:T(128)}, u32[]{:S(2)}) copy-start(s32[16]{0:T(128)} %constant.67.clone) | copy-start | bytes 196
  62.9 55.4 %copy-start.13 = (s32[16]{0:T(128)S(1)}, s32[16]{0:T(128)}, u32[]{:S(2)}) copy-start(s32[16]{0:T(128)} %constant.66.clone) | copy-start | bytes 196
  62.9 55.4 %copy-start.14 = (s32[16]{0:T(128)S(1)}, s32[16]{0:T(128)}, u32[]{:S(2)}) copy-start(s32[16]{0:T(128)} %constant.65.clone) | copy-start | bytes 196
  62.9 40.9 %collective-permute-start.1 = (bf16[384,2304]{1,0:T(8,128)(2,1)S(1)}, bf16[384,2304]{1,0:T(8,128)(2,1)S(1)}, u32[]{:S(2)}, u32[]{:S(2)}) collective-permute-start(bf16[384,2304]{1,0:T(8,128)(2,1)S(1)} %bitcast.17), channel_id=1, source_target_pairs={{0,32},{16,48},{32,0},{48,16},{64,96},{80,112},{96,64},{112,80},{1... | collective-permute-start | bytes 5308424 | tf_op jit(solution)/shard_map/ppermute | solution.py:263
  66.7 11.1 %all-to-all-start.1 = ((bf16[4,144,384]{2,1,0:T(8,128)(2,1)}), bf16[4,144,384]{2,1,0:T(8,128)(2,1)}, u32[]{:S(2)}, u32[]{:S(2)}) async-start(bf16[4,144,384]{2,1,0:T(8,128)(2,1)} %broadcast_in_dim.10), calls=%async_computation.1 | async-start | bytes 884736 | tf_op jit(solution)/shard_map/all_to_all | solution.py:259
  70.9 20.7 %collective-permute-start.3 = (bf16[4,144,512]{2,1,0:T(8,128)(2,1)}, bf16[4,144,512]{2,1,0:T(8,128)(2,1)}, u32[]{:S(2)}, u32[]{:S(2)}) collective-permute-start(bf16[4,144,512]{2,1,0:T(8,128)(2,1)} %copy-done.5), channel_id=1, source_target_pairs={{0,12},{1,13},{2,14},{3,15},{4,8},{5,9},{6,10},{7,11},{8,4},{9,5},... | collective-permute-start | bytes 1769480 | tf_op jit(solution)/shard_map/ppermute | solution.py:263
  75.4 19.6 %collective-permute-start.2 = (bf16[4,144,512]{2,1,0:T(8,128)(2,1)}, bf16[4,144,512]{2,1,0:T(8,128)(2,1)}, u32[]{:S(2)}, u32[]{:S(2)}) collective-permute-start(bf16[4,144,512]{2,1,0:T(8,128)(2,1)} %copy-done.5), channel_id=1, source_target_pairs={{0,4},{1,5},{2,6},{3,7},{4,0},{5,1},{6,2},{7,3},{8,12},{9,13},{10,... | collective-permute-start | bytes 1769480 | tf_op jit(solution)/shard_map/ppermute | solution.py:263
  77.8 17.3 %collective-permute-start.5 = (bf16[4,144,384]{2,1,0:T(8,128)(2,1)}, bf16[4,144,384]{2,1,0:T(8,128)(2,1)S(1)}, u32[]{:S(2)}, u32[]{:S(2)}) collective-permute-start(bf16[4,144,384]{2,1,0:T(8,128)(2,1)} %all-to-all-done.1.refs_4_.refs_9_), channel_id=1, source_target_pairs={{0,3},{1,2},{2,1},{3,0},{4,7},{5,6},{6,5},{7,4},{8,11},{9,10},{10,... | collective-permute-start | bytes 1327112 | tf_op jit(solution)/shard_map/ppermute | solution.py:263
  80.6 14.5 %collective-permute-start.4 = (bf16[4,144,384]{2,1,0:T(8,128)(2,1)}, bf16[4,144,384]{2,1,0:T(8,128)(2,1)S(1)}, u32[]{:S(2)}, u32[]{:S(2)}) collective-permute-start(bf16[4,144,384]{2,1,0:T(8,128)(2,1)} %all-to-all-done.1.refs_4_.refs_9_), channel_id=1, source_target_pairs={{0,1},{1,0},{2,3},{3,2},{4,5},{5,4},{6,7},{7,6},{8,9},{9,8},{10,11... | collective-permute-start | bytes 1327112 | tf_op jit(solution)/shard_map/ppermute | solution.py:263
  91.6 41.3 %collective-permute-start = (bf16[384,2304]{1,0:T(8,128)(2,1)S(1)}, bf16[384,2304]{1,0:T(8,128)(2,1)}, u32[]{:S(2)}, u32[]{:S(2)}) collective-permute-start(bf16[384,2304]{1,0:T(8,128)(2,1)S(1)} %bitcast.18), channel_id=1, source_target_pairs={{0,16},{16,0},{32,48},{48,32},{64,80},{80,64},{96,112},{112,96},{1... | collective-permute-start | bytes 5308424 | tf_op jit(solution)/shard_map/ppermute | solution.py:263
  95.1 8.7 %copy-start.3 = (bf16[4,144,384]{2,1,0:T(8,128)(2,1)}, bf16[4,144,384]{2,1,0:T(8,128)(2,1)S(1)}, u32[]{:S(2)}) copy-start(bf16[4,144,384]{2,1,0:T(8,128)(2,1)S(1)} %collective-permute-done.5.refs_6_.refs_11_) | copy-start | bytes 1327108
  95.1 8.7 %copy-start.4 = (bf16[4,144,384]{2,1,0:T(8,128)(2,1)}, bf16[4,144,384]{2,1,0:T(8,128)(2,1)S(1)}, u32[]{:S(2)}) copy-start(bf16[4,144,384]{2,1,0:T(8,128)(2,1)S(1)} %collective-permute-done.4.refs_5_.refs_10_) | copy-start | bytes 1327108
  103.8 29.1 %copy-start.1 = (bf16[384,2304]{1,0:T(8,128)(2,1)}, bf16[384,2304]{1,0:T(8,128)(2,1)S(1)}, u32[]{:S(2)}) copy-start(bf16[384,2304]{1,0:T(8,128)(2,1)S(1)} %collective-permute-done.1.refs_2_) | copy-start | bytes 5308420
  103.8 29.1 %collective-permute-start.6 = (bf16[384,2304]{1,0:T(8,128)(2,1)S(1)}, bf16[384,2304]{1,0:T(8,128)(2,1)}, u32[]{:S(2)}, u32[]{:S(2)}) collective-permute-start(bf16[384,2304]{1,0:T(8,128)(2,1)S(1)} %collective-permute-done.1.refs_2_), channel_id=1, source_target_pairs={{0,16},{16,0},{32,48},{48,32},{64,80},{80,64},{96,112},{112,96},{1... | collective-permute-start | bytes 5308424 | tf_op jit(solution)/shard_map/ppermute | solution.py:263
  109.6 14.1 %collective-permute-start.10 = (bf16[2,144,512]{2,1,0:T(8,128)(2,1)}, bf16[2,144,512]{2,1,0:T(8,128)(2,1)}, u32[]{:S(2)}, u32[]{:S(2)}) collective-permute-start(bf16[2,144,512]{2,1,0:T(8,128)(2,1)} %slice.101), channel_id=1, source_target_pairs={{0,4},{1,5},{2,6},{3,7},{4,0},{5,1},{6,2},{7,3},{8,12},{9,13},{10,... | collective-permute-start | bytes 884744 | tf_op jit(solution)/shard_map/ppermute | solution.py:263
  114.5 13.7 %collective-permute-start.9 = (bf16[2,144,512]{2,1,0:T(8,128)(2,1)}, bf16[2,144,512]{2,1,0:T(8,128)(2,1)}, u32[]{:S(2)}, u32[]{:S(2)}) collective-permute-start(bf16[2,144,512]{2,1,0:T(8,128)(2,1)} %slice.100), channel_id=1, source_target_pairs={{0,12},{1,13},{2,14},{3,15},{4,8},{5,9},{6,10},{7,11},{8,4},{9,5},... | collective-permute-start | bytes 884744 | tf_op jit(solution)/shard_map/ppermute | solution.py:263
  120.5 8.3 %collective-permute-start.8 = (bf16[2,144,384]{2,1,0:T(8,128)(2,1)S(1)}, bf16[2,144,384]{2,1,0:T(8,128)(2,1)S(1)}, u32[]{:S(2)}, u32[]{:S(2)}) collective-permute-start(bf16[2,144,384]{2,1,0:T(8,128)(2,1)S(1)} %slice.99), channel_id=1, source_target_pairs={{0,1},{1,0},{2,3},{3,2},{4,5},{5,4},{6,7},{7,6},{8,9},{9,8},{10,11... | collective-permute-start | bytes 663560 | tf_op jit(solution)/shard_map/ppermute | solution.py:263
  123.6 9.2 %collective-permute-start.7 = (bf16[2,144,384]{2,1,0:T(8,128)(2,1)S(1)}, bf16[2,144,384]{2,1,0:T(8,128)(2,1)S(1)}, u32[]{:S(2)}, u32[]{:S(2)}) collective-permute-start(bf16[2,144,384]{2,1,0:T(8,128)(2,1)S(1)} %slice.98), channel_id=1, source_target_pairs={{0,3},{1,2},{2,1},{3,0},{4,7},{5,6},{6,5},{7,4},{8,11},{9,10},{10,... | collective-permute-start | bytes 663560 | tf_op jit(solution)/shard_map/ppermute | solution.py:263
  148.8 18.6 %all-to-all-start.2 = ((f32[8,16,128]{2,1,0:T(8,128)}), f32[8,16,128]{2,1,0:T(8,128)S(1)}, u32[]{:S(2)}, u32[]{:S(2)}) async-start(f32[8,16,128]{2,1,0:T(8,128)} %state.1), calls=%async_computation.2 | async-start | bytes 131072 | tf_op jit(solution)/shard_map/all_to_all | solution.py:354
  168.1 15.5 %all-to-all-start.3 = ((f32[8,16,128]{2,1,0:T(8,128)}), f32[8,16,128]{2,1,0:T(8,128)S(1)}, u32[]{:S(2)}, u32[]{:S(2)}) async-start(f32[8,16,128]{2,1,0:T(8,128)} %broadcast_in_dim.11), calls=%async_computation.3 | async-start | bytes 131072 | tf_op jit(solution)/shard_map/all_to_all | solution.py:259
  (6 other events, 17.6 us)

commit v3 on v2

--- a/solution.py
+++ b/solution.py
@@ -14,7 +14,6 @@
 
 norm_eps = 1e-06
 attn_eps = 1e-06
-HIGHEST = lax.Precision.HIGHEST
 
 VMEM = pl.BlockSpec(memory_space=pltpu.VMEM)
 SMEM = pl.BlockSpec(memory_space=pltpu.SMEM)
@@ -34,6 +33,11 @@
 def live_rows(limit, tokens):
     token = lax.broadcasted_iota(jnp.int32, (tokens, LANES), 0)
     return (token < limit).astype(jnp.float32)
+
+
+def halves(value):
+    high = value.astype(jnp.bfloat16)
+    return high, (value - high.astype(jnp.float32)).astype(jnp.bfloat16)
 
 
 def load_blocks(place_ref, base, pieces, start, into_ref, sems):
@@ -66,15 +70,13 @@
 
 
 def state_kernel(place_ref, live_ref, *refs):
-    hidden, refs = refs[:TEAM], refs[TEAM:]
-    first, second, refs = refs[:5], refs[5:10], refs[10:]
-    out_ref, keys_ref, values_ref, pair_w, mixed_w, hidden_ref, pair_s, mixed_s, hidden_s = refs
+    hidden, first, refs = refs[:TEAM], refs[TEAM : TEAM + 5], refs[TEAM + 5 :]
+    out_ref, keys_ref, values_ref, weights_ref, hidden_ref, sems, hidden_s = refs
     tokens = hidden_ref.shape[1]
     full = values_ref.shape[1] // LANES
-    pair_copies = load_blocks(place_ref, 0, first, 0, pair_w, pair_s)
+    copies = load_blocks(place_ref, 0, first, 0, weights_ref, sems)
     hidden_copies = load_hidden(hidden, hidden_ref, hidden_s)
-    mixed_copies = load_blocks(place_ref, 16, second, full * LANES, mixed_w, mixed_s)
-    for copy in pair_copies:
+    for copy in copies:
         copy.wait()
     wide = full * LANES
     for at in range(TEAM):
@@ -82,18 +84,15 @@
         rows = slice(at * tokens, (at + 1) * tokens)
         block = hidden_ref[at]
         live = live_rows(live_ref[at], tokens)
-        keys = jnp.dot(block, pair_w[:, :wide], preferred_element_type=jnp.float32)
+        keys = jnp.dot(block, weights_ref[:, :wide], preferred_element_type=jnp.float32)
         for tile in range(full):
             lanes = slice(tile * LANES, (tile + 1) * LANES)
             keys_ref[rows, lanes] = jnp.maximum(keys[:, lanes], 0.0) * live
         values_ref[rows, :] = jnp.dot(
-            block, pair_w[:, wide:], preferred_element_type=jnp.float32
-        )
-        if at == 0:
-            for copy in mixed_copies:
-                copy.wait()
+            block, weights_ref[:, wide : 2 * wide], preferred_element_type=jnp.float32
+        )
         keys_ref[rows, wide:] = jnp.dot(
-            block, mixed_w[...], preferred_element_type=jnp.float32
+            block, weights_ref[:, 2 * wide :], preferred_element_type=jnp.float32
         )
     same_head = block_mask()
     column = lax.broadcasted_iota(jnp.int32, (LANES, LANES), 1)
@@ -113,13 +112,17 @@
             )
             keys = jnp.maximum(keys, 0.0) * live
             keep = jnp.logical_and(same_head, column < HDIM)
-        outer = lax.dot_general(
-            keys,
-            values,
-            (((0,), (0,)), ((), ())),
-            precision=HIGHEST,
+        key_high, key_low = halves(keys)
+        value_high, value_low = halves(values)
+        tall = (((0,), (0,)), ((), ()))
+        both = lax.dot_general(
+            key_high,
+            jnp.concatenate([value_high, value_low], axis=1),
+            tall,
             preferred_element_type=jnp.float32,
         )
+        outer = lax.dot_general(key_low, value_high, tall, preferred_element_type=jnp.float32)
+        outer = outer + both[:, LANES:] + both[:, :LANES]
         outer = jnp.where(keep, outer, 0.0)
         packed = outer[:HDIM]
         for head in range(1, GROUP):
@@ -149,66 +152,68 @@
         queries = jnp.dot(
             hidden_ref[at], weights_ref[...], preferred_element_type=jnp.float32
         )
-        edge = out_ref.shape[1] - LANES
-        out_ref[rows, :edge] = jnp.maximum(queries[:, :edge], 0.0)
-        out_ref[rows, edge:] = jnp.maximum(
-            pltpu.roll(queries[:, edge:], LANES - 2 * HDIM, 1), 0.0
-        )
-
-
-def attend_kernel(slot_ref, live_ref, query_ref, state_ref, out_ref):
+        out_ref[rows, :] = jnp.maximum(queries, 0.0)
+
+
+def attend_kernel(slot_ref, live_ref, query_ref, state_ref, out_ref, factor_ref):
     tokens = query_ref.shape[0]
     tiles = query_ref.shape[1] // LANES
     chunks = state_ref.shape[0]
     rows = HDIM // chunks
+
+    @pl.when(pl.program_id(0) == 0)
+    def _():
+        same_head = block_mask()
+        for tile in range(tiles):
+            packed = jnp.concatenate(
+                [
+                    state_ref[chunk, row * tiles + tile : row * tiles + tile + 1, :]
+                    for chunk in range(chunks)
+                    for row in range(rows)
+                ],
+                axis=0,
+            )
+            state = jnp.where(same_head, jnp.concatenate([packed] * GROUP, axis=0), 0.0)
+            total = state_ref[0, rows * tiles + tile : rows * tiles + tile + 1, :]
+            total = jnp.transpose(jnp.broadcast_to(total, (LANES, LANES)))
+            total = jnp.where(same_head, total, 0.0)
+            high, low = halves(jnp.concatenate([state, total], axis=1))
+            factor_ref[tile, :, : 2 * LANES] = high
+            factor_ref[tile, :, 2 * LANES :] = low
+
     live = live_rows(live_ref[pl.program_id(0)], tokens)
-    same_head = block_mask()
-    ones = same_head.astype(jnp.float32)
     for tile in range(tiles):
-        query = query_ref[:, tile * LANES : (tile + 1) * LANES]
-        packed = jnp.concatenate(
-            [
-                state_ref[chunk, row * tiles + tile : row * tiles + tile + 1, :]
-                for chunk in range(chunks)
-                for row in range(rows)
-            ],
-            axis=0,
-        )
-        state = jnp.where(same_head, jnp.concatenate([packed] * GROUP, axis=0), 0.0)
-        total = state_ref[0, rows * tiles + tile : rows * tiles + tile + 1, :]
-        numerator = jnp.dot(
-            query, state, precision=HIGHEST, preferred_element_type=jnp.float32
-        )
-        denominator = jnp.dot(
-            query * total, ones, precision=HIGHEST, preferred_element_type=jnp.float32
-        )
-        result = numerator / (denominator + attn_eps) * live
+        high, low = halves(query_ref[:, tile * LANES : (tile + 1) * LANES])
+        main = jnp.dot(high, factor_ref[tile], preferred_element_type=jnp.float32)
+        small = jnp.dot(
+            low, factor_ref[tile, :, : 2 * LANES], preferred_element_type=jnp.float32
+        )
+        total = main[:, 2 * LANES :] + small + main[:, : 2 * LANES]
+        result = total[:, :LANES] / (total[:, LANES:] + attn_eps) * live
         out_ref[0, :, tile * LANES : (tile + 1) * LANES] = result.astype(jnp.bfloat16)
 
 
-def compute_state(place, live, hidden, first, second, chunks):
+def compute_state(place, live, hidden, first, chunks):
     tokens, contraction = hidden[0].shape
-    wide = first[0].shape[2] // 2
+    wide = (first[0].shape[2] - LANES) // 2
     tiles = wide // LANES + 1
     slots = -(-(HDIM // chunks + 1) * tiles // 8) * 8
     return pl.pallas_call(
         state_kernel,
-        in_specs=[SMEM, SMEM] + [HBM] * (TEAM + len(first) + len(second)),
+        in_specs=[SMEM, SMEM] + [HBM] * (TEAM + len(first)),
         out_specs=VMEM,
         out_shape=jax.ShapeDtypeStruct((chunks, slots, LANES), jnp.float32),
         scratch_shapes=[
             pltpu.VMEM((TEAM * tokens, wide + LANES), jnp.float32),
             pltpu.VMEM((TEAM * tokens, wide), jnp.float32),
-            pltpu.VMEM((contraction, 2 * wide), jnp.bfloat16),
-            pltpu.VMEM((contraction, LANES), jnp.bfloat16),
+            pltpu.VMEM((contraction, 2 * wide + LANES), jnp.bfloat16),
             pltpu.VMEM((TEAM, tokens, contraction), jnp.bfloat16),
-            pltpu.SemaphoreType.DMA((16,)),
             pltpu.SemaphoreType.DMA((16,)),
             pltpu.SemaphoreType.DMA((TEAM,)),
         ],
         compiler_params=PARAMS,
         name="state",
-    )(place, live, *hidden, *first, *second)
+    )(place, live, *hidden, *first)
 
 
 def compute_queries(place, hidden, second):
@@ -247,6 +252,7 @@
                 pl.BlockSpec(state.shape, lambda i, slots, live: (0, 0, 0)),
             ],
             out_specs=pl.BlockSpec((1, tokens, width), lambda i, slots, live: (slots[i], 0, 0)),
+            scratch_shapes=[pltpu.VMEM((width // LANES, LANES, 4 * LANES), jnp.bfloat16)],
         ),
         out_shape=jax.ShapeDtypeStruct((TEAM, tokens, width), jnp.bfloat16),
         compiler_params=PARAMS,
@@ -306,19 +312,20 @@
         return chosen
 
     query_cols, key_cols, value_cols = pick(0), pick(1), pick(2)
-    first = jnp.concatenate([key_cols[:, :main], value_cols[:, :main]], axis=1)
-    second = jnp.concatenate(
+    first = jnp.concatenate(
         [
-            query_cols[:, :main],
+            key_cols[:, :main],
+            value_cols[:, :main],
             key_cols[:, main:],
             value_cols[:, main:],
-            query_cols[:, main:],
-            jnp.zeros((padded, LANES - 3 * rest), jnp.bfloat16),
+            jnp.zeros((padded, LANES - 2 * rest), jnp.bfloat16),
         ],
         axis=1,
     )
+    second = jnp.pad(query_cols, ((0, 0), (0, LANES - rest)))
+    first, tokens = lax.optimization_barrier((first, tokens))
     first_near = spread(first, side, "img", x_groups)
-    second, tokens, first_near = lax.optimization_barrier((second, tokens, first_near))
+    second, first_near = lax.optimization_barrier((second, first_near))
     second_near = spread(second, side, "img", y_groups)
     first_pieces = far_stage(first_near, side, 3 * side, img_size)
     second_pieces = far_stage(second_near, 1, 3, img_size)
@@ -342,7 +349,7 @@
     hidden = hidden.reshape(grid_rows, img_size * padded, grid_cols)
     mine = jnp.transpose(hidden, (0, 2, 1)).reshape(token_count, img_size * padded)
     beside = exchange(mine, 2, "seq", seq_size)
-    late, _ = lax.optimization_barrier((beside, first_pieces[1:3] + second_pieces[1:3]))
+    late, _ = lax.optimization_barrier((beside, first_pieces[1:3]))
     across = exchange(late, 1, "seq", seq_size)
     hidden = (mine, exchange(mine, 1, "seq", seq_size), beside, across)
 
@@ -350,7 +357,7 @@
     first_row = (seq_at - rank + slots) * grid_rows
     live = jnp.clip(bucket_rows[0] - first_row, 0, grid_rows) * grid_cols
 
-    part = compute_state(place, live, hidden, first_pieces, second_pieces, teams)
+    part = compute_state(place, live, hidden, first_pieces, teams)
     part = lax.all_to_all(part, "seq", 0, 0, axis_index_groups=same_rank)
     state = spread(jnp.sum(part, axis=0), teams, "seq", same_rank)
     queries = compute_queries(place, hidden, second_pieces)

time: 218 us -> 224 us (1.028)
  Pallas kernels: 32.2 us -> 28.9 us
  starting transfers between devices: 50.6 us -> 53.7 us
  local copies, waits for them, and re-layouts: 18.1 us -> 21 us
    all_to_all x3, waiting for transfers between devices: 10.9 us -> 21.2 us  [spread(): return lax.all_to_all(copies, axis, 0, 0, axis_index_groups=groups)]
    all_to_all x1, waiting for transfers between devices: 11.7 us -> 4.38 us  [body(): part = lax.all_to_all(part, 'seq', 0, 0, axis_index_groups=same_rank)]
    all_to_all x3, starting transfers between devices: 11.5 us -> 15.6 us  [spread(): return lax.all_to_all(copies, axis, 0, 0, axis_index_groups=groups)]
  transfers between devices with their start and end apart: 15 -> 15, of which waited for: 8 -> 7; matrix products, arithmetic and copies ran while one was open for 5% -> 5% of each run, Pallas kernels for 5% -> 10%
where the time goes in v3:
time: 224 us; the launch traced here: 222 us
  blocking collectives  64.2 us (29%)
  starting transfers between devices  53.7 us (24%)
  waiting for transfers between devices  46.6 us (21%)
  Pallas kernels  28.9 us (13%)
  local copies, waits for them, and re-layouts  21 us (9%)
  other arithmetic  6.3 us (3%)
    all_gather x1, blocking collectives, body(): gathered = lax.all_gather(w_qkv, 'seq', axis=0)  41 us
    ppermute x11, starting transfers between devices, exchange(): return lax.ppermute(block, axis, [(i, i ^ mask) for i in range(count)])  31.8 us
    all_to_all x1, blocking collectives, body(): result = lax.all_to_all(result, 'seq', 0, 0, axis_index_groups=team)  23.2 us
    all_to_all x3, waiting for transfers between devices, spread(): return lax.all_to_all(copies, axis, 0, 0, axis_index_groups=groups)  21.2 us
    ppermute x11, waiting for transfers between devices, exchange(): return lax.ppermute(block, axis, [(i, i ^ mask) for i in range(count)])  21 us
    all_to_all x3, starting transfers between devices, spread(): return lax.all_to_all(copies, axis, 0, 0, axis_index_groups=groups)  15.6 us
    pallas_call x1, Pallas kernels, compute_state(): pl.pallas_call(state_kernel, in_specs=[SMEM, SMEM] + [HBM] * (TEAM + len(...  13.5 us
    pallas_call x1, Pallas kernels, compute_queries(): pl.pallas_call(query_kernel, in_specs=[SMEM] + [HBM] * (TEAM + len(second...  9.67 us
  transfers between devices with their start and end apart: 15, of which 7 were waited for; matrix products, arithmetic and copies ran while one was open for 5% of the time, Pallas kernels for 10%

profile of v3, /device:TPU:1, one launch (start us, length us, event | category | flops | bytes accessed | tf_op | source)
XLA Modules:
  0.0 222.5 jit_solution(8787150270740677562)
XLA Ops:
  0.0 41.0 %all-gather.1 = bf16[32,140,108]{2,1,0:T(8,128)(2,1)S(1)} all-gather(bf16[1,140,108]{2,1,0:T(8,128)(2,1)} %bitcast.23), channel_id=2, replica_groups=mesh['seq'=32,'img'=16] {'seq'}, dimensions={0}, use_global_device_ids=true | all-gather | bytes 997920 | tf_op jit(solution)/shard_map/all_gather | solution.py:303
  41.3 3.6 %reshape.32 = bf16[140,3456]{1,0:T(8,128)(2,1)} reshape(bf16[140,32,108]{2,1,0:T(8,128)(2,1)S(1)} %copy.15) | data formatting | bytes 1935360 | tf_op jit(solution)/shard_map/reshape | solution.py:304
  44.9 2.8 %select_select_fusion = (bf16[144,288]{1,0:T(8,128)(2,1)}, bf16[144,288]{1,0:T(8,128)(2,1)S(1)}, bf16[144,288]{1,0:T(8,128)(2,1)S(1)}) fusion(bf16[140,3456]{1,0:T(8,128)(2,1)} %reshape.32, pred[]{:T(512)S(6)} %eq.20, pred[]{:T(512)S(6)} %eq.10, pred[]{:T(512)S(6)} %eq.9), kind=kLoop, calls=%fused_computation.8 | loop fusion | flops 373248 | bytes 1216515 | tf_op jit(solution)/shard_map/jit(_where)/select_n | solution.py:311
  56.2 4.2 %all-to-all-start = ((bf16[4,144,640]{2,1,0:T(8,128)(2,1)}), bf16[4,144,640]{2,1,0:T(8,128)(2,1)}, u32[]{:S(2)}, u32[]{:S(2)}) async-start(bf16[4,144,640]{2,1,0:T(8,128)(2,1)} %broadcast_in_dim.9), calls=%async_computation | async-start | bytes 1474560 | tf_op jit(solution)/shard_map/all_to_all | solution.py:265
  62.0 10.0 %all-to-all-done.refs_4_ = bf16[4,144,640]{2,1,0:T(8,128)(2,1)} async-done(((bf16[4,144,640]{2,1,0:T(8,128)(2,1)}), bf16[4,144,640]{2,1,0:T(8,128)(2,1)}, u32[]{:S(2)}, u32[]{:S(2)}) %all-to-all-start) | async-done | bytes 737312 | tf_op jit(solution)/shard_map/all_to_all | solution.py:265
  72.0 3.2 %collective-permute-start.2 = (bf16[4,144,640]{2,1,0:T(8,128)(2,1)}, bf16[4,144,640]{2,1,0:T(8,128)(2,1)S(1)}, u32[]{:S(2)}, u32[]{:S(2)}) collective-permute-start(bf16[4,144,640]{2,1,0:T(8,128)(2,1)} %all-to-all-done.refs_4_), channel_id=1, source_target_pairs={{0,4},{1,5},{2,6},{3,7},{4,0},{5,1},{6,2},{7,3},{8,12},{9,13},{10,... | collective-permute-start | bytes 2211848 | tf_op jit(solution)/shard_map/ppermute | solution.py:269
  75.2 3.8 %collective-permute-start.3 = (bf16[4,144,640]{2,1,0:T(8,128)(2,1)}, bf16[4,144,640]{2,1,0:T(8,128)(2,1)S(1)}, u32[]{:S(2)}, u32[]{:S(2)}) collective-permute-start(bf16[4,144,640]{2,1,0:T(8,128)(2,1)} %all-to-all-done.refs_4_), channel_id=1, source_target_pairs={{0,12},{1,13},{2,14},{3,15},{4,8},{5,9},{6,10},{7,11},{8,4},{9,5},... | collective-permute-start | bytes 2211848 | tf_op jit(solution)/shard_map/ppermute | solution.py:269
  79.0 3.6 %collective-permute-start = (bf16[384,2304]{1,0:T(8,128)(2,1)S(1)}, bf16[384,2304]{1,0:T(8,128)(2,1)}, u32[]{:S(2)}, u32[]{:S(2)}) collective-permute-start(bf16[384,2304]{1,0:T(8,128)(2,1)S(1)} %bitcast.18), channel_id=1, source_target_pairs={{0,16},{16,0},{32,48},{48,32},{64,80},{80,64},{96,112},{112,96},{1... | collective-permute-start | bytes 5308424 | tf_op jit(solution)/shard_map/ppermute | solution.py:269
  82.7 8.3 %collective-permute-done.2.refs_5_ = bf16[4,144,640]{2,1,0:T(8,128)(2,1)S(1)} collective-permute-done((bf16[4,144,640]{2,1,0:T(8,128)(2,1)}, bf16[4,144,640]{2,1,0:T(8,128)(2,1)S(1)}, u32[]{:S(2)}, u32[]{:S(2)}) %collective-permute-start.2) | collective-permute-done | bytes 737312 | tf_op jit(solution)/shard_map/ppermute | solution.py:269
  91.0 4.1 %collective-permute-done.3.refs_6_ = bf16[4,144,640]{2,1,0:T(8,128)(2,1)S(1)} collective-permute-done((bf16[4,144,640]{2,1,0:T(8,128)(2,1)}, bf16[4,144,640]{2,1,0:T(8,128)(2,1)S(1)}, u32[]{:S(2)}, u32[]{:S(2)}) %collective-permute-start.3) | collective-permute-done | bytes 737312 | tf_op jit(solution)/shard_map/ppermute | solution.py:269
  95.1 4.2 %collective-permute-start.4 = (bf16[384,2304]{1,0:T(8,128)(2,1)S(1)}, bf16[384,2304]{1,0:T(8,128)(2,1)}, u32[]{:S(2)}, u32[]{:S(2)}) collective-permute-start(bf16[384,2304]{1,0:T(8,128)(2,1)S(1)} %collective-permute-done.1.refs_2_), channel_id=1, source_target_pairs={{0,16},{16,0},{32,48},{48,32},{64,80},{80,64},{96,112},{112,96},{1... | collective-permute-start | bytes 5308424 | tf_op jit(solution)/shard_map/ppermute | solution.py:269
  103.8 4.3 %all-to-all-start.1 = ((bf16[4,144,384]{2,1,0:T(8,128)(2,1)}), bf16[4,144,384]{2,1,0:T(8,128)(2,1)}, u32[]{:S(2)}, u32[]{:S(2)}) async-start(bf16[4,144,384]{2,1,0:T(8,128)(2,1)} %broadcast_in_dim.10), calls=%async_computation.1 | async-start | bytes 884736 | tf_op jit(solution)/shard_map/all_to_all | solution.py:265
  108.8 10.0 %all-to-all-done.1.refs_4_ = bf16[4,144,384]{2,1,0:T(8,128)(2,1)} async-done(((bf16[4,144,384]{2,1,0:T(8,128)(2,1)}), bf16[4,144,384]{2,1,0:T(8,128)(2,1)}, u32[]{:S(2)}, u32[]{:S(2)}) %all-to-all-start.1) | async-done | bytes 442400 | tf_op jit(solution)/shard_map/all_to_all | solution.py:265
  118.8 2.2 collective-permute-start.5
  121.0 3.4 %collective-permute-start.6 = (bf16[4,144,384]{2,1,0:T(8,128)(2,1)}, bf16[4,144,384]{2,1,0:T(8,128)(2,1)}, u32[]{:S(2)}, u32[]{:S(2)}) collective-permute-start(bf16[4,144,384]{2,1,0:T(8,128)(2,1)} %all-to-all-done.1.refs_4_), channel_id=1, source_target_pairs={{0,3},{1,2},{2,1},{3,0},{4,7},{5,6},{6,5},{7,4},{8,11},{9,10},{10,... | collective-permute-start | bytes 1327112 | tf_op jit(solution)/shard_map/ppermute | solution.py:269
  128.7 8.5 %collective-permute-done.9.refs_7_ = bf16[2,144,640]{2,1,0:T(8,128)(2,1)S(1)} collective-permute-done((bf16[2,144,640]{2,1,0:T(8,128)(2,1)S(1)}, bf16[2,144,640]{2,1,0:T(8,128)(2,1)S(1)}, u32[]{:S(2)}, u32[]{:S(2)}) %collective-permute-start.9) | collective-permute-done | bytes 368672 | tf_op jit(solution)/shard_map/ppermute | solution.py:269
  138.0 13.5 %state.1 = f32[8,16,128]{2,1,0:T(8,128)} custom-call(s32[32]{0:T(128)} %pad_add_fusion.place_ref, s32[4]{0:T(128)} %clamp_multiply_fusion.live_ref, bf16[384,2304]{1,0:T(8,128)(2,1)} %bitcast.19, bf16[384,2304]{1,0:T(8,128)(2,1)} %collective-permute-done.refs_1_, bf16[384,2304]{1,0:T(8,128)(2,1)} %copy-done.1, ...), custom_call_target="tpu_custom_call" | custom-call | tf_op jit(solution)/shard_map/state/pallas_call | solution.py:201
  151.5 6.3 %all-to-all-start.2 = ((f32[8,16,128]{2,1,0:T(8,128)}), f32[8,16,128]{2,1,0:T(8,128)S(1)}, u32[]{:S(2)}, u32[]{:S(2)}) async-start(f32[8,16,128]{2,1,0:T(8,128)} %state.1), calls=%async_computation.2 | async-start | bytes 131072 | tf_op jit(solution)/shard_map/all_to_all | solution.py:361
  158.8 3.5 %collective-permute-start.7 = (bf16[2,144,384]{2,1,0:T(8,128)(2,1)S(1)}, bf16[2,144,384]{2,1,0:T(8,128)(2,1)S(1)}, u32[]{:S(2)}, u32[]{:S(2)}) collective-permute-start(bf16[2,144,384]{2,1,0:T(8,128)(2,1)S(1)} %slice.88), channel_id=1, source_target_pairs={{0,3},{1,2},{2,1},{3,0},{4,7},{5,6},{6,5},{7,4},{8,11},{9,10},{10,... | collective-permute-start | bytes 663560 | tf_op jit(solution)/shard_map/ppermute | solution.py:269
  165.9 4.4 %all-to-all-done.2 = f32[8,16,128]{2,1,0:T(8,128)S(1)} async-done(((f32[8,16,128]{2,1,0:T(8,128)}), f32[8,16,128]{2,1,0:T(8,128)S(1)}, u32[]{:S(2)}, u32[]{:S(2)}) %all-to-all-start.2) | async-done | bytes 65568 | tf_op jit(solution)/shard_map/all_to_all | solution.py:361
  170.9 7.1 %all-to-all-start.3 = ((f32[8,16,128]{2,1,0:T(8,128)}), f32[8,16,128]{2,1,0:T(8,128)S(1)}, u32[]{:S(2)}, u32[]{:S(2)}) async-start(f32[8,16,128]{2,1,0:T(8,128)} %broadcast_in_dim.11), calls=%async_computation.3 | async-start | bytes 131072 | tf_op jit(solution)/shard_map/all_to_all | solution.py:265
  179.3 9.7 %queries.1.query_ref = f32[1536,384]{1,0:T(8,128)} custom-call(s32[32]{0:T(128)} %pad_add_fusion.place_ref, bf16[384,2304]{1,0:T(8,128)(2,1)} %bitcast.20, bf16[384,2304]{1,0:T(8,128)(2,1)} %collective-permute-done.refs_1_, bf16[384,2304]{1,0:T(8,128)(2,1)} %copy-done.1, bf16[384,2304]{1,0:T(8,128)(2,1)} %collective-permute-done.4.refs_3_, ...), custom_call_target="tpu_custom_call" | custom-call | flops 2717908992 | bytes 11206656 | tf_op jit(solution)/shard_map/queries/pallas_call | solution.py:222
  190.8 5.7 %attend.1 = bf16[4,384,384]{2,1,0:T(8,128)(2,1)} custom-call(s32[4]{0:T(128)} %iota_xor_fusion.slot_ref, s32[4]{0:T(128)} %clamp_multiply_fusion.live_ref, f32[1536,384]{1,0:T(8,128)} %queries.1.query_ref, f32[8,16,128]{2,1,0:T(8,128)} %copy-done.6), custom_call_target="tpu_custom_call" | custom-call | tf_op jit(solution)/shard_map/attend/pallas_call | solution.py:245
  196.5 23.2 %all_to_all.25 = bf16[4,384,384]{2,1,0:T(8,128)(2,1)S(1)} all-to-all(bf16[4,384,384]{2,1,0:T(8,128)(2,1)} %attend.1), channel_id=1, replica_groups={{0,16,32,48},{64,80,96,112},{128,144,160,176},{192,208,224,240},{256,27..., dimensions={0} | all-to-all | bytes 2359296 | tf_op jit(solution)/shard_map/all_to_all | solution.py:366
  (75 shorter events, 30.0 us)
Async XLA Ops:
  41.3 7.3 %copy-start.2 = (bf16[1,3,128,2240]{2,3,1,0:T(8,128)(2,1)S(1)}, bf16[1,3,128,2240]{2,3,1,0:T(8,128)(2,1)}, u32[]{:S(2)}) copy-start(bf16[1,3,128,2240]{2,3,1,0:T(8,128)(2,1)} %param.10) | copy-start | bytes 5160964
  44.9 4.7 %copy-start.10 = (bf16[2240]{0:T(1024)(128)(2,1)S(1)}, bf16[2240]{0:T(1024)(128)(2,1)}, u32[]{:S(2)}) copy-start(bf16[2240]{0:T(1024)(128)(2,1)} %param.11) | copy-start | bytes 13444
  44.9 4.7 %copy-start.9 = (bf16[1,2240]{1,0:T(2,128)(2,1)S(1)}, bf16[1,2240]{1,0:T(2,128)(2,1)}, u32[]{:S(2)}) copy-start(bf16[1,2240]{1,0:T(2,128)(2,1)} %param.12) | copy-start | bytes 13444
  44.9 4.8 %copy-start.11 = (bf16[2240]{0:T(1024)(128)(2,1)S(1)}, bf16[2240]{0:T(1024)(128)(2,1)}, u32[]{:S(2)}) copy-start(bf16[2240]{0:T(1024)(128)(2,1)} %param.13) | copy-start | bytes 13444
  52.4 51.4 %copy-start = (bf16[3,128,2304]{2,1,0:T(8,128)(2,1)}, bf16[3,128,2304]{2,1,0:T(8,128)(2,1)S(1)}, u32[]{:S(2)}) copy-start(bf16[3,128,2304]{2,1,0:T(8,128)(2,1)S(1)} %copy.16) | copy-start | bytes 5308420
  52.4 42.7 %collective-permute-start.1 = (bf16[384,2304]{1,0:T(8,128)(2,1)S(1)}, bf16[384,2304]{1,0:T(8,128)(2,1)S(1)}, u32[]{:S(2)}, u32[]{:S(2)}) collective-permute-start(bf16[384,2304]{1,0:T(8,128)(2,1)S(1)} %bitcast.17), channel_id=1, source_target_pairs={{0,32},{16,48},{32,0},{48,16},{64,96},{80,112},{96,64},{112,80},{1... | collective-permute-start | bytes 5308424 | tf_op jit(solution)/shard_map/ppermute | solution.py:269
  56.2 15.8 %all-to-all-start = ((bf16[4,144,640]{2,1,0:T(8,128)(2,1)}), bf16[4,144,640]{2,1,0:T(8,128)(2,1)}, u32[]{:S(2)}, u32[]{:S(2)}) async-start(bf16[4,144,640]{2,1,0:T(8,128)(2,1)} %broadcast_in_dim.9), calls=%async_computation | async-start | bytes 1474560 | tf_op jit(solution)/shard_map/all_to_all | solution.py:265
  60.4 67.2 %copy-start.12 = (s32[16]{0:T(128)S(1)}, s32[16]{0:T(128)}, u32[]{:S(2)}) copy-start(s32[16]{0:T(128)} %constant.65.clone) | copy-start | bytes 196
  60.4 67.2 %copy-start.13 = (s32[16]{0:T(128)S(1)}, s32[16]{0:T(128)}, u32[]{:S(2)}) copy-start(s32[16]{0:T(128)} %constant.66.clone) | copy-start | bytes 196
  60.4 67.2 %copy-start.14 = (s32[16]{0:T(128)S(1)}, s32[16]{0:T(128)}, u32[]{:S(2)}) copy-start(s32[16]{0:T(128)} %constant.67.clone) | copy-start | bytes 196
  72.0 19.0 %collective-permute-start.2 = (bf16[4,144,640]{2,1,0:T(8,128)(2,1)}, bf16[4,144,640]{2,1,0:T(8,128)(2,1)S(1)}, u32[]{:S(2)}, u32[]{:S(2)}) collective-permute-start(bf16[4,144,640]{2,1,0:T(8,128)(2,1)} %all-to-all-done.refs_4_), channel_id=1, source_target_pairs={{0,4},{1,5},{2,6},{3,7},{4,0},{5,1},{6,2},{7,3},{8,12},{9,13},{10,... | collective-permute-start | bytes 2211848 | tf_op jit(solution)/shard_map/ppermute | solution.py:269
  75.2 19.9 %collective-permute-start.3 = (bf16[4,144,640]{2,1,0:T(8,128)(2,1)}, bf16[4,144,640]{2,1,0:T(8,128)(2,1)S(1)}, u32[]{:S(2)}, u32[]{:S(2)}) collective-permute-start(bf16[4,144,640]{2,1,0:T(8,128)(2,1)} %all-to-all-done.refs_4_), channel_id=1, source_target_pairs={{0,12},{1,13},{2,14},{3,15},{4,8},{5,9},{6,10},{7,11},{8,4},{9,5},... | collective-permute-start | bytes 2211848 | tf_op jit(solution)/shard_map/ppermute | solution.py:269
  79.0 58.2 %collective-permute-start = (bf16[384,2304]{1,0:T(8,128)(2,1)S(1)}, bf16[384,2304]{1,0:T(8,128)(2,1)}, u32[]{:S(2)}, u32[]{:S(2)}) collective-permute-start(bf16[384,2304]{1,0:T(8,128)(2,1)S(1)} %bitcast.18), channel_id=1, source_target_pairs={{0,16},{16,0},{32,48},{48,32},{64,80},{80,64},{96,112},{112,96},{1... | collective-permute-start | bytes 5308424 | tf_op jit(solution)/shard_map/ppermute | solution.py:269
  95.1 42.1 %copy-start.1 = (bf16[384,2304]{1,0:T(8,128)(2,1)}, bf16[384,2304]{1,0:T(8,128)(2,1)S(1)}, u32[]{:S(2)}) copy-start(bf16[384,2304]{1,0:T(8,128)(2,1)S(1)} %collective-permute-done.1.refs_2_) | copy-start | bytes 5308420
  95.1 42.1 %collective-permute-start.4 = (bf16[384,2304]{1,0:T(8,128)(2,1)S(1)}, bf16[384,2304]{1,0:T(8,128)(2,1)}, u32[]{:S(2)}, u32[]{:S(2)}) collective-permute-start(bf16[384,2304]{1,0:T(8,128)(2,1)S(1)} %collective-permute-done.1.refs_2_), channel_id=1, source_target_pairs={{0,16},{16,0},{32,48},{48,32},{64,80},{80,64},{96,112},{112,96},{1... | collective-permute-start | bytes 5308424 | tf_op jit(solution)/shard_map/ppermute | solution.py:269
  100.1 25.3 %collective-permute-start.10 = (bf16[2,144,640]{2,1,0:T(8,128)(2,1)}, bf16[2,144,640]{2,1,0:T(8,128)(2,1)}, u32[]{:S(2)}, u32[]{:S(2)}) collective-permute-start(bf16[2,144,640]{2,1,0:T(8,128)(2,1)} %slice.91), channel_id=1, source_target_pairs={{0,4},{1,5},{2,6},{3,7},{4,0},{5,1},{6,2},{7,3},{8,12},{9,13},{10,... | collective-permute-start | bytes 1105928 | tf_op jit(solution)/shard_map/ppermute | solution.py:269
  103.8 15.0 %all-to-all-start.1 = ((bf16[4,144,384]{2,1,0:T(8,128)(2,1)}), bf16[4,144,384]{2,1,0:T(8,128)(2,1)}, u32[]{:S(2)}, u32[]{:S(2)}) async-start(bf16[4,144,384]{2,1,0:T(8,128)(2,1)} %broadcast_in_dim.10), calls=%async_computation.1 | async-start | bytes 884736 | tf_op jit(solution)/shard_map/all_to_all | solution.py:265
  118.8 39.0 %collective-permute-start.5 = (bf16[4,144,384]{2,1,0:T(8,128)(2,1)}, bf16[4,144,384]{2,1,0:T(8,128)(2,1)}, u32[]{:S(2)}, u32[]{:S(2)}) collective-permute-start(bf16[4,144,384]{2,1,0:T(8,128)(2,1)} %all-to-all-done.1.refs_4_), channel_id=1, source_target_pairs={{0,1},{1,0},{2,3},{3,2},{4,5},{5,4},{6,7},{7,6},{8,9},{9,8},{10,11... | collective-permute-start | bytes 1327112 | tf_op jit(solution)/shard_map/ppermute | solution.py:269
  121.0 41.3 %collective-permute-start.6 = (bf16[4,144,384]{2,1,0:T(8,128)(2,1)}, bf16[4,144,384]{2,1,0:T(8,128)(2,1)}, u32[]{:S(2)}, u32[]{:S(2)}) collective-permute-start(bf16[4,144,384]{2,1,0:T(8,128)(2,1)} %all-to-all-done.1.refs_4_), channel_id=1, source_target_pairs={{0,3},{1,2},{2,1},{3,0},{4,7},{5,6},{6,5},{7,4},{8,11},{9,10},{10,... | collective-permute-start | bytes 1327112 | tf_op jit(solution)/shard_map/ppermute | solution.py:269
  125.4 11.8 %collective-permute-start.9 = (bf16[2,144,640]{2,1,0:T(8,128)(2,1)S(1)}, bf16[2,144,640]{2,1,0:T(8,128)(2,1)S(1)}, u32[]{:S(2)}, u32[]{:S(2)}) collective-permute-start(bf16[2,144,640]{2,1,0:T(8,128)(2,1)S(1)} %slice.90), channel_id=1, source_target_pairs={{0,12},{1,13},{2,14},{3,15},{4,8},{5,9},{6,10},{7,11},{8,4},{9,5},... | collective-permute-start | bytes 1105928 | tf_op jit(solution)/shard_map/ppermute | solution.py:269
  151.5 18.7 %all-to-all-start.2 = ((f32[8,16,128]{2,1,0:T(8,128)}), f32[8,16,128]{2,1,0:T(8,128)S(1)}, u32[]{:S(2)}, u32[]{:S(2)}) async-start(f32[8,16,128]{2,1,0:T(8,128)} %state.1), calls=%async_computation.2 | async-start | bytes 131072 | tf_op jit(solution)/shard_map/all_to_all | solution.py:361
  158.8 19.1 %collective-permute-start.7 = (bf16[2,144,384]{2,1,0:T(8,128)(2,1)S(1)}, bf16[2,144,384]{2,1,0:T(8,128)(2,1)S(1)}, u32[]{:S(2)}, u32[]{:S(2)}) collective-permute-start(bf16[2,144,384]{2,1,0:T(8,128)(2,1)S(1)} %slice.88), channel_id=1, source_target_pairs={{0,3},{1,2},{2,1},{3,0},{4,7},{5,6},{6,5},{7,4},{8,11},{9,10},{10,... | collective-permute-start | bytes 663560 | tf_op jit(solution)/shard_map/ppermute | solution.py:269
  163.3 14.6 %collective-permute-start.8 = (bf16[2,144,384]{2,1,0:T(8,128)(2,1)S(1)}, bf16[2,144,384]{2,1,0:T(8,128)(2,1)S(1)}, u32[]{:S(2)}, u32[]{:S(2)}) collective-permute-start(bf16[2,144,384]{2,1,0:T(8,128)(2,1)S(1)} %slice.89), channel_id=1, source_target_pairs={{0,1},{1,0},{2,3},{3,2},{4,5},{5,4},{6,7},{7,6},{8,9},{9,8},{10,11... | collective-permute-start | bytes 663560 | tf_op jit(solution)/shard_map/ppermute | solution.py:269
  170.9 19.3 %all-to-all-start.3 = ((f32[8,16,128]{2,1,0:T(8,128)}), f32[8,16,128]{2,1,0:T(8,128)S(1)}, u32[]{:S(2)}, u32[]{:S(2)}) async-start(f32[8,16,128]{2,1,0:T(8,128)} %broadcast_in_dim.11), calls=%async_computation.3 | async-start | bytes 131072 | tf_op jit(solution)/shard_map/all_to_all | solution.py:265
  (6 other events, 11.2 us)

commit v4 on v3

--- a/solution.py
+++ b/solution.py
@@ -21,7 +21,8 @@
 PARAMS = pltpu.CompilerParams(vmem_limit_bytes=58 * 1024 * 1024)
 
 FAR_MASKS = np.array([0] * 4 + [1] * 4 + [3] * 4 + [2] * 4)
-NEAR_SLOTS = np.array([0, 1, 2, 3] * 3 + [0, 1] + [2, 3])
+NEAR_SLOTS = np.array([0, 1, 2, 3] * 4)
+PIECES = 4
 
 
 def block_mask():
@@ -70,7 +71,7 @@
 
 
 def state_kernel(place_ref, live_ref, *refs):
-    hidden, first, refs = refs[:TEAM], refs[TEAM : TEAM + 5], refs[TEAM + 5 :]
+    hidden, first, refs = refs[:TEAM], refs[TEAM : TEAM + PIECES], refs[TEAM + PIECES :]
     out_ref, keys_ref, values_ref, weights_ref, hidden_ref, sems, hidden_s = refs
     tokens = hidden_ref.shape[1]
     full = values_ref.shape[1] // LANES
@@ -96,9 +97,9 @@
         )
     same_head = block_mask()
     column = lax.broadcasted_iota(jnp.int32, (LANES, LANES), 1)
-    chunks = out_ref.shape[0]
-    rows = HDIM // chunks
     tiles = full + 1
+    tail = full * HDIM
+    fold = HDIM // GROUP
     out_ref[...] = jnp.zeros_like(out_ref)
     for tile in range(tiles):
         keys = keys_ref[:, tile * LANES : (tile + 1) * LANES]
@@ -127,19 +128,23 @@
         packed = outer[:HDIM]
         for head in range(1, GROUP):
             packed = packed + outer[head * HDIM : (head + 1) * HDIM]
-        total = jnp.sum(keys, axis=0, keepdims=True)
-        for chunk in range(chunks):
-            for row in range(rows):
-                source = chunk * rows + row
-                target = row * tiles + tile
-                out_ref[chunk, target : target + 1, :] = packed[source : source + 1]
-            target = rows * tiles + tile
-            out_ref[chunk, target : target + 1, :] = total
+        if tile < full:
+            out_ref[tile * HDIM : (tile + 1) * HDIM, :] = packed
+        else:
+            folded = packed[:fold]
+            for part in range(1, GROUP):
+                folded = folded + pltpu.roll(
+                    packed[part * fold : (part + 1) * fold], part * HDIM, 1
+                )
+            out_ref[tail : tail + fold, :] = folded
+        out_ref[tail + fold + tile : tail + fold + tile + 1, :] = jnp.sum(
+            keys, axis=0, keepdims=True
+        )
 
 
 def query_kernel(place_ref, *refs):
     hidden, refs = refs[:TEAM], refs[TEAM:]
-    second, refs = refs[:5], refs[5:]
+    second, refs = refs[:PIECES], refs[PIECES:]
     out_ref, weights_ref, hidden_ref, sems, hidden_s = refs
     tokens = hidden_ref.shape[1]
     copies = load_blocks(place_ref, 16, second, 0, weights_ref, sems)
@@ -158,23 +163,25 @@
 def attend_kernel(slot_ref, live_ref, query_ref, state_ref, out_ref, factor_ref):
     tokens = query_ref.shape[0]
     tiles = query_ref.shape[1] // LANES
-    chunks = state_ref.shape[0]
-    rows = HDIM // chunks
+    tail = (tiles - 1) * HDIM
+    fold = HDIM // GROUP
 
     @pl.when(pl.program_id(0) == 0)
     def _():
         same_head = block_mask()
+        summed = jnp.sum(state_ref[...], axis=0)
         for tile in range(tiles):
-            packed = jnp.concatenate(
-                [
-                    state_ref[chunk, row * tiles + tile : row * tiles + tile + 1, :]
-                    for chunk in range(chunks)
-                    for row in range(rows)
-                ],
-                axis=0,
-            )
+            if tile < tiles - 1:
+                packed = summed[tile * HDIM : (tile + 1) * HDIM]
+            else:
+                folded = summed[tail : tail + fold]
+                packed = jnp.concatenate(
+                    [folded]
+                    + [pltpu.roll(folded, LANES - part * HDIM, 1) for part in range(1, GROUP)],
+                    axis=0,
+                )
             state = jnp.where(same_head, jnp.concatenate([packed] * GROUP, axis=0), 0.0)
-            total = state_ref[0, rows * tiles + tile : rows * tiles + tile + 1, :]
+            total = summed[tail + fold + tile : tail + fold + tile + 1]
             total = jnp.transpose(jnp.broadcast_to(total, (LANES, LANES)))
             total = jnp.where(same_head, total, 0.0)
             high, low = halves(jnp.concatenate([state, total], axis=1))
@@ -193,16 +200,16 @@
         out_ref[0, :, tile * LANES : (tile + 1) * LANES] = result.astype(jnp.bfloat16)
 
 
-def compute_state(place, live, hidden, first, chunks):
+def compute_state(place, live, hidden, first):
     tokens, contraction = hidden[0].shape
     wide = (first[0].shape[2] - LANES) // 2
     tiles = wide // LANES + 1
-    slots = -(-(HDIM // chunks + 1) * tiles // 8) * 8
+    slots = -(-((tiles - 1) * HDIM + HDIM // GROUP + tiles) // 8) * 8
     return pl.pallas_call(
         state_kernel,
         in_specs=[SMEM, SMEM] + [HBM] * (TEAM + len(first)),
         out_specs=VMEM,
-        out_shape=jax.ShapeDtypeStruct((chunks, slots, LANES), jnp.float32),
+        out_shape=jax.ShapeDtypeStruct((slots, LANES), jnp.float32),
         scratch_shapes=[
             pltpu.VMEM((TEAM * tokens, wide + LANES), jnp.float32),
             pltpu.VMEM((TEAM * tokens, wide), jnp.float32),
@@ -270,12 +277,10 @@
 
 
 def far_stage(held, one, two, count):
-    middle = held.shape[0] // 2
     from_one = exchange(held, one, "img", count)
     from_two = exchange(held, two, "img", count)
-    low = exchange(from_one[:middle], two, "img", count)
-    high = exchange(from_two[middle:], one, "img", count)
-    return [held, from_one, from_two, low, high]
+    opposite = exchange(from_one, two, "img", count)
+    return [held, from_one, from_two, opposite]
 
 
 def body(tokens, norm_gain, caption, null_caption, keep, bucket_rows, w_qkv):
@@ -325,10 +330,6 @@
     second = jnp.pad(query_cols, ((0, 0), (0, LANES - rest)))
     first, tokens = lax.optimization_barrier((first, tokens))
     first_near = spread(first, side, "img", x_groups)
-    second, first_near = lax.optimization_barrier((second, first_near))
-    second_near = spread(second, side, "img", y_groups)
-    first_pieces = far_stage(first_near, side, 3 * side, img_size)
-    second_pieces = far_stage(second_near, 1, 3, img_size)
     y_at, x_at = img_at // side, img_at % side
     place = jnp.concatenate(
         [
@@ -336,7 +337,15 @@
             NEAR_SLOTS * side + jnp.bitwise_xor(x_at, FAR_MASKS),
         ]
     ).astype(jnp.int32)
-
+    slots = jnp.bitwise_xor(rank, jnp.arange(TEAM, dtype=jnp.int32))
+    first_row = (seq_at - rank + slots) * grid_rows
+    live = jnp.clip(bucket_rows[0] - first_row, 0, grid_rows) * grid_cols
+    second, first_near, place, live, slots = lax.optimization_barrier(
+        (second, first_near, place, live, slots)
+    )
+    second_near = spread(second, side, "img", y_groups)
+    first_pieces = far_stage(first_near, side, 3 * side, img_size)
+    second_pieces = far_stage(second_near, 1, 3, img_size)
     features = jnp.transpose(tokens[0], (0, 2, 1)).astype(jnp.float32)
     mean_square = jnp.mean(features * features, axis=1, keepdims=True)
     condition = jnp.where(keep[0] > 0, caption[0], null_caption).astype(jnp.float32)
@@ -353,13 +362,8 @@
     across = exchange(late, 1, "seq", seq_size)
     hidden = (mine, exchange(mine, 1, "seq", seq_size), beside, across)
 
-    slots = jnp.bitwise_xor(rank, jnp.arange(TEAM, dtype=jnp.int32))
-    first_row = (seq_at - rank + slots) * grid_rows
-    live = jnp.clip(bucket_rows[0] - first_row, 0, grid_rows) * grid_cols
-
-    part = compute_state(place, live, hidden, first_pieces, teams)
-    part = lax.all_to_all(part, "seq", 0, 0, axis_index_groups=same_rank)
-    state = spread(jnp.sum(part, axis=0), teams, "seq", same_rank)
+    part = compute_state(place, live, hidden, first_pieces)
+    state = spread(part, teams, "seq", same_rank)
     queries = compute_queries(place, hidden, second_pieces)
 
     result = compute_output(slots, live, queries, state)

time: 224 us -> 213 us (0.951)
  starting transfers between devices: 53.7 us -> 43.4 us
  waiting for transfers between devices: 46.6 us -> 51.6 us
  local copies, waits for them, and re-layouts: 21 us -> 17.8 us
    ppermute x11 -> x9, waiting for transfers between devices: 21 us -> 43.4 us  [exchange(): return lax.ppermute(block, axis, [(i, i ^ mask) for i in range(count)])]
    all_to_all x3, waiting for transfers between devices: 21.2 us -> 8.15 us  [spread(): return lax.all_to_all(copies, axis, 0, 0, axis_index_groups=groups)]
    all_to_all x1 -> x0, starting transfers between devices: 6.35 us -> none  [body(): part = lax.all_to_all(part, 'seq', 0, 0, axis_index_groups=same_rank)]
    all_to_all x1 -> x0, waiting for transfers between devices: 4.38 us -> none  [body(): part = lax.all_to_all(part, 'seq', 0, 0, axis_index_groups=same_rank)]
    slice x4 -> x0, local copies, waits for them, and re-layouts: 3.71 us -> none  [the longest x2 1.98 us: far_stage(): low = exchange(from_one[:middle], two, 'img', count)]
    ppermute x11 -> x9, starting transfers between devices: 31.8 us -> 28.2 us  [exchange(): return lax.ppermute(block, axis, [(i, i ^ mask) for i in range(count)])]
  transfers between devices with their start and end apart: 15 -> 12, of which waited for: 7 -> 7; matrix products, arithmetic and copies ran while one was open for 5% -> 3% of each run, Pallas kernels for 10% -> 11%
where the time goes in v4:
time: 213 us; the launch traced here: 212 us
  blocking collectives  62.6 us (29%)
  waiting for transfers between devices  51.6 us (24%)
  starting transfers between devices  43.4 us (20%)
  Pallas kernels  29.1 us (14%)
  local copies, waits for them, and re-layouts  17.8 us (8%)
  other arithmetic  5.76 us (3%)
    ppermute x9, waiting for transfers between devices, exchange(): return lax.ppermute(block, axis, [(i, i ^ mask) for i in range(count)])  43.4 us
    all_gather x1, blocking collectives, body(): gathered = lax.all_gather(w_qkv, 'seq', axis=0)  41 us
    ppermute x9, starting transfers between devices, exchange(): return lax.ppermute(block, axis, [(i, i ^ mask) for i in range(count)])  28.2 us
    all_to_all x1, blocking collectives, body(): result = lax.all_to_all(result, 'seq', 0, 0, axis_index_groups=team)  21.6 us
    all_to_all x3, starting transfers between devices, spread(): return lax.all_to_all(copies, axis, 0, 0, axis_index_groups=groups)  15.2 us
    pallas_call x1, Pallas kernels, compute_state(): pl.pallas_call(state_kernel, in_specs=[SMEM, SMEM] + [HBM] * (TEAM + len(...  13.6 us
    pallas_call x1, Pallas kernels, compute_queries(): pl.pallas_call(query_kernel, in_specs=[SMEM] + [HBM] * (TEAM + len(second...  9.67 us
    all_to_all x3, waiting for transfers between devices, spread(): return lax.all_to_all(copies, axis, 0, 0, axis_index_groups=groups)  8.15 us
  transfers between devices with their start and end apart: 12, of which 7 were waited for; matrix products, arithmetic and copies ran while one was open for 3% of the time, Pallas kernels for 11%

profile of v4, /device:TPU:1, one launch (start us, length us, event | category | flops | bytes accessed | tf_op | source)
XLA Modules:
  0.0 211.9 jit_solution(6636122289613195242)
XLA Ops:
  0.0 41.0 %all-gather.1 = bf16[32,140,108]{2,1,0:T(8,128)(2,1)S(1)} all-gather(bf16[1,140,108]{2,1,0:T(8,128)(2,1)} %bitcast.23), channel_id=2, replica_groups=mesh['seq'=32,'img'=16] {'seq'}, dimensions={0}, use_global_device_ids=true | all-gather | bytes 997920 | tf_op jit(solution)/shard_map/all_gather | solution.py:308
  41.3 3.6 %reshape.32 = bf16[140,3456]{1,0:T(8,128)(2,1)} reshape(bf16[140,32,108]{2,1,0:T(8,128)(2,1)S(1)} %copy.15) | data formatting | bytes 1935360 | tf_op jit(solution)/shard_map/reshape | solution.py:309
  44.9 2.8 %select_select_fusion = (bf16[144,288]{1,0:T(8,128)(2,1)S(1)}, bf16[144,288]{1,0:T(8,128)(2,1)S(1)}, bf16[144,288]{1,0:T(8,128)(2,1)}) fusion(bf16[140,3456]{1,0:T(8,128)(2,1)} %reshape.32, pred[]{:T(512)S(6)} %eq.20, pred[]{:T(512)S(6)} %eq.10, pred[]{:T(512)S(6)} %eq.9), kind=kLoop, calls=%fused_computation.8 | loop fusion | flops 373248 | bytes 1216515 | tf_op jit(solution)/shard_map/jit(_where)/select_n | solution.py:316
  56.4 4.2 %all-to-all-start = ((bf16[4,144,640]{2,1,0:T(8,128)(2,1)}), bf16[4,144,640]{2,1,0:T(8,128)(2,1)}, u32[]{:S(2)}, u32[]{:S(2)}) async-start(bf16[4,144,640]{2,1,0:T(8,128)(2,1)} %broadcast_in_dim.9), calls=%async_computation | async-start | bytes 1474560 | tf_op jit(solution)/shard_map/all_to_all | solution.py:272
  64.0 8.1 %all-to-all-done.refs_4_ = bf16[4,144,640]{2,1,0:T(8,128)(2,1)} async-done(((bf16[4,144,640]{2,1,0:T(8,128)(2,1)}), bf16[4,144,640]{2,1,0:T(8,128)(2,1)}, u32[]{:S(2)}, u32[]{:S(2)}) %all-to-all-start) | async-done | bytes 737312 | tf_op jit(solution)/shard_map/all_to_all | solution.py:272
  72.2 3.2 %collective-permute-start.2 = (bf16[4,144,640]{2,1,0:T(8,128)(2,1)}, bf16[4,144,640]{2,1,0:T(8,128)(2,1)}, u32[]{:S(2)}, u32[]{:S(2)}) collective-permute-start(bf16[4,144,640]{2,1,0:T(8,128)(2,1)} %all-to-all-done.refs_4_), channel_id=1, source_target_pairs={{0,4},{1,5},{2,6},{3,7},{4,0},{5,1},{6,2},{7,3},{8,12},{9,13},{10,... | collective-permute-start | bytes 2211848 | tf_op jit(solution)/shard_map/ppermute | solution.py:276
  75.4 3.8 %collective-permute-start.3 = (bf16[4,144,640]{2,1,0:T(8,128)(2,1)}, bf16[4,144,640]{2,1,0:T(8,128)(2,1)S(1)}, u32[]{:S(2)}, u32[]{:S(2)}) collective-permute-start(bf16[4,144,640]{2,1,0:T(8,128)(2,1)} %all-to-all-done.refs_4_), channel_id=1, source_target_pairs={{0,12},{1,13},{2,14},{3,15},{4,8},{5,9},{6,10},{7,11},{8,4},{9,5},... | collective-permute-start | bytes 2211848 | tf_op jit(solution)/shard_map/ppermute | solution.py:276
  79.2 3.6 %collective-permute-start = (bf16[384,2304]{1,0:T(8,128)(2,1)S(1)}, bf16[384,2304]{1,0:T(8,128)(2,1)}, u32[]{:S(2)}, u32[]{:S(2)}) collective-permute-start(bf16[384,2304]{1,0:T(8,128)(2,1)S(1)} %bitcast.18), channel_id=1, source_target_pairs={{0,16},{16,0},{32,48},{48,32},{64,80},{80,64},{96,112},{112,96},{1... | collective-permute-start | bytes 5308424 | tf_op jit(solution)/shard_map/ppermute | solution.py:276
  82.8 8.4 %collective-permute-done.2.refs_5_ = bf16[4,144,640]{2,1,0:T(8,128)(2,1)} collective-permute-done((bf16[4,144,640]{2,1,0:T(8,128)(2,1)}, bf16[4,144,640]{2,1,0:T(8,128)(2,1)}, u32[]{:S(2)}, u32[]{:S(2)}) %collective-permute-start.2) | collective-permute-done | bytes 737312 | tf_op jit(solution)/shard_map/ppermute | solution.py:276
  91.2 4.0 %collective-permute-done.3.refs_6_ = bf16[4,144,640]{2,1,0:T(8,128)(2,1)S(1)} collective-permute-done((bf16[4,144,640]{2,1,0:T(8,128)(2,1)}, bf16[4,144,640]{2,1,0:T(8,128)(2,1)S(1)}, u32[]{:S(2)}, u32[]{:S(2)}) %collective-permute-start.3) | collective-permute-done | bytes 737312 | tf_op jit(solution)/shard_map/ppermute | solution.py:276
  96.1 4.2 %collective-permute-start.4 = (bf16[384,2304]{1,0:T(8,128)(2,1)S(1)}, bf16[384,2304]{1,0:T(8,128)(2,1)}, u32[]{:S(2)}, u32[]{:S(2)}) collective-permute-start(bf16[384,2304]{1,0:T(8,128)(2,1)S(1)} %collective-permute-done.1.refs_2_), channel_id=1, source_target_pairs={{0,16},{16,0},{32,48},{48,32},{64,80},{80,64},{96,112},{112,96},{1... | collective-permute-start | bytes 5308424 | tf_op jit(solution)/shard_map/ppermute | solution.py:276
  100.4 3.8 %collective-permute-start.8 = (bf16[4,144,640]{2,1,0:T(8,128)(2,1)}, bf16[4,144,640]{2,1,0:T(8,128)(2,1)}, u32[]{:S(2)}, u32[]{:S(2)}) collective-permute-start(bf16[4,144,640]{2,1,0:T(8,128)(2,1)} %collective-permute-done.2.refs_5_), channel_id=1, source_target_pairs={{0,12},{1,13},{2,14},{3,15},{4,8},{5,9},{6,10},{7,11},{8,4},{9,5},... | collective-permute-start | bytes 2211848 | tf_op jit(solution)/shard_map/ppermute | solution.py:276
  105.9 4.3 %all-to-all-start.1 = ((bf16[4,144,384]{2,1,0:T(8,128)(2,1)}), bf16[4,144,384]{2,1,0:T(8,128)(2,1)}, u32[]{:S(2)}, u32[]{:S(2)}) async-start(bf16[4,144,384]{2,1,0:T(8,128)(2,1)} %broadcast_in_dim.10), calls=%async_computation.1 | async-start | bytes 884736 | tf_op jit(solution)/shard_map/all_to_all | solution.py:272
  110.2 13.9 %collective-permute-done.8.refs_7_ = bf16[4,144,640]{2,1,0:T(8,128)(2,1)} collective-permute-done((bf16[4,144,640]{2,1,0:T(8,128)(2,1)}, bf16[4,144,640]{2,1,0:T(8,128)(2,1)}, u32[]{:S(2)}, u32[]{:S(2)}) %collective-permute-start.8) | collective-permute-done | bytes 737312 | tf_op jit(solution)/shard_map/ppermute | solution.py:276
  124.2 13.6 %state.1 = f32[80,128]{1,0:T(8,128)} custom-call(s32[32]{0:T(128)} %pad_add_fusion.place_ref, s32[4]{0:T(128)} %get-tuple-element.15.live_ref, bf16[384,2304]{1,0:T(8,128)(2,1)} %bitcast.19, bf16[384,2304]{1,0:T(8,128)(2,1)} %collective-permute-done.refs_1_, bf16[384,2304]{1,0:T(8,128)(2,1)} %copy-done.1, bf16[384,2304]{1,0:T(8,128)(2,1)} %collective-permute-done.4.refs_3_, ...), custom_call_target="tpu_custom_call" | custom-call | tf_op jit(solution)/shard_map/state/pallas_call | solution.py:208
  139.3 6.7 %all-to-all-start.2 = ((f32[8,80,128]{2,1,0:T(8,128)}), f32[8,80,128]{2,1,0:T(8,128)S(1)}, u32[]{:S(2)}, u32[]{:S(2)}) async-start(f32[8,80,128]{2,1,0:T(8,128)} %broadcast_in_dim.11), calls=%async_computation.2 | async-start | bytes 655360 | tf_op jit(solution)/shard_map/all_to_all | solution.py:272
  146.0 2.2 %collective-permute-start.5 = (bf16[4,144,384]{2,1,0:T(8,128)(2,1)}, bf16[4,144,384]{2,1,0:T(8,128)(2,1)S(1)}, u32[]{:S(2)}, u32[]{:S(2)}) collective-permute-start(bf16[4,144,384]{2,1,0:T(8,128)(2,1)} %all-to-all-done.1.refs_4_), channel_id=1, source_target_pairs={{0,1},{1,0},{2,3},{3,2},{4,5},{5,4},{6,7},{7,6},{8,9},{9,8},{10,11... | collective-permute-start | bytes 1327112 | tf_op jit(solution)/shard_map/ppermute | solution.py:276
  148.2 2.5 %collective-permute-start.6 = (bf16[4,144,384]{2,1,0:T(8,128)(2,1)}, bf16[4,144,384]{2,1,0:T(8,128)(2,1)S(1)}, u32[]{:S(2)}, u32[]{:S(2)}) collective-permute-start(bf16[4,144,384]{2,1,0:T(8,128)(2,1)} %all-to-all-done.1.refs_4_), channel_id=1, source_target_pairs={{0,3},{1,2},{2,1},{3,0},{4,7},{5,6},{6,5},{7,4},{8,11},{9,10},{10,... | collective-permute-start | bytes 1327112 | tf_op jit(solution)/shard_map/ppermute | solution.py:276
  150.7 7.5 %collective-permute-done.5.refs_5_ = bf16[4,144,384]{2,1,0:T(8,128)(2,1)S(1)} collective-permute-done((bf16[4,144,384]{2,1,0:T(8,128)(2,1)}, bf16[4,144,384]{2,1,0:T(8,128)(2,1)S(1)}, u32[]{:S(2)}, u32[]{:S(2)}) %collective-permute-start.5) | collective-permute-done | bytes 442400 | tf_op jit(solution)/shard_map/ppermute | solution.py:276
  158.2 2.8 %collective-permute-start.7 = (bf16[4,144,384]{2,1,0:T(8,128)(2,1)S(1)}, bf16[4,144,384]{2,1,0:T(8,128)(2,1)S(1)}, u32[]{:S(2)}, u32[]{:S(2)}) collective-permute-start(bf16[4,144,384]{2,1,0:T(8,128)(2,1)S(1)} %collective-permute-done.5.refs_5_), channel_id=1, source_target_pairs={{0,3},{1,2},{2,1},{3,0},{4,7},{5,6},{6,5},{7,4},{8,11},{9,10},{10,... | collective-permute-start | bytes 1327112 | tf_op jit(solution)/shard_map/ppermute | solution.py:276
  161.3 9.2 %collective-permute-done.7.refs_7_ = bf16[4,144,384]{2,1,0:T(8,128)(2,1)S(1)} collective-permute-done((bf16[4,144,384]{2,1,0:T(8,128)(2,1)S(1)}, bf16[4,144,384]{2,1,0:T(8,128)(2,1)S(1)}, u32[]{:S(2)}, u32[]{:S(2)}) %collective-permute-start.7) | collective-permute-done | bytes 442400 | tf_op jit(solution)/shard_map/ppermute | solution.py:276
  171.3 9.7 %queries.1.query_ref = f32[1536,384]{1,0:T(8,128)} custom-call(s32[32]{0:T(128)} %pad_add_fusion.place_ref, bf16[384,2304]{1,0:T(8,128)(2,1)} %bitcast.20, bf16[384,2304]{1,0:T(8,128)(2,1)} %collective-permute-done.refs_1_, bf16[384,2304]{1,0:T(8,128)(2,1)} %copy-done.1, bf16[384,2304]{1,0:T(8,128)(2,1)} %collective-permute-done.4.refs_3_, ...), custom_call_target="tpu_custom_call" | custom-call | flops 2717908992 | bytes 11206656 | tf_op jit(solution)/shard_map/queries/pallas_call | solution.py:229
  181.8 5.8 %attend.1 = bf16[4,384,384]{2,1,0:T(8,128)(2,1)} custom-call(s32[4]{0:T(128)} %get-tuple-element.14.slot_ref, s32[4]{0:T(128)} %get-tuple-element.15.live_ref, f32[1536,384]{1,0:T(8,128)} %queries.1.query_ref, f32[8,80,128]{2,1,0:T(8,128)} %copy-done.3), custom_call_target="tpu_custom_call" | custom-call | tf_op jit(solution)/shard_map/attend/pallas_call | solution.py:252
  187.6 21.6 %all_to_all.20 = bf16[4,384,384]{2,1,0:T(8,128)(2,1)S(1)} all-to-all(bf16[4,384,384]{2,1,0:T(8,128)(2,1)} %attend.1), channel_id=1, replica_groups={{0,16,32,48},{64,80,96,112},{128,144,160,176},{192,208,224,240},{256,27..., dimensions={0} | all-to-all | bytes 2359296 | tf_op jit(solution)/shard_map/all_to_all | solution.py:370
  (61 shorter events, 19.6 us)
Async XLA Ops:
  41.3 7.3 %copy-start.2 = (bf16[1,3,128,2240]{2,3,1,0:T(8,128)(2,1)S(1)}, bf16[1,3,128,2240]{2,3,1,0:T(8,128)(2,1)}, u32[]{:S(2)}) copy-start(bf16[1,3,128,2240]{2,3,1,0:T(8,128)(2,1)} %param.10) | copy-start | bytes 5160964
  44.9 4.7 %copy-start.9 = (bf16[2240]{0:T(1024)(128)(2,1)S(1)}, bf16[2240]{0:T(1024)(128)(2,1)}, u32[]{:S(2)}) copy-start(bf16[2240]{0:T(1024)(128)(2,1)} %param.11) | copy-start | bytes 13444
  44.9 4.7 %copy-start.8 = (bf16[1,2240]{1,0:T(2,128)(2,1)S(1)}, bf16[1,2240]{1,0:T(2,128)(2,1)}, u32[]{:S(2)}) copy-start(bf16[1,2240]{1,0:T(2,128)(2,1)} %param.12) | copy-start | bytes 13444
  44.9 4.8 %copy-start.10 = (bf16[2240]{0:T(1024)(128)(2,1)S(1)}, bf16[2240]{0:T(1024)(128)(2,1)}, u32[]{:S(2)}) copy-start(bf16[2240]{0:T(1024)(128)(2,1)} %param.13) | copy-start | bytes 13444
  52.4 53.5 %copy-start = (bf16[3,128,2304]{2,1,0:T(8,128)(2,1)}, bf16[3,128,2304]{2,1,0:T(8,128)(2,1)S(1)}, u32[]{:S(2)}) copy-start(bf16[3,128,2304]{2,1,0:T(8,128)(2,1)S(1)} %copy.16) | copy-start | bytes 5308420
  52.4 10.4 %copy-start.11 = (s32[16]{0:T(128)S(1)}, s32[16]{0:T(128)}, u32[]{:S(2)}) copy-start(s32[16]{0:T(128)} %constant.65.clone) | copy-start | bytes 196
  52.4 10.4 %copy-start.12 = (s32[16]{0:T(128)S(1)}, s32[16]{0:T(128)}, u32[]{:S(2)}) copy-start(s32[16]{0:T(128)} %constant.66.clone) | copy-start | bytes 196
  52.5 10.4 %copy-start.13 = (s32[16]{0:T(128)S(1)}, s32[16]{0:T(128)}, u32[]{:S(2)}) copy-start(s32[16]{0:T(128)} %constant.67.clone) | copy-start | bytes 196
  52.5 42.8 %collective-permute-start.1 = (bf16[384,2304]{1,0:T(8,128)(2,1)S(1)}, bf16[384,2304]{1,0:T(8,128)(2,1)S(1)}, u32[]{:S(2)}, u32[]{:S(2)}) collective-permute-start(bf16[384,2304]{1,0:T(8,128)(2,1)S(1)} %bitcast.17), channel_id=1, source_target_pairs={{0,32},{16,48},{32,0},{48,16},{64,96},{80,112},{96,64},{112,80},{1... | collective-permute-start | bytes 5308424 | tf_op jit(solution)/shard_map/ppermute | solution.py:276
  56.4 15.8 %all-to-all-start = ((bf16[4,144,640]{2,1,0:T(8,128)(2,1)}), bf16[4,144,640]{2,1,0:T(8,128)(2,1)}, u32[]{:S(2)}, u32[]{:S(2)}) async-start(bf16[4,144,640]{2,1,0:T(8,128)(2,1)} %broadcast_in_dim.9), calls=%async_computation | async-start | bytes 1474560 | tf_op jit(solution)/shard_map/all_to_all | solution.py:272
  72.2 19.1 %collective-permute-start.2 = (bf16[4,144,640]{2,1,0:T(8,128)(2,1)}, bf16[4,144,640]{2,1,0:T(8,128)(2,1)}, u32[]{:S(2)}, u32[]{:S(2)}) collective-permute-start(bf16[4,144,640]{2,1,0:T(8,128)(2,1)} %all-to-all-done.refs_4_), channel_id=1, source_target_pairs={{0,4},{1,5},{2,6},{3,7},{4,0},{5,1},{6,2},{7,3},{8,12},{9,13},{10,... | collective-permute-start | bytes 2211848 | tf_op jit(solution)/shard_map/ppermute | solution.py:276
  75.4 19.9 %collective-permute-start.3 = (bf16[4,144,640]{2,1,0:T(8,128)(2,1)}, bf16[4,144,640]{2,1,0:T(8,128)(2,1)S(1)}, u32[]{:S(2)}, u32[]{:S(2)}) collective-permute-start(bf16[4,144,640]{2,1,0:T(8,128)(2,1)} %all-to-all-done.refs_4_), channel_id=1, source_target_pairs={{0,12},{1,13},{2,14},{3,15},{4,8},{5,9},{6,10},{7,11},{8,4},{9,5},... | collective-permute-start | bytes 2211848 | tf_op jit(solution)/shard_map/ppermute | solution.py:276
  79.2 31.0 %collective-permute-start = (bf16[384,2304]{1,0:T(8,128)(2,1)S(1)}, bf16[384,2304]{1,0:T(8,128)(2,1)}, u32[]{:S(2)}, u32[]{:S(2)}) collective-permute-start(bf16[384,2304]{1,0:T(8,128)(2,1)S(1)} %bitcast.18), channel_id=1, source_target_pairs={{0,16},{16,0},{32,48},{48,32},{64,80},{80,64},{96,112},{112,96},{1... | collective-permute-start | bytes 5308424 | tf_op jit(solution)/shard_map/ppermute | solution.py:276
  95.3 0.9 copy-start.4
  96.1 28.0 %copy-start.1 = (bf16[384,2304]{1,0:T(8,128)(2,1)}, bf16[384,2304]{1,0:T(8,128)(2,1)S(1)}, u32[]{:S(2)}) copy-start(bf16[384,2304]{1,0:T(8,128)(2,1)S(1)} %collective-permute-done.1.refs_2_) | copy-start | bytes 5308420
  96.1 28.0 %collective-permute-start.4 = (bf16[384,2304]{1,0:T(8,128)(2,1)S(1)}, bf16[384,2304]{1,0:T(8,128)(2,1)}, u32[]{:S(2)}, u32[]{:S(2)}) collective-permute-start(bf16[384,2304]{1,0:T(8,128)(2,1)S(1)} %collective-permute-done.1.refs_2_), channel_id=1, source_target_pairs={{0,16},{16,0},{32,48},{48,32},{64,80},{80,64},{96,112},{112,96},{1... | collective-permute-start | bytes 5308424 | tf_op jit(solution)/shard_map/ppermute | solution.py:276
  100.4 23.8 %collective-permute-start.8 = (bf16[4,144,640]{2,1,0:T(8,128)(2,1)}, bf16[4,144,640]{2,1,0:T(8,128)(2,1)}, u32[]{:S(2)}, u32[]{:S(2)}) collective-permute-start(bf16[4,144,640]{2,1,0:T(8,128)(2,1)} %collective-permute-done.2.refs_5_), channel_id=1, source_target_pairs={{0,12},{1,13},{2,14},{3,15},{4,8},{5,9},{6,10},{7,11},{8,4},{9,5},... | collective-permute-start | bytes 2211848 | tf_op jit(solution)/shard_map/ppermute | solution.py:276
  105.9 31.8 %all-to-all-start.1 = ((bf16[4,144,384]{2,1,0:T(8,128)(2,1)}), bf16[4,144,384]{2,1,0:T(8,128)(2,1)}, u32[]{:S(2)}, u32[]{:S(2)}) async-start(bf16[4,144,384]{2,1,0:T(8,128)(2,1)} %broadcast_in_dim.10), calls=%async_computation.1 | async-start | bytes 884736 | tf_op jit(solution)/shard_map/all_to_all | solution.py:272
  139.3 41.7 %all-to-all-start.2 = ((f32[8,80,128]{2,1,0:T(8,128)}), f32[8,80,128]{2,1,0:T(8,128)S(1)}, u32[]{:S(2)}, u32[]{:S(2)}) async-start(f32[8,80,128]{2,1,0:T(8,128)} %broadcast_in_dim.11), calls=%async_computation.2 | async-start | bytes 655360 | tf_op jit(solution)/shard_map/all_to_all | solution.py:272
  146.0 12.2 %collective-permute-start.5 = (bf16[4,144,384]{2,1,0:T(8,128)(2,1)}, bf16[4,144,384]{2,1,0:T(8,128)(2,1)S(1)}, u32[]{:S(2)}, u32[]{:S(2)}) collective-permute-start(bf16[4,144,384]{2,1,0:T(8,128)(2,1)} %all-to-all-done.1.refs_4_), channel_id=1, source_target_pairs={{0,1},{1,0},{2,3},{3,2},{4,5},{5,4},{6,7},{7,6},{8,9},{9,8},{10,11... | collective-permute-start | bytes 1327112 | tf_op jit(solution)/shard_map/ppermute | solution.py:276
  148.2 13.1 %collective-permute-start.6 = (bf16[4,144,384]{2,1,0:T(8,128)(2,1)}, bf16[4,144,384]{2,1,0:T(8,128)(2,1)S(1)}, u32[]{:S(2)}, u32[]{:S(2)}) collective-permute-start(bf16[4,144,384]{2,1,0:T(8,128)(2,1)} %all-to-all-done.1.refs_4_), channel_id=1, source_target_pairs={{0,3},{1,2},{2,1},{3,0},{4,7},{5,6},{6,5},{7,4},{8,11},{9,10},{10,... | collective-permute-start | bytes 1327112 | tf_op jit(solution)/shard_map/ppermute | solution.py:276
  158.2 12.3 %copy-start.5 = (bf16[4,144,384]{2,1,0:T(8,128)(2,1)}, bf16[4,144,384]{2,1,0:T(8,128)(2,1)S(1)}, u32[]{:S(2)}) copy-start(bf16[4,144,384]{2,1,0:T(8,128)(2,1)S(1)} %collective-permute-done.5.refs_5_) | copy-start | bytes 1327108
  158.2 12.3 %collective-permute-start.7 = (bf16[4,144,384]{2,1,0:T(8,128)(2,1)S(1)}, bf16[4,144,384]{2,1,0:T(8,128)(2,1)S(1)}, u32[]{:S(2)}, u32[]{:S(2)}) collective-permute-start(bf16[4,144,384]{2,1,0:T(8,128)(2,1)S(1)} %collective-permute-done.5.refs_5_), channel_id=1, source_target_pairs={{0,3},{1,2},{2,1},{3,0},{4,7},{5,6},{6,5},{7,4},{8,11},{9,10},{10,... | collective-permute-start | bytes 1327112 | tf_op jit(solution)/shard_map/ppermute | solution.py:276
  161.3 9.2 %copy-start.6 = (bf16[4,144,384]{2,1,0:T(8,128)(2,1)}, bf16[4,144,384]{2,1,0:T(8,128)(2,1)S(1)}, u32[]{:S(2)}) copy-start(bf16[4,144,384]{2,1,0:T(8,128)(2,1)S(1)} %collective-permute-done.6.refs_6_) | copy-start | bytes 1327108
  (2 other events, 1.5 us)

commit v5 on v4

--- a/solution.py
+++ b/solution.py
@@ -17,8 +17,8 @@
 
 VMEM = pl.BlockSpec(memory_space=pltpu.VMEM)
 SMEM = pl.BlockSpec(memory_space=pltpu.SMEM)
-HBM = pl.BlockSpec(memory_space=pltpu.HBM)
-PARAMS = pltpu.CompilerParams(vmem_limit_bytes=58 * 1024 * 1024)
+HBM = pl.BlockSpec(memory_space=pl.ANY)
+PARAMS = pltpu.CompilerParams(vmem_limit_bytes=32 * 1024 * 1024)
 
 FAR_MASKS = np.array([0] * 4 + [1] * 4 + [3] * 4 + [2] * 4)
 NEAR_SLOTS = np.array([0, 1, 2, 3] * 4)
@@ -197,7 +197,42 @@
         )
         total = main[:, 2 * LANES :] + small + main[:, : 2 * LANES]
         result = total[:, :LANES] / (total[:, LANES:] + attn_eps) * live
-        out_ref[0, :, tile * LANES : (tile + 1) * LANES] = result.astype(jnp.bfloat16)
+        if tile < tiles - 1:
+            out_ref[0, tile * tokens : (tile + 1) * tokens, :] = result.astype(jnp.bfloat16)
+        else:
+            quarter = tokens // GROUP
+            folded = result[:quarter]
+            for part in range(1, GROUP):
+                folded = folded + pltpu.roll(
+                    result[part * quarter : (part + 1) * quarter], part * HDIM, 1
+                )
+            out_ref[0, tile * tokens :, :] = folded.astype(jnp.bfloat16)
+
+
+def assemble_kernel(packed_ref, out_ref):
+    tokens = out_ref.shape[0]
+    full = (packed_ref.shape[1] - tokens // GROUP) // tokens
+    lane = lax.broadcasted_iota(jnp.int32, (tokens, LANES), 1)
+    carried = jnp.zeros((tokens, LANES), jnp.float32)
+    for rank in range(TEAM):
+        shift = rank * HDIM
+        for tile in range(full):
+            part = packed_ref[rank, tile * tokens : (tile + 1) * tokens, :].astype(jnp.float32)
+            part = part if rank == 0 else pltpu.roll(part, shift, 1)
+            at = (rank * full + tile) * LANES
+            out_ref[:, at : at + LANES] = jnp.where(lane < shift, carried, part).astype(
+                jnp.bfloat16
+            )
+            carried = part
+        folded = packed_ref[rank, full * tokens :, :].astype(jnp.float32)
+        pieces = []
+        for row in range(GROUP):
+            turn = (rank - row) % GROUP * HDIM
+            pieces.append(folded if turn == 0 else pltpu.roll(folded, turn, 1))
+        edge = jnp.concatenate(pieces, axis=0)
+        carried = jnp.where(lane < shift, carried, edge)
+    at = TEAM * full * LANES
+    out_ref[:, at:] = carried.astype(jnp.bfloat16)
 
 
 def compute_state(place, live, hidden, first):
@@ -249,6 +284,7 @@
 
 def compute_output(slots, live, queries, state):
     tokens, width = queries.shape[0] // TEAM, queries.shape[1]
+    packed = (width // LANES - 1) * tokens + tokens // GROUP
     return pl.pallas_call(
         attend_kernel,
         grid_spec=pltpu.PrefetchScalarGridSpec(
@@ -258,11 +294,11 @@
                 pl.BlockSpec((tokens, width), lambda i, slots, live: (i, 0)),
                 pl.BlockSpec(state.shape, lambda i, slots, live: (0, 0, 0)),
             ],
-            out_specs=pl.BlockSpec((1, tokens, width), lambda i, slots, live: (slots[i], 0, 0)),
+            out_specs=pl.BlockSpec((1, packed, LANES), lambda i, slots, live: (slots[i], 0, 0)),
             scratch_shapes=[pltpu.VMEM((width // LANES, LANES, 4 * LANES), jnp.bfloat16)],
         ),
-        out_shape=jax.ShapeDtypeStruct((TEAM, tokens, width), jnp.bfloat16),
-        compiler_params=PARAMS,
+        out_shape=jax.ShapeDtypeStruct((TEAM, packed, LANES), jnp.bfloat16),
+        compiler_params=pltpu.CompilerParams(vmem_limit_bytes=58 * 1024 * 1024),
         name="attend",
     )(slots, live, queries, state)
 
@@ -368,7 +404,14 @@
 
     result = compute_output(slots, live, queries, state)
     result = lax.all_to_all(result, "seq", 0, 0, axis_index_groups=team)
-    result = jnp.transpose(result[:, :, :share], (1, 0, 2))
+    result = pl.pallas_call(
+        assemble_kernel,
+        in_specs=[VMEM],
+        out_specs=VMEM,
+        out_shape=jax.ShapeDtypeStruct((token_count, inner), jnp.bfloat16),
+        compiler_params=pltpu.CompilerParams(vmem_limit_bytes=16 * 1024 * 1024),
+        name="assemble",
+    )(result)
     return result.reshape(1, grid_rows, grid_cols, inner)
 
 

time: 213 us -> 207 us (0.972)
  blocking collectives: 62.6 us -> 59.5 us
  Pallas kernels: 29.1 us -> 26.7 us
    all_to_all x1, blocking collectives: 21.6 us -> 18.5 us  [body(): result = lax.all_to_all(result, 'seq', 0, 0, axis_index_groups=team)]
  transfers between devices with their start and end apart: 12 -> 12, of which waited for: 7 -> 7; matrix products, arithmetic and copies ran while one was open for 3% -> 3% of each run, Pallas kernels for 11% -> 9%
where the time goes in v5:
time: 207 us; the launch traced here: 206 us
  blocking collectives  59.5 us (29%)
  waiting for transfers between devices  52.4 us (25%)
  starting transfers between devices  43.4 us (21%)
  Pallas kernels  26.7 us (13%)
  local copies, waits for them, and re-layouts  16.7 us (8%)
  other arithmetic  5.23 us (3%)
    ppermute x9, waiting for transfers between devices, exchange(): return lax.ppermute(block, axis, [(i, i ^ mask) for i in range(count)])  43.7 us
    all_gather x1, blocking collectives, body(): gathered = lax.all_gather(w_qkv, 'seq', axis=0)  41 us
    ppermute x9, starting transfers between devices, exchange(): return lax.ppermute(block, axis, [(i, i ^ mask) for i in range(count)])  28.2 us
    all_to_all x1, blocking collectives, body(): result = lax.all_to_all(result, 'seq', 0, 0, axis_index_groups=team)  18.5 us
    all_to_all x3, starting transfers between devices, spread(): return lax.all_to_all(copies, axis, 0, 0, axis_index_groups=groups)  15.2 us
    pallas_call x1, Pallas kernels, compute_state(): pl.pallas_call(state_kernel, in_specs=[SMEM, SMEM] + [HBM] * (TEAM + len(...  11.6 us
    all_to_all x3, waiting for transfers between devices, spread(): return lax.all_to_all(copies, axis, 0, 0, axis_index_groups=groups)  8.69 us
    pallas_call x1, Pallas kernels, compute_queries(): pl.pallas_call(query_kernel, in_specs=[SMEM] + [HBM] * (TEAM + len(second...  7.88 us
  transfers between devices with their start and end apart: 12, of which 7 were waited for; matrix products, arithmetic and copies ran while one was open for 3% of the time, Pallas kernels for 9%

profile of v5, /device:TPU:1, one launch (start us, length us, event | category | flops | bytes accessed | tf_op | source)
XLA Modules:
  0.0 205.5 jit_solution(168059524990201164)
XLA Ops:
  0.0 41.0 %all-gather.1 = bf16[32,140,108]{2,1,0:T(8,128)(2,1)S(1)} all-gather(bf16[1,140,108]{2,1,0:T(8,128)(2,1)} %bitcast.22), channel_id=2, replica_groups=mesh['seq'=32,'img'=16] {'seq'}, dimensions={0}, use_global_device_ids=true | all-gather | bytes 997920 | tf_op jit(solution)/shard_map/all_gather | solution.py:344
  41.3 3.6 %reshape.32 = bf16[140,3456]{1,0:T(8,128)(2,1)} reshape(bf16[140,32,108]{2,1,0:T(8,128)(2,1)S(1)} %copy.14) | data formatting | bytes 1935360 | tf_op jit(solution)/shard_map/reshape | solution.py:345
  44.9 2.8 %select_select_fusion = (bf16[144,288]{1,0:T(8,128)(2,1)S(1)}, bf16[144,288]{1,0:T(8,128)(2,1)S(1)}, bf16[144,288]{1,0:T(8,128)(2,1)}) fusion(bf16[140,3456]{1,0:T(8,128)(2,1)} %reshape.32, pred[]{:T(512)S(6)} %eq.20, pred[]{:T(512)S(6)} %eq.10, pred[]{:T(512)S(6)} %eq.9), kind=kLoop, calls=%fused_computation.7 | loop fusion | flops 373248 | bytes 1216515 | tf_op jit(solution)/shard_map/jit(_where)/select_n | solution.py:352
  56.4 4.2 %all-to-all-start = ((bf16[4,144,640]{2,1,0:T(8,128)(2,1)}), bf16[4,144,640]{2,1,0:T(8,128)(2,1)}, u32[]{:S(2)}, u32[]{:S(2)}) async-start(bf16[4,144,640]{2,1,0:T(8,128)(2,1)} %broadcast_in_dim.9), calls=%async_computation | async-start | bytes 1474560 | tf_op jit(solution)/shard_map/all_to_all | solution.py:308
  63.5 8.7 %all-to-all-done.refs_4_ = bf16[4,144,640]{2,1,0:T(8,128)(2,1)} async-done(((bf16[4,144,640]{2,1,0:T(8,128)(2,1)}), bf16[4,144,640]{2,1,0:T(8,128)(2,1)}, u32[]{:S(2)}, u32[]{:S(2)}) %all-to-all-start) | async-done | bytes 737312 | tf_op jit(solution)/shard_map/all_to_all | solution.py:308
  72.2 3.2 %collective-permute-start.2 = (bf16[4,144,640]{2,1,0:T(8,128)(2,1)}, bf16[4,144,640]{2,1,0:T(8,128)(2,1)}, u32[]{:S(2)}, u32[]{:S(2)}) collective-permute-start(bf16[4,144,640]{2,1,0:T(8,128)(2,1)} %all-to-all-done.refs_4_), channel_id=1, source_target_pairs={{0,4},{1,5},{2,6},{3,7},{4,0},{5,1},{6,2},{7,3},{8,12},{9,13},{10,... | collective-permute-start | bytes 2211848 | tf_op jit(solution)/shard_map/ppermute | solution.py:312
  75.4 3.8 %collective-permute-start.3 = (bf16[4,144,640]{2,1,0:T(8,128)(2,1)}, bf16[4,144,640]{2,1,0:T(8,128)(2,1)S(1)}, u32[]{:S(2)}, u32[]{:S(2)}) collective-permute-start(bf16[4,144,640]{2,1,0:T(8,128)(2,1)} %all-to-all-done.refs_4_), channel_id=1, source_target_pairs={{0,12},{1,13},{2,14},{3,15},{4,8},{5,9},{6,10},{7,11},{8,4},{9,5},... | collective-permute-start | bytes 2211848 | tf_op jit(solution)/shard_map/ppermute | solution.py:312
  79.2 3.6 %collective-permute-start = (bf16[384,2304]{1,0:T(8,128)(2,1)S(1)}, bf16[384,2304]{1,0:T(8,128)(2,1)}, u32[]{:S(2)}, u32[]{:S(2)}) collective-permute-start(bf16[384,2304]{1,0:T(8,128)(2,1)S(1)} %bitcast.17), channel_id=1, source_target_pairs={{0,16},{16,0},{32,48},{48,32},{64,80},{80,64},{96,112},{112,96},{1... | collective-permute-start | bytes 5308424 | tf_op jit(solution)/shard_map/ppermute | solution.py:312
  82.8 8.4 %collective-permute-done.2.refs_5_ = bf16[4,144,640]{2,1,0:T(8,128)(2,1)} collective-permute-done((bf16[4,144,640]{2,1,0:T(8,128)(2,1)}, bf16[4,144,640]{2,1,0:T(8,128)(2,1)}, u32[]{:S(2)}, u32[]{:S(2)}) %collective-permute-start.2) | collective-permute-done | bytes 737312 | tf_op jit(solution)/shard_map/ppermute | solution.py:312
  91.3 4.0 %collective-permute-done.3.refs_6_ = bf16[4,144,640]{2,1,0:T(8,128)(2,1)S(1)} collective-permute-done((bf16[4,144,640]{2,1,0:T(8,128)(2,1)}, bf16[4,144,640]{2,1,0:T(8,128)(2,1)S(1)}, u32[]{:S(2)}, u32[]{:S(2)}) %collective-permute-start.3) | collective-permute-done | bytes 737312 | tf_op jit(solution)/shard_map/ppermute | solution.py:312
  96.2 4.2 %collective-permute-start.4 = (bf16[384,2304]{1,0:T(8,128)(2,1)S(1)}, bf16[384,2304]{1,0:T(8,128)(2,1)}, u32[]{:S(2)}, u32[]{:S(2)}) collective-permute-start(bf16[384,2304]{1,0:T(8,128)(2,1)S(1)} %collective-permute-done.1.refs_2_), channel_id=1, source_target_pairs={{0,16},{16,0},{32,48},{48,32},{64,80},{80,64},{96,112},{112,96},{1... | collective-permute-start | bytes 5308424 | tf_op jit(solution)/shard_map/ppermute | solution.py:312
  100.4 3.8 %collective-permute-start.8 = (bf16[4,144,640]{2,1,0:T(8,128)(2,1)}, bf16[4,144,640]{2,1,0:T(8,128)(2,1)}, u32[]{:S(2)}, u32[]{:S(2)}) collective-permute-start(bf16[4,144,640]{2,1,0:T(8,128)(2,1)} %collective-permute-done.2.refs_5_), channel_id=1, source_target_pairs={{0,12},{1,13},{2,14},{3,15},{4,8},{5,9},{6,10},{7,11},{8,4},{9,5},... | collective-permute-start | bytes 2211848 | tf_op jit(solution)/shard_map/ppermute | solution.py:312
  105.9 4.3 %all-to-all-start.1 = ((bf16[4,144,384]{2,1,0:T(8,128)(2,1)}), bf16[4,144,384]{2,1,0:T(8,128)(2,1)}, u32[]{:S(2)}, u32[]{:S(2)}) async-start(bf16[4,144,384]{2,1,0:T(8,128)(2,1)} %broadcast_in_dim.10), calls=%async_computation.1 | async-start | bytes 884736 | tf_op jit(solution)/shard_map/all_to_all | solution.py:308
  110.2 14.0 %collective-permute-done.8.refs_7_ = bf16[4,144,640]{2,1,0:T(8,128)(2,1)} collective-permute-done((bf16[4,144,640]{2,1,0:T(8,128)(2,1)}, bf16[4,144,640]{2,1,0:T(8,128)(2,1)}, u32[]{:S(2)}, u32[]{:S(2)}) %collective-permute-start.8) | collective-permute-done | bytes 737312 | tf_op jit(solution)/shard_map/ppermute | solution.py:312
  125.3 11.6 %state.1 = f32[80,128]{1,0:T(8,128)S(1)} custom-call(s32[32]{0:T(128)S(1)} %pad_add_fusion.place_ref, s32[4]{0:T(128)S(1)} %get-tuple-element.15.live_ref, bf16[384,2304]{1,0:T(8,128)(2,1)S(1)} %bitcast.18, bf16[384,2304]{1,0:T(8,128)(2,1)} %collective-permute-done.refs_1_, bf16[384,2304]{1,0:T(8,128)(2,1)S(1)} %collective-permute-done.1.refs_2_, ...), custom_call_target="tpu_custom_call" | custom-call | tf_op jit(solution)/shard_map/state/pallas_call | solution.py:243
  139.0 6.7 %all-to-all-start.2 = ((f32[8,80,128]{2,1,0:T(8,128)}), f32[8,80,128]{2,1,0:T(8,128)}, u32[]{:S(2)}, u32[]{:S(2)}) async-start(f32[8,80,128]{2,1,0:T(8,128)} %broadcast_in_dim.11), calls=%async_computation.2 | async-start | bytes 655360 | tf_op jit(solution)/shard_map/all_to_all | solution.py:308
  145.8 2.2 %collective-permute-start.5 = (bf16[4,144,384]{2,1,0:T(8,128)(2,1)}, bf16[4,144,384]{2,1,0:T(8,128)(2,1)S(1)}, u32[]{:S(2)}, u32[]{:S(2)}) collective-permute-start(bf16[4,144,384]{2,1,0:T(8,128)(2,1)} %all-to-all-done.1.refs_4_), channel_id=1, source_target_pairs={{0,1},{1,0},{2,3},{3,2},{4,5},{5,4},{6,7},{7,6},{8,9},{9,8},{10,11... | collective-permute-start | bytes 1327112 | tf_op jit(solution)/shard_map/ppermute | solution.py:312
  148.0 2.5 %collective-permute-start.6 = (bf16[4,144,384]{2,1,0:T(8,128)(2,1)}, bf16[4,144,384]{2,1,0:T(8,128)(2,1)S(1)}, u32[]{:S(2)}, u32[]{:S(2)}) collective-permute-start(bf16[4,144,384]{2,1,0:T(8,128)(2,1)} %all-to-all-done.1.refs_4_), channel_id=1, source_target_pairs={{0,3},{1,2},{2,1},{3,0},{4,7},{5,6},{6,5},{7,4},{8,11},{9,10},{10,... | collective-permute-start | bytes 1327112 | tf_op jit(solution)/shard_map/ppermute | solution.py:312
  150.5 7.6 %collective-permute-done.5.refs_5_ = bf16[4,144,384]{2,1,0:T(8,128)(2,1)S(1)} collective-permute-done((bf16[4,144,384]{2,1,0:T(8,128)(2,1)}, bf16[4,144,384]{2,1,0:T(8,128)(2,1)S(1)}, u32[]{:S(2)}, u32[]{:S(2)}) %collective-permute-start.5) | collective-permute-done | bytes 442400 | tf_op jit(solution)/shard_map/ppermute | solution.py:312
  158.1 2.8 %collective-permute-start.7 = (bf16[4,144,384]{2,1,0:T(8,128)(2,1)S(1)}, bf16[4,144,384]{2,1,0:T(8,128)(2,1)S(1)}, u32[]{:S(2)}, u32[]{:S(2)}) collective-permute-start(bf16[4,144,384]{2,1,0:T(8,128)(2,1)S(1)} %collective-permute-done.5.refs_5_), channel_id=1, source_target_pairs={{0,3},{1,2},{2,1},{3,0},{4,7},{5,6},{6,5},{7,4},{8,11},{9,10},{10,... | collective-permute-start | bytes 1327112 | tf_op jit(solution)/shard_map/ppermute | solution.py:312
  161.2 9.3 %collective-permute-done.7.refs_7_ = bf16[4,144,384]{2,1,0:T(8,128)(2,1)S(1)} collective-permute-done((bf16[4,144,384]{2,1,0:T(8,128)(2,1)S(1)}, bf16[4,144,384]{2,1,0:T(8,128)(2,1)S(1)}, u32[]{:S(2)}, u32[]{:S(2)}) %collective-permute-start.7) | collective-permute-done | bytes 442400 | tf_op jit(solution)/shard_map/ppermute | solution.py:312
  170.5 7.9 %queries.1.query_ref = f32[1536,384]{1,0:T(8,128)S(1)} custom-call(s32[32]{0:T(128)S(1)} %pad_add_fusion.place_ref, bf16[384,2304]{1,0:T(8,128)(2,1)S(1)} %bitcast.19, bf16[384,2304]{1,0:T(8,128)(2,1)} %collective-permute-done.refs_1_, bf16[384,2304]{1,0:T(8,128)(2,1)S(1)} %collective-permute-done.1.refs_2_, ...), custom_call_target="tpu_custom_call" | custom-call | flops 2717908992 | bytes 11206656 | tf_op jit(solution)/shard_map/queries/pallas_call | solution.py:264
  179.9 6.0 %attend.1 = bf16[4,864,128]{2,1,0:T(8,128)(2,1)} custom-call(s32[4]{0:T(128)} %get-tuple-element.14.slot_ref, s32[4]{0:T(128)} %copy-done.4, f32[1536,384]{1,0:T(8,128)} %copy-done, f32[8,80,128]{2,1,0:T(8,128)} %all-to-all-done.2.state_ref), custom_call_target="tpu_custom_call" | custom-call | tf_op jit(solution)/shard_map/attend/pallas_call | solution.py:288
  185.8 18.5 %all_to_all.20.packed_ref = bf16[4,864,128]{2,1,0:T(8,128)(2,1)S(1)} all-to-all(bf16[4,864,128]{2,1,0:T(8,128)(2,1)} %attend.1), channel_id=1, replica_groups={{0,16,32,48},{64,80,96,112},{128,144,160,176},{192,208,224,240},{256,27..., dimensions={0} | all-to-all | bytes 1769472 | tf_op jit(solution)/shard_map/all_to_all | solution.py:406
  (55 shorter events, 19.2 us)
Async XLA Ops:
  41.3 7.3 %copy-start.5 = (bf16[1,3,128,2240]{2,3,1,0:T(8,128)(2,1)S(1)}, bf16[1,3,128,2240]{2,3,1,0:T(8,128)(2,1)}, u32[]{:S(2)}) copy-start(bf16[1,3,128,2240]{2,3,1,0:T(8,128)(2,1)} %param.10) | copy-start | bytes 5160964
  44.9 4.7 %copy-start.7 = (bf16[2240]{0:T(1024)(128)(2,1)S(1)}, bf16[2240]{0:T(1024)(128)(2,1)}, u32[]{:S(2)}) copy-start(bf16[2240]{0:T(1024)(128)(2,1)} %param.11) | copy-start | bytes 13444
  44.9 4.7 %copy-start.6 = (bf16[1,2240]{1,0:T(2,128)(2,1)S(1)}, bf16[1,2240]{1,0:T(2,128)(2,1)}, u32[]{:S(2)}) copy-start(bf16[1,2240]{1,0:T(2,128)(2,1)} %param.12) | copy-start | bytes 13444
  44.9 4.8 %copy-start.8 = (bf16[2240]{0:T(1024)(128)(2,1)S(1)}, bf16[2240]{0:T(1024)(128)(2,1)}, u32[]{:S(2)}) copy-start(bf16[2240]{0:T(1024)(128)(2,1)} %param.13) | copy-start | bytes 13444
  52.4 10.4 %copy-start.9 = (s32[16]{0:T(128)S(1)}, s32[16]{0:T(128)}, u32[]{:S(2)}) copy-start(s32[16]{0:T(128)} %constant.65.clone) | copy-start | bytes 196
  52.4 10.4 %copy-start.10 = (s32[16]{0:T(128)S(1)}, s32[16]{0:T(128)}, u32[]{:S(2)}) copy-start(s32[16]{0:T(128)} %constant.66.clone) | copy-start | bytes 196
  52.4 10.4 %copy-start.11 = (s32[16]{0:T(128)S(1)}, s32[16]{0:T(128)}, u32[]{:S(2)}) copy-start(s32[16]{0:T(128)} %constant.67.clone) | copy-start | bytes 196
  52.5 43.7 %collective-permute-start.1 = (bf16[384,2304]{1,0:T(8,128)(2,1)S(1)}, bf16[384,2304]{1,0:T(8,128)(2,1)S(1)}, u32[]{:S(2)}, u32[]{:S(2)}) collective-permute-start(bf16[384,2304]{1,0:T(8,128)(2,1)S(1)} %bitcast.16), channel_id=1, source_target_pairs={{0,32},{16,48},{32,0},{48,16},{64,96},{80,112},{96,64},{112,80},{1... | collective-permute-start | bytes 5308424 | tf_op jit(solution)/shard_map/ppermute | solution.py:312
  56.4 15.8 %all-to-all-start = ((bf16[4,144,640]{2,1,0:T(8,128)(2,1)}), bf16[4,144,640]{2,1,0:T(8,128)(2,1)}, u32[]{:S(2)}, u32[]{:S(2)}) async-start(bf16[4,144,640]{2,1,0:T(8,128)(2,1)} %broadcast_in_dim.9), calls=%async_computation | async-start | bytes 1474560 | tf_op jit(solution)/shard_map/all_to_all | solution.py:308
  63.5 73.4 %copy-start.4 = (s32[4]{0:T(128)}, s32[4]{0:T(128)S(1)}, u32[]{:S(2)}) copy-start(s32[4]{0:T(128)S(1)} %get-tuple-element.15.live_ref) | copy-start | bytes 52
  72.2 19.1 %collective-permute-start.2 = (bf16[4,144,640]{2,1,0:T(8,128)(2,1)}, bf16[4,144,640]{2,1,0:T(8,128)(2,1)}, u32[]{:S(2)}, u32[]{:S(2)}) collective-permute-start(bf16[4,144,640]{2,1,0:T(8,128)(2,1)} %all-to-all-done.refs_4_), channel_id=1, source_target_pairs={{0,4},{1,5},{2,6},{3,7},{4,0},{5,1},{6,2},{7,3},{8,12},{9,13},{10,... | collective-permute-start | bytes 2211848 | tf_op jit(solution)/shard_map/ppermute | solution.py:312
  75.4 19.9 %collective-permute-start.3 = (bf16[4,144,640]{2,1,0:T(8,128)(2,1)}, bf16[4,144,640]{2,1,0:T(8,128)(2,1)S(1)}, u32[]{:S(2)}, u32[]{:S(2)}) collective-permute-start(bf16[4,144,640]{2,1,0:T(8,128)(2,1)} %all-to-all-done.refs_4_), channel_id=1, source_target_pairs={{0,12},{1,13},{2,14},{3,15},{4,8},{5,9},{6,10},{7,11},{8,4},{9,5},... | collective-permute-start | bytes 2211848 | tf_op jit(solution)/shard_map/ppermute | solution.py:312
  79.2 31.0 %collective-permute-start = (bf16[384,2304]{1,0:T(8,128)(2,1)S(1)}, bf16[384,2304]{1,0:T(8,128)(2,1)}, u32[]{:S(2)}, u32[]{:S(2)}) collective-permute-start(bf16[384,2304]{1,0:T(8,128)(2,1)S(1)} %bitcast.17), channel_id=1, source_target_pairs={{0,16},{16,0},{32,48},{48,32},{64,80},{80,64},{96,112},{112,96},{1... | collective-permute-start | bytes 5308424 | tf_op jit(solution)/shard_map/ppermute | solution.py:312
  95.3 0.9 copy-start.1
  96.2 28.0 %collective-permute-start.4 = (bf16[384,2304]{1,0:T(8,128)(2,1)S(1)}, bf16[384,2304]{1,0:T(8,128)(2,1)}, u32[]{:S(2)}, u32[]{:S(2)}) collective-permute-start(bf16[384,2304]{1,0:T(8,128)(2,1)S(1)} %collective-permute-done.1.refs_2_), channel_id=1, source_target_pairs={{0,16},{16,0},{32,48},{48,32},{64,80},{80,64},{96,112},{112,96},{1... | collective-permute-start | bytes 5308424 | tf_op jit(solution)/shard_map/ppermute | solution.py:312
  100.4 23.8 %collective-permute-start.8 = (bf16[4,144,640]{2,1,0:T(8,128)(2,1)}, bf16[4,144,640]{2,1,0:T(8,128)(2,1)}, u32[]{:S(2)}, u32[]{:S(2)}) collective-permute-start(bf16[4,144,640]{2,1,0:T(8,128)(2,1)} %collective-permute-done.2.refs_5_), channel_id=1, source_target_pairs={{0,12},{1,13},{2,14},{3,15},{4,8},{5,9},{6,10},{7,11},{8,4},{9,5},... | collective-permute-start | bytes 2211848 | tf_op jit(solution)/shard_map/ppermute | solution.py:312
  105.9 31.6 %all-to-all-start.1 = ((bf16[4,144,384]{2,1,0:T(8,128)(2,1)}), bf16[4,144,384]{2,1,0:T(8,128)(2,1)}, u32[]{:S(2)}, u32[]{:S(2)}) async-start(bf16[4,144,384]{2,1,0:T(8,128)(2,1)} %broadcast_in_dim.10), calls=%async_computation.1 | async-start | bytes 884736 | tf_op jit(solution)/shard_map/all_to_all | solution.py:308
  124.2 1.1 copy-start.2
  136.9 0.6 copy-start.3
  139.0 40.8 %all-to-all-start.2 = ((f32[8,80,128]{2,1,0:T(8,128)}), f32[8,80,128]{2,1,0:T(8,128)}, u32[]{:S(2)}, u32[]{:S(2)}) async-start(f32[8,80,128]{2,1,0:T(8,128)} %broadcast_in_dim.11), calls=%async_computation.2 | async-start | bytes 655360 | tf_op jit(solution)/shard_map/all_to_all | solution.py:308
  145.8 12.3 %collective-permute-start.5 = (bf16[4,144,384]{2,1,0:T(8,128)(2,1)}, bf16[4,144,384]{2,1,0:T(8,128)(2,1)S(1)}, u32[]{:S(2)}, u32[]{:S(2)}) collective-permute-start(bf16[4,144,384]{2,1,0:T(8,128)(2,1)} %all-to-all-done.1.refs_4_), channel_id=1, source_target_pairs={{0,1},{1,0},{2,3},{3,2},{4,5},{5,4},{6,7},{7,6},{8,9},{9,8},{10,11... | collective-permute-start | bytes 1327112 | tf_op jit(solution)/shard_map/ppermute | solution.py:312
  148.0 13.2 %collective-permute-start.6 = (bf16[4,144,384]{2,1,0:T(8,128)(2,1)}, bf16[4,144,384]{2,1,0:T(8,128)(2,1)S(1)}, u32[]{:S(2)}, u32[]{:S(2)}) collective-permute-start(bf16[4,144,384]{2,1,0:T(8,128)(2,1)} %all-to-all-done.1.refs_4_), channel_id=1, source_target_pairs={{0,3},{1,2},{2,1},{3,0},{4,7},{5,6},{6,5},{7,4},{8,11},{9,10},{10,... | collective-permute-start | bytes 1327112 | tf_op jit(solution)/shard_map/ppermute | solution.py:312
  158.1 12.4 %collective-permute-start.7 = (bf16[4,144,384]{2,1,0:T(8,128)(2,1)S(1)}, bf16[4,144,384]{2,1,0:T(8,128)(2,1)S(1)}, u32[]{:S(2)}, u32[]{:S(2)}) collective-permute-start(bf16[4,144,384]{2,1,0:T(8,128)(2,1)S(1)} %collective-permute-done.5.refs_5_), channel_id=1, source_target_pairs={{0,3},{1,2},{2,1},{3,0},{4,7},{5,6},{6,5},{7,4},{8,11},{9,10},{10,... | collective-permute-start | bytes 1327112 | tf_op jit(solution)/shard_map/ppermute | solution.py:312
  178.4 1.4 copy-start

commit v6 on v5

--- a/solution.py
+++ b/solution.py
@@ -1,3 +1,5 @@
+import functools
+
 import jax
 import jax.numpy as jnp
 import numpy as np
@@ -68,6 +70,59 @@
     for copy in copies:
         copy.start()
     return copies
+
+
+def layout_kernel(plan, rank_ref, gathered_ref, first_ref, second_ref):
+    depth = gathered_ref.shape[1]
+    rows = first_ref.shape[1]
+    lane = lax.broadcasted_iota(jnp.int32, (depth, LANES), 1)
+    for rank, tiles in enumerate(plan):
+
+        @pl.when(rank_ref[0] == rank)
+        def _(tiles=tiles):
+            for out_ref, at, pieces in (
+                (first_ref if which == 0 else second_ref, tile, parts)
+                for which, tile, parts in tiles
+            ):
+                value = jnp.zeros((depth, LANES), jnp.float32)
+                for shard, source, target, size in pieces:
+                    part = gathered_ref[shard].astype(jnp.float32)
+                    part = jnp.concatenate(
+                        [part, jnp.zeros((depth, LANES - part.shape[1]), jnp.float32)], axis=1
+                    )
+                    turn = (target - source) % LANES
+                    part = part if turn == 0 else pltpu.roll(part, turn, 1)
+                    inside = jnp.logical_and(lane >= target, lane < target + size)
+                    value = jnp.where(inside, part, value)
+                value = jnp.concatenate(
+                    [value, jnp.zeros((rows - depth, LANES), jnp.float32)], axis=0
+                ).astype(jnp.bfloat16)
+                for copy in range(out_ref.shape[0]):
+                    out_ref[copy, :, at * LANES : (at + 1) * LANES] = value
+
+
+def layout_plan(shard, inner, share, main):
+    plan = []
+    for rank in range(TEAM):
+        query, key, value = (part * inner + rank * share for part in range(3))
+        rest = share - main
+        spans = [
+            (0, 0, key, main),
+            (0, main, value, main),
+            (0, 2 * main, key + main, rest),
+            (0, 2 * main + rest, value + main, rest),
+            (1, 0, query, share),
+        ]
+        tiles = {}
+        for which, target, source, size in spans:
+            while size:
+                step = min(size, LANES - target % LANES, shard - source % shard)
+                tiles.setdefault((which, target // LANES), []).append(
+                    (source // shard, source % shard, target % LANES, step)
+                )
+                target, source, size = target + step, source + step, size - step
+        plan.append([(which, tile, parts) for (which, tile), parts in sorted(tiles.items())])
+    return plan
 
 
 def state_kernel(place_ref, live_ref, *refs):
@@ -100,7 +155,8 @@
     tiles = full + 1
     tail = full * HDIM
     fold = HDIM // GROUP
-    out_ref[...] = jnp.zeros_like(out_ref)
+    lines = [None] * tiles
+    totals = [None] * tiles
     for tile in range(tiles):
         keys = keys_ref[:, tile * LANES : (tile + 1) * LANES]
         if tile < full:
@@ -128,18 +184,20 @@
         packed = outer[:HDIM]
         for head in range(1, GROUP):
             packed = packed + outer[head * HDIM : (head + 1) * HDIM]
-        if tile < full:
-            out_ref[tile * HDIM : (tile + 1) * HDIM, :] = packed
-        else:
+        if tile == full:
             folded = packed[:fold]
             for part in range(1, GROUP):
                 folded = folded + pltpu.roll(
                     packed[part * fold : (part + 1) * fold], part * HDIM, 1
                 )
-            out_ref[tail : tail + fold, :] = folded
-        out_ref[tail + fold + tile : tail + fold + tile + 1, :] = jnp.sum(
-            keys, axis=0, keepdims=True
-        )
+            packed = folded
+        lines[tile] = packed
+        totals[tile] = jnp.sum(keys, axis=0, keepdims=True)
+    used = tail + fold + tiles
+    spare = jnp.zeros((out_ref.shape[1] - used, LANES), jnp.float32)
+    block = jnp.concatenate(lines + totals + [spare], axis=0)
+    for copy in range(out_ref.shape[0]):
+        out_ref[copy] = block
 
 
 def query_kernel(place_ref, *refs):
@@ -235,7 +293,7 @@
     out_ref[:, at:] = carried.astype(jnp.bfloat16)
 
 
-def compute_state(place, live, hidden, first):
+def compute_state(place, live, hidden, first, copies):
     tokens, contraction = hidden[0].shape
     wide = (first[0].shape[2] - LANES) // 2
     tiles = wide // LANES + 1
@@ -244,7 +302,7 @@
         state_kernel,
         in_specs=[SMEM, SMEM] + [HBM] * (TEAM + len(first)),
         out_specs=VMEM,
-        out_shape=jax.ShapeDtypeStruct((slots, LANES), jnp.float32),
+        out_shape=jax.ShapeDtypeStruct((copies, slots, LANES), jnp.float32),
         scratch_shapes=[
             pltpu.VMEM((TEAM * tokens, wide + LANES), jnp.float32),
             pltpu.VMEM((TEAM * tokens, wide), jnp.float32),
@@ -303,11 +361,6 @@
     )(slots, live, queries, state)
 
 
-def spread(block, count, axis, groups):
-    copies = jnp.broadcast_to(block[None], (count,) + block.shape)
-    return lax.all_to_all(copies, axis, 0, 0, axis_index_groups=groups)
-
-
 def exchange(block, mask, axis, count):
     return lax.ppermute(block, axis, [(i, i ^ mask) for i in range(count)])
 
@@ -339,33 +392,22 @@
     inner = columns // 3
     share = inner // TEAM
     main = share // LANES * LANES
-    rest = share - main
 
     gathered = lax.all_gather(w_qkv, "seq", axis=0)
-    rows = jnp.transpose(gathered, (1, 0, 2)).reshape(depth, columns)
-    rows = jnp.pad(rows, ((0, padded - depth), (0, 0)))
-
-    def pick(part):
-        chosen = rows[:, part * inner : part * inner + share]
-        for r in range(1, TEAM):
-            start = part * inner + r * share
-            chosen = jnp.where(rank == r, rows[:, start : start + share], chosen)
-        return chosen
-
-    query_cols, key_cols, value_cols = pick(0), pick(1), pick(2)
-    first = jnp.concatenate(
-        [
-            key_cols[:, :main],
-            value_cols[:, :main],
-            key_cols[:, main:],
-            value_cols[:, main:],
-            jnp.zeros((padded, LANES - 2 * rest), jnp.bfloat16),
+    wide = 2 * main + LANES
+    first, second = pl.pallas_call(
+        functools.partial(layout_kernel, layout_plan(w_qkv.shape[1], inner, share, main)),
+        in_specs=[SMEM, VMEM],
+        out_specs=[VMEM, VMEM],
+        out_shape=[
+            jax.ShapeDtypeStruct((side, padded, wide), jnp.bfloat16),
+            jax.ShapeDtypeStruct((side, padded, main + LANES), jnp.bfloat16),
         ],
-        axis=1,
-    )
-    second = jnp.pad(query_cols, ((0, 0), (0, LANES - rest)))
+        compiler_params=pltpu.CompilerParams(vmem_limit_bytes=16 * 1024 * 1024),
+        name="layout",
+    )(rank.reshape(1).astype(jnp.int32), gathered)
     first, tokens = lax.optimization_barrier((first, tokens))
-    first_near = spread(first, side, "img", x_groups)
+    first_near = lax.all_to_all(first, "img", 0, 0, axis_index_groups=x_groups)
     y_at, x_at = img_at // side, img_at % side
     place = jnp.concatenate(
         [
@@ -379,7 +421,7 @@
     second, first_near, place, live, slots = lax.optimization_barrier(
         (second, first_near, place, live, slots)
     )
-    second_near = spread(second, side, "img", y_groups)
+    second_near = lax.all_to_all(second, "img", 0, 0, axis_index_groups=y_groups)
     first_pieces = far_stage(first_near, side, 3 * side, img_size)
     second_pieces = far_stage(second_near, 1, 3, img_size)
     features = jnp.transpose(tokens[0], (0, 2, 1)).astype(jnp.float32)
@@ -398,8 +440,8 @@
     across = exchange(late, 1, "seq", seq_size)
     hidden = (mine, exchange(mine, 1, "seq", seq_size), beside, across)
 
-    part = compute_state(place, live, hidden, first_pieces)
-    state = spread(part, teams, "seq", same_rank)
+    part = compute_state(place, live, hidden, first_pieces, teams)
+    state = lax.all_to_all(part, "seq", 0, 0, axis_index_groups=same_rank)
     queries = compute_queries(place, hidden, second_pieces)
 
     result = compute_output(slots, live, queries, state)
@@ -427,6 +469,4 @@
     )
     out_specs = P("img", "seq", None, None)
 
-    return jax.shard_map(
-        body, mesh=mesh, in_specs=in_specs, out_specs=out_specs, check_vma=False
-    )
+    return jax.shard_map(body, mesh=mesh, in_specs=in_specs, out_specs=out_specs, check_vma=False)

time: 207 us -> 202 us (0.976)
  local copies, waits for them, and re-layouts: 16.7 us -> 8.55 us
  waiting for transfers between devices: 52.4 us -> 54.6 us
    broadcast_in_dim x4 -> x0, local copies, waits for them, and re-layouts: 5.07 us -> none  [the longest x3 5.07 us: spread(): copies = jnp.broadcast_to(block[None], (count,) + block.shape)]
    reshape x1 -> x0, local copies, waits for them, and re-layouts: 3.55 us -> none  [body(): rows = jnp.transpose(gathered, (1, 0, 2)).reshape(depth, columns)]
    select_n x1 -> x0, other arithmetic: 2.84 us -> none  [pick(): chosen = jnp.where(rank == r, rows[:, start:start + share], chosen)]
    unnamed x24 -> x26, local copies, waits for them, and re-layouts: 4.05 us -> 4.17 us
  transfers between devices with their start and end apart: 12 -> 12, of which waited for: 7 -> 7; matrix products, arithmetic and copies ran while one was open for 3% -> 0% of each run, Pallas kernels for 9% -> 10%
where the time goes in v6:
time: 202 us; the launch traced here: 201 us
  blocking collectives  59.6 us (30%)
  waiting for transfers between devices  54.6 us (27%)
  starting transfers between devices  44.3 us (22%)
  Pallas kernels  26.9 us (13%)
  local copies, waits for them, and re-layouts  8.55 us (4%)
  other arithmetic  5.46 us (3%)
    ppermute x9, waiting for transfers between devices, exchange(): return lax.ppermute(block, axis, [(i, i ^ mask) for i in range(count)])  44.4 us
    all_gather x1, blocking collectives, body(): gathered = lax.all_gather(w_qkv, 'seq', axis=0)  41.1 us
    ppermute x9, starting transfers between devices, exchange(): return lax.ppermute(block, axis, [(i, i ^ mask) for i in range(count)])  29.2 us
    all_to_all x1, blocking collectives, body(): result = lax.all_to_all(result, 'seq', 0, 0, axis_index_groups=team)  18.5 us
    pallas_call x1, Pallas kernels, compute_state(): pl.pallas_call(state_kernel, in_specs=[SMEM, SMEM] + [HBM] * (TEAM + len(...  11.6 us
    all_to_all x1, waiting for transfers between devices, body(): first_near = lax.all_to_all(first, 'img', 0, 0, axis_index_groups=x_groups)  10.2 us
    pallas_call x1, Pallas kernels, compute_queries(): pl.pallas_call(query_kernel, in_specs=[SMEM] + [HBM] * (TEAM + len(second...  7.88 us
    all_to_all x1, starting transfers between devices, body(): state = lax.all_to_all(part, 'seq', 0, 0, axis_index_groups=same_rank)  6.72 us
  transfers between devices with their start and end apart: 12, of which 7 were waited for; matrix products, arithmetic and copies ran while one was open for 0% of the time, Pallas kernels for 10%

profile of v6, /device:TPU:1, one launch (start us, length us, event | category | flops | bytes accessed | tf_op | source)
XLA Modules:
  0.0 201.1 jit_solution(8540364082772121828)
XLA Ops:
  0.0 41.1 %all-gather.1.gathered_ref = bf16[32,140,108]{2,1,0:T(8,128)(2,1)S(1)} all-gather(bf16[1,140,108]{2,1,0:T(8,128)(2,1)} %bitcast.21), channel_id=2, replica_groups=mesh['seq'=32,'img'=16] {'seq'}, dimensions={0}, use_global_device_ids=true | all-gather | bytes 997920 | tf_op jit(solution)/shard_map/all_gather | solution.py:396
  41.4 2.2 %fusion = f32[3,128]{1,0:T(4,128)S(1)} fusion(bf16[1,3,128,2240]{2,3,1,0:T(8,128)(2,1)} %param.10), kind=kLoop, calls=%fused_computation.2 | loop fusion | flops 2580096 | bytes 1721856 | tf_op jit(solution)/shard_map/reduce_sum | solution.py:428
  44.4 2.5 %fusion.4 = bf16[3,2240,128]{2,1,0:T(8,128)(2,1)S(1)} fusion(bf16[1,3,128,2240]{2,3,1,0:T(8,128)(2,1)} %param.10, f32[2240]{0:T(1024)S(1)} %select_convert_fusion, f32[2240]{0:T(1024)S(1)} %convert_element_type.18, f32[3,128]{1,0:T(4,128)S(1)} %add_rsqrt_fusion), kind=kLoop, calls=%fused_computation.6 | loop fusion | flops 4300800 | bytes 3460096 | tf_op jit(solution)/shard_map/add | solution.py:431
  53.3 4.2 %all-to-all-start = ((bf16[4,144,640]{2,1,0:T(8,128)(2,1)}), bf16[4,144,640]{2,1,0:T(8,128)(2,1)}, u32[]{:S(2)}, u32[]{:S(2)}) async-start(bf16[4,144,640]{2,1,0:T(8,128)(2,1)} %copy-done.2), calls=%async_computation | async-start | bytes 1474560 | tf_op jit(solution)/shard_map/all_to_all | solution.py:410
  58.9 10.2 %all-to-all-done.refs_4_ = bf16[4,144,640]{2,1,0:T(8,128)(2,1)} async-done(((bf16[4,144,640]{2,1,0:T(8,128)(2,1)}), bf16[4,144,640]{2,1,0:T(8,128)(2,1)}, u32[]{:S(2)}, u32[]{:S(2)}) %all-to-all-start) | async-done | bytes 737312 | tf_op jit(solution)/shard_map/all_to_all | solution.py:410
  69.1 3.2 %collective-permute-start.2 = (bf16[4,144,640]{2,1,0:T(8,128)(2,1)}, bf16[4,144,640]{2,1,0:T(8,128)(2,1)}, u32[]{:S(2)}, u32[]{:S(2)}) collective-permute-start(bf16[4,144,640]{2,1,0:T(8,128)(2,1)} %all-to-all-done.refs_4_), channel_id=1, source_target_pairs={{0,4},{1,5},{2,6},{3,7},{4,0},{5,1},{6,2},{7,3},{8,12},{9,13},{10,... | collective-permute-start | bytes 2211848 | tf_op jit(solution)/shard_map/ppermute | solution.py:365
  72.3 3.8 %collective-permute-start.3 = (bf16[4,144,640]{2,1,0:T(8,128)(2,1)}, bf16[4,144,640]{2,1,0:T(8,128)(2,1)S(1)}, u32[]{:S(2)}, u32[]{:S(2)}) collective-permute-start(bf16[4,144,640]{2,1,0:T(8,128)(2,1)} %all-to-all-done.refs_4_), channel_id=1, source_target_pairs={{0,12},{1,13},{2,14},{3,15},{4,8},{5,9},{6,10},{7,11},{8,4},{9,5},... | collective-permute-start | bytes 2211848 | tf_op jit(solution)/shard_map/ppermute | solution.py:365
  76.1 3.6 %collective-permute-start = (bf16[384,2304]{1,0:T(8,128)(2,1)S(1)}, bf16[384,2304]{1,0:T(8,128)(2,1)}, u32[]{:S(2)}, u32[]{:S(2)}) collective-permute-start(bf16[384,2304]{1,0:T(8,128)(2,1)S(1)} %bitcast.17), channel_id=1, source_target_pairs={{0,16},{16,0},{32,48},{48,32},{64,80},{80,64},{96,112},{112,96},{1... | collective-permute-start | bytes 5308424 | tf_op jit(solution)/shard_map/ppermute | solution.py:365
  79.8 8.4 %collective-permute-done.2.refs_5_ = bf16[4,144,640]{2,1,0:T(8,128)(2,1)} collective-permute-done((bf16[4,144,640]{2,1,0:T(8,128)(2,1)}, bf16[4,144,640]{2,1,0:T(8,128)(2,1)}, u32[]{:S(2)}, u32[]{:S(2)}) %collective-permute-start.2) | collective-permute-done | bytes 737312 | tf_op jit(solution)/shard_map/ppermute | solution.py:365
  88.2 4.0 %collective-permute-done.3.refs_6_ = bf16[4,144,640]{2,1,0:T(8,128)(2,1)S(1)} collective-permute-done((bf16[4,144,640]{2,1,0:T(8,128)(2,1)}, bf16[4,144,640]{2,1,0:T(8,128)(2,1)S(1)}, u32[]{:S(2)}, u32[]{:S(2)}) %collective-permute-start.3) | collective-permute-done | bytes 737312 | tf_op jit(solution)/shard_map/ppermute | solution.py:365
  93.3 4.0 %collective-permute-start.4 = (bf16[384,2304]{1,0:T(8,128)(2,1)S(1)}, bf16[384,2304]{1,0:T(8,128)(2,1)}, u32[]{:S(2)}, u32[]{:S(2)}) collective-permute-start(bf16[384,2304]{1,0:T(8,128)(2,1)S(1)} %collective-permute-done.1.refs_2_), channel_id=1, source_target_pairs={{0,16},{16,0},{32,48},{48,32},{64,80},{80,64},{96,112},{112,96},{1... | collective-permute-start | bytes 5308424 | tf_op jit(solution)/shard_map/ppermute | solution.py:365
  97.3 3.8 %collective-permute-start.8 = (bf16[4,144,640]{2,1,0:T(8,128)(2,1)}, bf16[4,144,640]{2,1,0:T(8,128)(2,1)}, u32[]{:S(2)}, u32[]{:S(2)}) collective-permute-start(bf16[4,144,640]{2,1,0:T(8,128)(2,1)} %collective-permute-done.2.refs_5_), channel_id=1, source_target_pairs={{0,12},{1,13},{2,14},{3,15},{4,8},{5,9},{6,10},{7,11},{8,4},{9,5},... | collective-permute-start | bytes 2211848 | tf_op jit(solution)/shard_map/ppermute | solution.py:365
  101.1 4.1 %all-to-all-start.1 = ((bf16[4,144,384]{2,1,0:T(8,128)(2,1)}), bf16[4,144,384]{2,1,0:T(8,128)(2,1)}, u32[]{:S(2)}, u32[]{:S(2)}) async-start(bf16[4,144,384]{2,1,0:T(8,128)(2,1)} %copy-done.5), calls=%async_computation.1 | async-start | bytes 884736 | tf_op jit(solution)/shard_map/all_to_all | solution.py:424
  105.3 15.8 %collective-permute-done.8.refs_7_ = bf16[4,144,640]{2,1,0:T(8,128)(2,1)} collective-permute-done((bf16[4,144,640]{2,1,0:T(8,128)(2,1)}, bf16[4,144,640]{2,1,0:T(8,128)(2,1)}, u32[]{:S(2)}, u32[]{:S(2)}) %collective-permute-start.8) | collective-permute-done | bytes 737312 | tf_op jit(solution)/shard_map/ppermute | solution.py:365
  122.3 11.6 %state.1 = f32[8,80,128]{2,1,0:T(8,128)S(1)} custom-call(s32[32]{0:T(128)S(1)} %pad_add_fusion.place_ref, s32[4]{0:T(128)S(1)} %get-tuple-element.19.live_ref, bf16[384,2304]{1,0:T(8,128)(2,1)S(1)} %bitcast.18, bf16[384,2304]{1,0:T(8,128)(2,1)} %collective-permute-done.refs_1_, bf16[384,2304]{1,0:T(8,128)(2,1)S(1)} %collective-permute-done.1.refs_2_, ...), custom_call_target="tpu_custom_call" | custom-call | tf_op jit(solution)/shard_map/state/pallas_call | solution.py:301
  134.6 6.7 %all-to-all-start.2 = ((f32[8,80,128]{2,1,0:T(8,128)}), f32[8,80,128]{2,1,0:T(8,128)}, u32[]{:S(2)}, u32[]{:S(2)}) async-start(f32[8,80,128]{2,1,0:T(8,128)} %copy-done.1), calls=%async_computation.2 | async-start | bytes 655360 | tf_op jit(solution)/shard_map/all_to_all | solution.py:444
  141.3 2.2 %collective-permute-start.5 = (bf16[4,144,384]{2,1,0:T(8,128)(2,1)}, bf16[4,144,384]{2,1,0:T(8,128)(2,1)S(1)}, u32[]{:S(2)}, u32[]{:S(2)}) collective-permute-start(bf16[4,144,384]{2,1,0:T(8,128)(2,1)} %all-to-all-done.1.refs_4_), channel_id=1, source_target_pairs={{0,1},{1,0},{2,3},{3,2},{4,5},{5,4},{6,7},{7,6},{8,9},{9,8},{10,11... | collective-permute-start | bytes 1327112 | tf_op jit(solution)/shard_map/ppermute | solution.py:365
  143.5 3.3 %collective-permute-start.6 = (bf16[4,144,384]{2,1,0:T(8,128)(2,1)}, bf16[4,144,384]{2,1,0:T(8,128)(2,1)S(1)}, u32[]{:S(2)}, u32[]{:S(2)}) collective-permute-start(bf16[4,144,384]{2,1,0:T(8,128)(2,1)} %all-to-all-done.1.refs_4_), channel_id=1, source_target_pairs={{0,3},{1,2},{2,1},{3,0},{4,7},{5,6},{6,5},{7,4},{8,11},{9,10},{10,... | collective-permute-start | bytes 1327112 | tf_op jit(solution)/shard_map/ppermute | solution.py:365
  146.8 6.8 %collective-permute-done.5.refs_5_ = bf16[4,144,384]{2,1,0:T(8,128)(2,1)S(1)} collective-permute-done((bf16[4,144,384]{2,1,0:T(8,128)(2,1)}, bf16[4,144,384]{2,1,0:T(8,128)(2,1)S(1)}, u32[]{:S(2)}, u32[]{:S(2)}) %collective-permute-start.5) | collective-permute-done | bytes 442400 | tf_op jit(solution)/shard_map/ppermute | solution.py:365
  153.6 3.3 %collective-permute-start.7 = (bf16[4,144,384]{2,1,0:T(8,128)(2,1)S(1)}, bf16[4,144,384]{2,1,0:T(8,128)(2,1)S(1)}, u32[]{:S(2)}, u32[]{:S(2)}) collective-permute-start(bf16[4,144,384]{2,1,0:T(8,128)(2,1)S(1)} %collective-permute-done.5.refs_5_), channel_id=1, source_target_pairs={{0,3},{1,2},{2,1},{3,0},{4,7},{5,6},{6,5},{7,4},{8,11},{9,10},{10,... | collective-permute-start | bytes 1327112 | tf_op jit(solution)/shard_map/ppermute | solution.py:365
  157.0 9.1 %collective-permute-done.7.refs_7_ = bf16[4,144,384]{2,1,0:T(8,128)(2,1)S(1)} collective-permute-done((bf16[4,144,384]{2,1,0:T(8,128)(2,1)S(1)}, bf16[4,144,384]{2,1,0:T(8,128)(2,1)S(1)}, u32[]{:S(2)}, u32[]{:S(2)}) %collective-permute-start.7) | collective-permute-done | bytes 442400 | tf_op jit(solution)/shard_map/ppermute | solution.py:365
  166.1 7.9 %queries.1.query_ref = f32[1536,384]{1,0:T(8,128)S(1)} custom-call(s32[32]{0:T(128)S(1)} %pad_add_fusion.place_ref, bf16[384,2304]{1,0:T(8,128)(2,1)S(1)} %bitcast.19, bf16[384,2304]{1,0:T(8,128)(2,1)} %collective-permute-done.refs_1_, bf16[384,2304]{1,0:T(8,128)(2,1)S(1)} %collective-permute-done.1.refs_2_, ...), custom_call_target="tpu_custom_call" | custom-call | flops 2717908992 | bytes 11206656 | tf_op jit(solution)/shard_map/queries/pallas_call | solution.py:322
  175.4 6.0 %attend.1 = bf16[4,864,128]{2,1,0:T(8,128)(2,1)} custom-call(s32[4]{0:T(128)} %get-tuple-element.18.slot_ref, s32[4]{0:T(128)} %copy-done.6, f32[1536,384]{1,0:T(8,128)} %copy-done, f32[8,80,128]{2,1,0:T(8,128)} %all-to-all-done.2.state_ref), custom_call_target="tpu_custom_call" | custom-call | tf_op jit(solution)/shard_map/attend/pallas_call | solution.py:346
  181.3 18.5 %all_to_all.20.packed_ref = bf16[4,864,128]{2,1,0:T(8,128)(2,1)S(1)} all-to-all(bf16[4,864,128]{2,1,0:T(8,128)(2,1)} %attend.1), channel_id=1, replica_groups={{0,16,32,48},{64,80,96,112},{128,144,160,176},{192,208,224,240},{256,27..., dimensions={0} | all-to-all | bytes 1769472 | tf_op jit(solution)/shard_map/all_to_all | solution.py:448
  (45 shorter events, 12.9 us)
Async XLA Ops:
  0.0 44.3 %copy-start.8 = (bf16[2240]{0:T(1024)(128)(2,1)S(1)}, bf16[2240]{0:T(1024)(128)(2,1)}, u32[]{:S(2)}) copy-start(bf16[2240]{0:T(1024)(128)(2,1)} %param.11) | copy-start | bytes 13444
  41.1 3.2 %copy-start.7 = (bf16[1,2240]{1,0:T(2,128)(2,1)S(1)}, bf16[1,2240]{1,0:T(2,128)(2,1)}, u32[]{:S(2)}) copy-start(bf16[1,2240]{1,0:T(2,128)(2,1)} %param.12) | copy-start | bytes 13444
  41.1 3.3 %copy-start.9 = (bf16[2240]{0:T(1024)(128)(2,1)S(1)}, bf16[2240]{0:T(1024)(128)(2,1)}, u32[]{:S(2)}) copy-start(bf16[2240]{0:T(1024)(128)(2,1)} %param.13) | copy-start | bytes 13444
  41.4 5.5 %copy-start.2 = (bf16[4,144,640]{2,1,0:T(8,128)(2,1)}, bf16[4,144,640]{2,1,0:T(8,128)(2,1)S(1)}, u32[]{:S(2)}) copy-start(bf16[4,144,640]{2,1,0:T(8,128)(2,1)S(1)} %get-tuple-element.17) | copy-start | bytes 2211844
  41.4 5.5 %copy-start.5 = (bf16[4,144,384]{2,1,0:T(8,128)(2,1)}, bf16[4,144,384]{2,1,0:T(8,128)(2,1)S(1)}, u32[]{:S(2)}) copy-start(bf16[4,144,384]{2,1,0:T(8,128)(2,1)S(1)} %get-tuple-element.24) | copy-start | bytes 1327108
  50.4 7.7 %copy-start.10 = (s32[16]{0:T(128)S(1)}, s32[16]{0:T(128)}, u32[]{:S(2)}) copy-start(s32[16]{0:T(128)} %constant.62.clone) | copy-start | bytes 196
  50.5 7.7 %copy-start.11 = (s32[16]{0:T(128)S(1)}, s32[16]{0:T(128)}, u32[]{:S(2)}) copy-start(s32[16]{0:T(128)} %constant.63.clone) | copy-start | bytes 196
  50.5 7.7 %copy-start.12 = (s32[16]{0:T(128)S(1)}, s32[16]{0:T(128)}, u32[]{:S(2)}) copy-start(s32[16]{0:T(128)} %constant.64.clone) | copy-start | bytes 196
  51.4 41.9 %collective-permute-start.1 = (bf16[384,2304]{1,0:T(8,128)(2,1)S(1)}, bf16[384,2304]{1,0:T(8,128)(2,1)S(1)}, u32[]{:S(2)}, u32[]{:S(2)}) collective-permute-start(bf16[384,2304]{1,0:T(8,128)(2,1)S(1)} %bitcast.16), channel_id=1, source_target_pairs={{0,32},{16,48},{32,0},{48,16},{64,96},{80,112},{96,64},{112,80},{1... | collective-permute-start | bytes 5308424 | tf_op jit(solution)/shard_map/ppermute | solution.py:365
  53.3 15.8 %all-to-all-start = ((bf16[4,144,640]{2,1,0:T(8,128)(2,1)}), bf16[4,144,640]{2,1,0:T(8,128)(2,1)}, u32[]{:S(2)}, u32[]{:S(2)}) async-start(bf16[4,144,640]{2,1,0:T(8,128)(2,1)} %copy-done.2), calls=%async_computation | async-start | bytes 1474560 | tf_op jit(solution)/shard_map/all_to_all | solution.py:410
  58.9 75.0 %copy-start.6 = (s32[4]{0:T(128)}, s32[4]{0:T(128)S(1)}, u32[]{:S(2)}) copy-start(s32[4]{0:T(128)S(1)} %get-tuple-element.19.live_ref) | copy-start | bytes 52
  69.1 19.1 %collective-permute-start.2 = (bf16[4,144,640]{2,1,0:T(8,128)(2,1)}, bf16[4,144,640]{2,1,0:T(8,128)(2,1)}, u32[]{:S(2)}, u32[]{:S(2)}) collective-permute-start(bf16[4,144,640]{2,1,0:T(8,128)(2,1)} %all-to-all-done.refs_4_), channel_id=1, source_target_pairs={{0,4},{1,5},{2,6},{3,7},{4,0},{5,1},{6,2},{7,3},{8,12},{9,13},{10,... | collective-permute-start | bytes 2211848 | tf_op jit(solution)/shard_map/ppermute | solution.py:365
  72.3 19.9 %collective-permute-start.3 = (bf16[4,144,640]{2,1,0:T(8,128)(2,1)}, bf16[4,144,640]{2,1,0:T(8,128)(2,1)S(1)}, u32[]{:S(2)}, u32[]{:S(2)}) collective-permute-start(bf16[4,144,640]{2,1,0:T(8,128)(2,1)} %all-to-all-done.refs_4_), channel_id=1, source_target_pairs={{0,12},{1,13},{2,14},{3,15},{4,8},{5,9},{6,10},{7,11},{8,4},{9,5},... | collective-permute-start | bytes 2211848 | tf_op jit(solution)/shard_map/ppermute | solution.py:365
  76.1 29.1 %collective-permute-start = (bf16[384,2304]{1,0:T(8,128)(2,1)S(1)}, bf16[384,2304]{1,0:T(8,128)(2,1)}, u32[]{:S(2)}, u32[]{:S(2)}) collective-permute-start(bf16[384,2304]{1,0:T(8,128)(2,1)S(1)} %bitcast.17), channel_id=1, source_target_pairs={{0,16},{16,0},{32,48},{48,32},{64,80},{80,64},{96,112},{112,96},{1... | collective-permute-start | bytes 5308424 | tf_op jit(solution)/shard_map/ppermute | solution.py:365
  92.3 0.9 copy-start.3
  93.3 27.9 %collective-permute-start.4 = (bf16[384,2304]{1,0:T(8,128)(2,1)S(1)}, bf16[384,2304]{1,0:T(8,128)(2,1)}, u32[]{:S(2)}, u32[]{:S(2)}) collective-permute-start(bf16[384,2304]{1,0:T(8,128)(2,1)S(1)} %collective-permute-done.1.refs_2_), channel_id=1, source_target_pairs={{0,16},{16,0},{32,48},{48,32},{64,80},{80,64},{96,112},{112,96},{1... | collective-permute-start | bytes 5308424 | tf_op jit(solution)/shard_map/ppermute | solution.py:365
  97.3 23.8 %collective-permute-start.8 = (bf16[4,144,640]{2,1,0:T(8,128)(2,1)}, bf16[4,144,640]{2,1,0:T(8,128)(2,1)}, u32[]{:S(2)}, u32[]{:S(2)}) collective-permute-start(bf16[4,144,640]{2,1,0:T(8,128)(2,1)} %collective-permute-done.2.refs_5_), channel_id=1, source_target_pairs={{0,12},{1,13},{2,14},{3,15},{4,8},{5,9},{6,10},{7,11},{8,4},{9,5},... | collective-permute-start | bytes 2211848 | tf_op jit(solution)/shard_map/ppermute | solution.py:365
  101.1 33.4 %all-to-all-start.1 = ((bf16[4,144,384]{2,1,0:T(8,128)(2,1)}), bf16[4,144,384]{2,1,0:T(8,128)(2,1)}, u32[]{:S(2)}, u32[]{:S(2)}) async-start(bf16[4,144,384]{2,1,0:T(8,128)(2,1)} %copy-done.5), calls=%async_computation.1 | async-start | bytes 884736 | tf_op jit(solution)/shard_map/all_to_all | solution.py:424
  121.1 1.1 copy-start.4
  134.6 40.8 %all-to-all-start.2 = ((f32[8,80,128]{2,1,0:T(8,128)}), f32[8,80,128]{2,1,0:T(8,128)}, u32[]{:S(2)}, u32[]{:S(2)}) async-start(f32[8,80,128]{2,1,0:T(8,128)} %copy-done.1), calls=%async_computation.2 | async-start | bytes 655360 | tf_op jit(solution)/shard_map/all_to_all | solution.py:444
  141.3 12.3 %collective-permute-start.5 = (bf16[4,144,384]{2,1,0:T(8,128)(2,1)}, bf16[4,144,384]{2,1,0:T(8,128)(2,1)S(1)}, u32[]{:S(2)}, u32[]{:S(2)}) collective-permute-start(bf16[4,144,384]{2,1,0:T(8,128)(2,1)} %all-to-all-done.1.refs_4_), channel_id=1, source_target_pairs={{0,1},{1,0},{2,3},{3,2},{4,5},{5,4},{6,7},{7,6},{8,9},{9,8},{10,11... | collective-permute-start | bytes 1327112 | tf_op jit(solution)/shard_map/ppermute | solution.py:365
  143.5 13.4 %collective-permute-start.6 = (bf16[4,144,384]{2,1,0:T(8,128)(2,1)}, bf16[4,144,384]{2,1,0:T(8,128)(2,1)S(1)}, u32[]{:S(2)}, u32[]{:S(2)}) collective-permute-start(bf16[4,144,384]{2,1,0:T(8,128)(2,1)} %all-to-all-done.1.refs_4_), channel_id=1, source_target_pairs={{0,3},{1,2},{2,1},{3,0},{4,7},{5,6},{6,5},{7,4},{8,11},{9,10},{10,... | collective-permute-start | bytes 1327112 | tf_op jit(solution)/shard_map/ppermute | solution.py:365
  153.6 12.4 %collective-permute-start.7 = (bf16[4,144,384]{2,1,0:T(8,128)(2,1)S(1)}, bf16[4,144,384]{2,1,0:T(8,128)(2,1)S(1)}, u32[]{:S(2)}, u32[]{:S(2)}) collective-permute-start(bf16[4,144,384]{2,1,0:T(8,128)(2,1)S(1)} %collective-permute-done.5.refs_5_), channel_id=1, source_target_pairs={{0,3},{1,2},{2,1},{3,0},{4,7},{5,6},{6,5},{7,4},{8,11},{9,10},{10,... | collective-permute-start | bytes 1327112 | tf_op jit(solution)/shard_map/ppermute | solution.py:365
  173.9 1.4 copy-start
  (1 other events, 0.7 us)

commit v7 on v6

--- a/solution.py
+++ b/solution.py
@@ -403,7 +403,7 @@
             jax.ShapeDtypeStruct((side, padded, wide), jnp.bfloat16),
             jax.ShapeDtypeStruct((side, padded, main + LANES), jnp.bfloat16),
         ],
-        compiler_params=pltpu.CompilerParams(vmem_limit_bytes=16 * 1024 * 1024),
+        compiler_params=pltpu.CompilerParams(vmem_limit_bytes=58 * 1024 * 1024),
         name="layout",
     )(rank.reshape(1).astype(jnp.int32), gathered)
     first, tokens = lax.optimization_barrier((first, tokens))
@@ -440,7 +440,8 @@
     across = exchange(late, 1, "seq", seq_size)
     hidden = (mine, exchange(mine, 1, "seq", seq_size), beside, across)
 
-    part = compute_state(place, live, hidden, first_pieces, teams)
+    part = compute_state(place, live, hidden, first_pieces, 1)
+    part = jnp.broadcast_to(part, (teams,) + part.shape[1:])
     state = lax.all_to_all(part, "seq", 0, 0, axis_index_groups=same_rank)
     queries = compute_queries(place, hidden, second_pieces)
 

time: 202 us -> 202 us (level)
  other arithmetic: 5.46 us -> 2.39 us
  blocking collectives: 59.6 us -> 62.2 us
  Pallas kernels: 26.9 us -> 29.3 us
    all_gather x1, blocking collectives: 41.1 us -> 43.8 us  [body(): gathered = lax.all_gather(w_qkv, 'seq', axis=0)]
    pallas_call x1, Pallas kernels: 0.26 us -> 2.58 us  [body(): pl.pallas_call(functools.partial(layout_kernel, layout_plan(w_qkv.shape[1...]
    unnamed x26 -> x24, local copies, waits for them, and re-layouts: 4.17 us -> 4.05 us
where the time goes in v7:
time: 202 us; the launch traced here: 201 us
  blocking collectives  62.2 us (31%)
  waiting for transfers between devices  54.7 us (27%)
  starting transfers between devices  44.3 us (22%)
  Pallas kernels  29.3 us (15%)
  local copies, waits for them, and re-layouts  6.96 us (3%)
  other arithmetic  2.39 us (1%)
    ppermute x9, waiting for transfers between devices, exchange(): return lax.ppermute(block, axis, [(i, i ^ mask) for i in range(count)])  44.4 us
    all_gather x1, blocking collectives, body(): gathered = lax.all_gather(w_qkv, 'seq', axis=0)  43.8 us
    ppermute x9, starting transfers between devices, exchange(): return lax.ppermute(block, axis, [(i, i ^ mask) for i in range(count)])  29.2 us
    all_to_all x1, blocking collectives, body(): result = lax.all_to_all(result, 'seq', 0, 0, axis_index_groups=team)  18.5 us
    pallas_call x1, Pallas kernels, compute_state(): pl.pallas_call(state_kernel, in_specs=[SMEM, SMEM] + [HBM] * (TEAM + len(...  11.6 us
    all_to_all x1, waiting for transfers between devices, body(): first_near = lax.all_to_all(first, 'img', 0, 0, axis_index_groups=x_groups)  10.3 us
    pallas_call x1, Pallas kernels, compute_queries(): pl.pallas_call(query_kernel, in_specs=[SMEM] + [HBM] * (TEAM + len(second...  7.88 us
    all_to_all x1, starting transfers between devices, body(): state = lax.all_to_all(part, 'seq', 0, 0, axis_index_groups=same_rank)  6.73 us
  transfers between devices with their start and end apart: 12, of which 7 were waited for; matrix products, arithmetic and copies ran while one was open for 0% of the time, Pallas kernels for 10%

profile of v7, /device:TPU:1, one launch (start us, length us, event | category | flops | bytes accessed | tf_op | source)
XLA Modules:
  0.0 201.4 jit_solution(4597016272079896592)
XLA Ops:
  0.0 43.8 %all-gather.1.gathered_ref = bf16[32,140,108]{2,1,0:T(8,128)(2,1)} all-gather(bf16[1,140,108]{2,1,0:T(8,128)(2,1)} %bitcast.23), channel_id=2, replica_groups=mesh['seq'=32,'img'=16] {'seq'}, dimensions={0}, use_global_device_ids=true | all-gather | bytes 997920 | tf_op jit(solution)/shard_map/all_gather | solution.py:396
  43.8 2.6 %layout.1 = (bf16[4,144,640]{2,1,0:T(8,128)(2,1)}, bf16[4,144,384]{2,1,0:T(8,128)(2,1)}) custom-call(s32[1]{0:T(128)} %bitcast.rank_ref, bf16[32,140,108]{2,1,0:T(8,128)(2,1)} %all-gather.1.gathered_ref), custom_call_target="tpu_custom_call" | custom-call | tf_op jit(solution)/shard_map/layout/pallas_call | solution.py:398
  50.3 1.9 collective-permute-start.1
  52.2 4.2 %all-to-all-start = ((bf16[4,144,640]{2,1,0:T(8,128)(2,1)}), bf16[4,144,640]{2,1,0:T(8,128)(2,1)}, u32[]{:S(2)}, u32[]{:S(2)}) async-start(bf16[4,144,640]{2,1,0:T(8,128)(2,1)} %get-tuple-element.17), calls=%async_computation | async-start | bytes 1474560 | tf_op jit(solution)/shard_map/all_to_all | solution.py:410
  57.8 10.3 %all-to-all-done.refs_4_ = bf16[4,144,640]{2,1,0:T(8,128)(2,1)} async-done(((bf16[4,144,640]{2,1,0:T(8,128)(2,1)}), bf16[4,144,640]{2,1,0:T(8,128)(2,1)}, u32[]{:S(2)}, u32[]{:S(2)}) %all-to-all-start) | async-done | bytes 737312 | tf_op jit(solution)/shard_map/all_to_all | solution.py:410
  68.0 3.2 %collective-permute-start.2 = (bf16[4,144,640]{2,1,0:T(8,128)(2,1)}, bf16[4,144,640]{2,1,0:T(8,128)(2,1)}, u32[]{:S(2)}, u32[]{:S(2)}) collective-permute-start(bf16[4,144,640]{2,1,0:T(8,128)(2,1)} %all-to-all-done.refs_4_), channel_id=1, source_target_pairs={{0,4},{1,5},{2,6},{3,7},{4,0},{5,1},{6,2},{7,3},{8,12},{9,13},{10,... | collective-permute-start | bytes 2211848 | tf_op jit(solution)/shard_map/ppermute | solution.py:365
  71.2 3.8 %collective-permute-start.3 = (bf16[4,144,640]{2,1,0:T(8,128)(2,1)}, bf16[4,144,640]{2,1,0:T(8,128)(2,1)S(1)}, u32[]{:S(2)}, u32[]{:S(2)}) collective-permute-start(bf16[4,144,640]{2,1,0:T(8,128)(2,1)} %all-to-all-done.refs_4_), channel_id=1, source_target_pairs={{0,12},{1,13},{2,14},{3,15},{4,8},{5,9},{6,10},{7,11},{8,4},{9,5},... | collective-permute-start | bytes 2211848 | tf_op jit(solution)/shard_map/ppermute | solution.py:365
  75.1 3.6 %collective-permute-start = (bf16[384,2304]{1,0:T(8,128)(2,1)S(1)}, bf16[384,2304]{1,0:T(8,128)(2,1)}, u32[]{:S(2)}, u32[]{:S(2)}) collective-permute-start(bf16[384,2304]{1,0:T(8,128)(2,1)S(1)} %bitcast.18), channel_id=1, source_target_pairs={{0,16},{16,0},{32,48},{48,32},{64,80},{80,64},{96,112},{112,96},{1... | collective-permute-start | bytes 5308424 | tf_op jit(solution)/shard_map/ppermute | solution.py:365
  78.7 8.4 %collective-permute-done.2.refs_5_ = bf16[4,144,640]{2,1,0:T(8,128)(2,1)} collective-permute-done((bf16[4,144,640]{2,1,0:T(8,128)(2,1)}, bf16[4,144,640]{2,1,0:T(8,128)(2,1)}, u32[]{:S(2)}, u32[]{:S(2)}) %collective-permute-start.2) | collective-permute-done | bytes 737312 | tf_op jit(solution)/shard_map/ppermute | solution.py:365
  87.1 4.0 %collective-permute-done.3.refs_6_ = bf16[4,144,640]{2,1,0:T(8,128)(2,1)S(1)} collective-permute-done((bf16[4,144,640]{2,1,0:T(8,128)(2,1)}, bf16[4,144,640]{2,1,0:T(8,128)(2,1)S(1)}, u32[]{:S(2)}, u32[]{:S(2)}) %collective-permute-start.3) | collective-permute-done | bytes 737312 | tf_op jit(solution)/shard_map/ppermute | solution.py:365
  92.2 4.0 %collective-permute-start.4 = (bf16[384,2304]{1,0:T(8,128)(2,1)S(1)}, bf16[384,2304]{1,0:T(8,128)(2,1)}, u32[]{:S(2)}, u32[]{:S(2)}) collective-permute-start(bf16[384,2304]{1,0:T(8,128)(2,1)S(1)} %collective-permute-done.1.refs_2_), channel_id=1, source_target_pairs={{0,16},{16,0},{32,48},{48,32},{64,80},{80,64},{96,112},{112,96},{1... | collective-permute-start | bytes 5308424 | tf_op jit(solution)/shard_map/ppermute | solution.py:365
  96.2 3.8 %collective-permute-start.8 = (bf16[4,144,640]{2,1,0:T(8,128)(2,1)}, bf16[4,144,640]{2,1,0:T(8,128)(2,1)}, u32[]{:S(2)}, u32[]{:S(2)}) collective-permute-start(bf16[4,144,640]{2,1,0:T(8,128)(2,1)} %collective-permute-done.2.refs_5_), channel_id=1, source_target_pairs={{0,12},{1,13},{2,14},{3,15},{4,8},{5,9},{6,10},{7,11},{8,4},{9,5},... | collective-permute-start | bytes 2211848 | tf_op jit(solution)/shard_map/ppermute | solution.py:365
  100.0 4.1 %all-to-all-start.1 = ((bf16[4,144,384]{2,1,0:T(8,128)(2,1)}), bf16[4,144,384]{2,1,0:T(8,128)(2,1)}, u32[]{:S(2)}, u32[]{:S(2)}) async-start(bf16[4,144,384]{2,1,0:T(8,128)(2,1)} %get-tuple-element.24), calls=%async_computation.1 | async-start | bytes 884736 | tf_op jit(solution)/shard_map/all_to_all | solution.py:424
  104.2 15.9 %collective-permute-done.8.refs_7_ = bf16[4,144,640]{2,1,0:T(8,128)(2,1)} collective-permute-done((bf16[4,144,640]{2,1,0:T(8,128)(2,1)}, bf16[4,144,640]{2,1,0:T(8,128)(2,1)}, u32[]{:S(2)}, u32[]{:S(2)}) %collective-permute-start.8) | collective-permute-done | bytes 737312 | tf_op jit(solution)/shard_map/ppermute | solution.py:365
  121.2 11.6 %state.1 = f32[1,80,128]{2,1,0:T(8,128)S(1)} custom-call(s32[32]{0:T(128)S(1)} %pad_add_fusion.place_ref, s32[4]{0:T(128)S(1)} %get-tuple-element.19.live_ref, bf16[384,2304]{1,0:T(8,128)(2,1)S(1)} %bitcast.19, bf16[384,2304]{1,0:T(8,128)(2,1)} %collective-permute-done.refs_1_, bf16[384,2304]{1,0:T(8,128)(2,1)S(1)} %collective-permute-done.1.refs_2_, ...), custom_call_target="tpu_custom_call" | custom-call | tf_op jit(solution)/shard_map/state/pallas_call | solution.py:301
  134.9 6.7 %all-to-all-start.2 = ((f32[8,80,128]{2,1,0:T(8,128)}), f32[8,80,128]{2,1,0:T(8,128)}, u32[]{:S(2)}, u32[]{:S(2)}) async-start(f32[8,80,128]{2,1,0:T(8,128)} %broadcast_in_dim.5), calls=%async_computation.2 | async-start | bytes 655360 | tf_op jit(solution)/shard_map/all_to_all | solution.py:445
  141.6 2.2 %collective-permute-start.5 = (bf16[4,144,384]{2,1,0:T(8,128)(2,1)}, bf16[4,144,384]{2,1,0:T(8,128)(2,1)S(1)}, u32[]{:S(2)}, u32[]{:S(2)}) collective-permute-start(bf16[4,144,384]{2,1,0:T(8,128)(2,1)} %all-to-all-done.1.refs_4_), channel_id=1, source_target_pairs={{0,1},{1,0},{2,3},{3,2},{4,5},{5,4},{6,7},{7,6},{8,9},{9,8},{10,11... | collective-permute-start | bytes 1327112 | tf_op jit(solution)/shard_map/ppermute | solution.py:365
  143.8 3.3 %collective-permute-start.6 = (bf16[4,144,384]{2,1,0:T(8,128)(2,1)}, bf16[4,144,384]{2,1,0:T(8,128)(2,1)S(1)}, u32[]{:S(2)}, u32[]{:S(2)}) collective-permute-start(bf16[4,144,384]{2,1,0:T(8,128)(2,1)} %all-to-all-done.1.refs_4_), channel_id=1, source_target_pairs={{0,3},{1,2},{2,1},{3,0},{4,7},{5,6},{6,5},{7,4},{8,11},{9,10},{10,... | collective-permute-start | bytes 1327112 | tf_op jit(solution)/shard_map/ppermute | solution.py:365
  147.1 6.8 %collective-permute-done.5.refs_5_ = bf16[4,144,384]{2,1,0:T(8,128)(2,1)S(1)} collective-permute-done((bf16[4,144,384]{2,1,0:T(8,128)(2,1)}, bf16[4,144,384]{2,1,0:T(8,128)(2,1)S(1)}, u32[]{:S(2)}, u32[]{:S(2)}) %collective-permute-start.5) | collective-permute-done | bytes 442400 | tf_op jit(solution)/shard_map/ppermute | solution.py:365
  153.9 3.3 %collective-permute-start.7 = (bf16[4,144,384]{2,1,0:T(8,128)(2,1)S(1)}, bf16[4,144,384]{2,1,0:T(8,128)(2,1)S(1)}, u32[]{:S(2)}, u32[]{:S(2)}) collective-permute-start(bf16[4,144,384]{2,1,0:T(8,128)(2,1)S(1)} %collective-permute-done.5.refs_5_), channel_id=1, source_target_pairs={{0,3},{1,2},{2,1},{3,0},{4,7},{5,6},{6,5},{7,4},{8,11},{9,10},{10,... | collective-permute-start | bytes 1327112 | tf_op jit(solution)/shard_map/ppermute | solution.py:365
  157.3 9.1 %collective-permute-done.7.refs_7_ = bf16[4,144,384]{2,1,0:T(8,128)(2,1)S(1)} collective-permute-done((bf16[4,144,384]{2,1,0:T(8,128)(2,1)S(1)}, bf16[4,144,384]{2,1,0:T(8,128)(2,1)S(1)}, u32[]{:S(2)}, u32[]{:S(2)}) %collective-permute-start.7) | collective-permute-done | bytes 442400 | tf_op jit(solution)/shard_map/ppermute | solution.py:365
  166.4 7.9 %queries.1.query_ref = f32[1536,384]{1,0:T(8,128)S(1)} custom-call(s32[32]{0:T(128)S(1)} %pad_add_fusion.place_ref, bf16[384,2304]{1,0:T(8,128)(2,1)S(1)} %bitcast.20, bf16[384,2304]{1,0:T(8,128)(2,1)} %collective-permute-done.refs_1_, bf16[384,2304]{1,0:T(8,128)(2,1)S(1)} %collective-permute-done.1.refs_2_, ...), custom_call_target="tpu_custom_call" | custom-call | flops 2717908992 | bytes 11206656 | tf_op jit(solution)/shard_map/queries/pallas_call | solution.py:322
  175.7 6.0 %attend.1 = bf16[4,864,128]{2,1,0:T(8,128)(2,1)} custom-call(s32[4]{0:T(128)} %get-tuple-element.18.slot_ref, s32[4]{0:T(128)} %copy-done.4, f32[1536,384]{1,0:T(8,128)} %copy-done, f32[8,80,128]{2,1,0:T(8,128)} %all-to-all-done.2.state_ref), custom_call_target="tpu_custom_call" | custom-call | tf_op jit(solution)/shard_map/attend/pallas_call | solution.py:346
  181.7 18.5 %all_to_all.20.packed_ref = bf16[4,864,128]{2,1,0:T(8,128)(2,1)S(1)} all-to-all(bf16[4,864,128]{2,1,0:T(8,128)(2,1)} %attend.1), channel_id=1, replica_groups={{0,16,32,48},{64,80,96,112},{128,144,160,176},{192,208,224,240},{256,27..., dimensions={0} | all-to-all | bytes 1769472 | tf_op jit(solution)/shard_map/all_to_all | solution.py:449
  (44 shorter events, 10.8 us)
Async XLA Ops:
  0.0 46.4 %copy-start.5 = (bf16[1,3,128,2240]{2,3,1,0:T(8,128)(2,1)S(1)}, bf16[1,3,128,2240]{2,3,1,0:T(8,128)(2,1)}, u32[]{:S(2)}) copy-start(bf16[1,3,128,2240]{2,3,1,0:T(8,128)(2,1)} %param.10) | copy-start | bytes 5160964
  0.0 47.4 %copy-start.7 = (bf16[2240]{0:T(1024)(128)(2,1)S(1)}, bf16[2240]{0:T(1024)(128)(2,1)}, u32[]{:S(2)}) copy-start(bf16[2240]{0:T(1024)(128)(2,1)} %param.11) | copy-start | bytes 13444
  43.8 3.6 %copy-start.6 = (bf16[1,2240]{1,0:T(2,128)(2,1)S(1)}, bf16[1,2240]{1,0:T(2,128)(2,1)}, u32[]{:S(2)}) copy-start(bf16[1,2240]{1,0:T(2,128)(2,1)} %param.12) | copy-start | bytes 13444
  43.8 3.7 %copy-start.8 = (bf16[2240]{0:T(1024)(128)(2,1)S(1)}, bf16[2240]{0:T(1024)(128)(2,1)}, u32[]{:S(2)}) copy-start(bf16[2240]{0:T(1024)(128)(2,1)} %param.13) | copy-start | bytes 13444
  49.3 7.7 %copy-start.9 = (s32[16]{0:T(128)S(1)}, s32[16]{0:T(128)}, u32[]{:S(2)}) copy-start(s32[16]{0:T(128)} %constant.62.clone) | copy-start | bytes 196
  49.4 7.7 %copy-start.10 = (s32[16]{0:T(128)S(1)}, s32[16]{0:T(128)}, u32[]{:S(2)}) copy-start(s32[16]{0:T(128)} %constant.63.clone) | copy-start | bytes 196
  49.4 7.7 %copy-start.11 = (s32[16]{0:T(128)S(1)}, s32[16]{0:T(128)}, u32[]{:S(2)}) copy-start(s32[16]{0:T(128)} %constant.64.clone) | copy-start | bytes 196
  50.3 41.9 %collective-permute-start.1 = (bf16[384,2304]{1,0:T(8,128)(2,1)S(1)}, bf16[384,2304]{1,0:T(8,128)(2,1)S(1)}, u32[]{:S(2)}, u32[]{:S(2)}) collective-permute-start(bf16[384,2304]{1,0:T(8,128)(2,1)S(1)} %bitcast.17), channel_id=1, source_target_pairs={{0,32},{16,48},{32,0},{48,16},{64,96},{80,112},{96,64},{112,80},{1... | collective-permute-start | bytes 5308424 | tf_op jit(solution)/shard_map/ppermute | solution.py:365
  52.2 15.8 %all-to-all-start = ((bf16[4,144,640]{2,1,0:T(8,128)(2,1)}), bf16[4,144,640]{2,1,0:T(8,128)(2,1)}, u32[]{:S(2)}, u32[]{:S(2)}) async-start(bf16[4,144,640]{2,1,0:T(8,128)(2,1)} %get-tuple-element.17), calls=%async_computation | async-start | bytes 1474560 | tf_op jit(solution)/shard_map/all_to_all | solution.py:410
  57.8 75.0 %copy-start.4 = (s32[4]{0:T(128)}, s32[4]{0:T(128)S(1)}, u32[]{:S(2)}) copy-start(s32[4]{0:T(128)S(1)} %get-tuple-element.19.live_ref) | copy-start | bytes 52
  68.0 19.1 %collective-permute-start.2 = (bf16[4,144,640]{2,1,0:T(8,128)(2,1)}, bf16[4,144,640]{2,1,0:T(8,128)(2,1)}, u32[]{:S(2)}, u32[]{:S(2)}) collective-permute-start(bf16[4,144,640]{2,1,0:T(8,128)(2,1)} %all-to-all-done.refs_4_), channel_id=1, source_target_pairs={{0,4},{1,5},{2,6},{3,7},{4,0},{5,1},{6,2},{7,3},{8,12},{9,13},{10,... | collective-permute-start | bytes 2211848 | tf_op jit(solution)/shard_map/ppermute | solution.py:365
  71.2 19.9 %collective-permute-start.3 = (bf16[4,144,640]{2,1,0:T(8,128)(2,1)}, bf16[4,144,640]{2,1,0:T(8,128)(2,1)S(1)}, u32[]{:S(2)}, u32[]{:S(2)}) collective-permute-start(bf16[4,144,640]{2,1,0:T(8,128)(2,1)} %all-to-all-done.refs_4_), channel_id=1, source_target_pairs={{0,12},{1,13},{2,14},{3,15},{4,8},{5,9},{6,10},{7,11},{8,4},{9,5},... | collective-permute-start | bytes 2211848 | tf_op jit(solution)/shard_map/ppermute | solution.py:365
  75.1 29.1 %collective-permute-start = (bf16[384,2304]{1,0:T(8,128)(2,1)S(1)}, bf16[384,2304]{1,0:T(8,128)(2,1)}, u32[]{:S(2)}, u32[]{:S(2)}) collective-permute-start(bf16[384,2304]{1,0:T(8,128)(2,1)S(1)} %bitcast.18), channel_id=1, source_target_pairs={{0,16},{16,0},{32,48},{48,32},{64,80},{80,64},{96,112},{112,96},{1... | collective-permute-start | bytes 5308424 | tf_op jit(solution)/shard_map/ppermute | solution.py:365
  91.2 0.9 copy-start.1
  92.2 27.9 %collective-permute-start.4 = (bf16[384,2304]{1,0:T(8,128)(2,1)S(1)}, bf16[384,2304]{1,0:T(8,128)(2,1)}, u32[]{:S(2)}, u32[]{:S(2)}) collective-permute-start(bf16[384,2304]{1,0:T(8,128)(2,1)S(1)} %collective-permute-done.1.refs_2_), channel_id=1, source_target_pairs={{0,16},{16,0},{32,48},{48,32},{64,80},{80,64},{96,112},{112,96},{1... | collective-permute-start | bytes 5308424 | tf_op jit(solution)/shard_map/ppermute | solution.py:365
  96.2 23.8 %collective-permute-start.8 = (bf16[4,144,640]{2,1,0:T(8,128)(2,1)}, bf16[4,144,640]{2,1,0:T(8,128)(2,1)}, u32[]{:S(2)}, u32[]{:S(2)}) collective-permute-start(bf16[4,144,640]{2,1,0:T(8,128)(2,1)} %collective-permute-done.2.refs_5_), channel_id=1, source_target_pairs={{0,12},{1,13},{2,14},{3,15},{4,8},{5,9},{6,10},{7,11},{8,4},{9,5},... | collective-permute-start | bytes 2211848 | tf_op jit(solution)/shard_map/ppermute | solution.py:365
  100.0 33.3 %all-to-all-start.1 = ((bf16[4,144,384]{2,1,0:T(8,128)(2,1)}), bf16[4,144,384]{2,1,0:T(8,128)(2,1)}, u32[]{:S(2)}, u32[]{:S(2)}) async-start(bf16[4,144,384]{2,1,0:T(8,128)(2,1)} %get-tuple-element.24), calls=%async_computation.1 | async-start | bytes 884736 | tf_op jit(solution)/shard_map/all_to_all | solution.py:424
  120.1 1.1 copy-start.2
  132.8 0.6 copy-start.3
  134.9 40.8 %all-to-all-start.2 = ((f32[8,80,128]{2,1,0:T(8,128)}), f32[8,80,128]{2,1,0:T(8,128)}, u32[]{:S(2)}, u32[]{:S(2)}) async-start(f32[8,80,128]{2,1,0:T(8,128)} %broadcast_in_dim.5), calls=%async_computation.2 | async-start | bytes 655360 | tf_op jit(solution)/shard_map/all_to_all | solution.py:445
  141.6 12.3 %collective-permute-start.5 = (bf16[4,144,384]{2,1,0:T(8,128)(2,1)}, bf16[4,144,384]{2,1,0:T(8,128)(2,1)S(1)}, u32[]{:S(2)}, u32[]{:S(2)}) collective-permute-start(bf16[4,144,384]{2,1,0:T(8,128)(2,1)} %all-to-all-done.1.refs_4_), channel_id=1, source_target_pairs={{0,1},{1,0},{2,3},{3,2},{4,5},{5,4},{6,7},{7,6},{8,9},{9,8},{10,11... | collective-permute-start | bytes 1327112 | tf_op jit(solution)/shard_map/ppermute | solution.py:365
  143.8 13.4 %collective-permute-start.6 = (bf16[4,144,384]{2,1,0:T(8,128)(2,1)}, bf16[4,144,384]{2,1,0:T(8,128)(2,1)S(1)}, u32[]{:S(2)}, u32[]{:S(2)}) collective-permute-start(bf16[4,144,384]{2,1,0:T(8,128)(2,1)} %all-to-all-done.1.refs_4_), channel_id=1, source_target_pairs={{0,3},{1,2},{2,1},{3,0},{4,7},{5,6},{6,5},{7,4},{8,11},{9,10},{10,... | collective-permute-start | bytes 1327112 | tf_op jit(solution)/shard_map/ppermute | solution.py:365
  153.9 12.4 %collective-permute-start.7 = (bf16[4,144,384]{2,1,0:T(8,128)(2,1)S(1)}, bf16[4,144,384]{2,1,0:T(8,128)(2,1)S(1)}, u32[]{:S(2)}, u32[]{:S(2)}) collective-permute-start(bf16[4,144,384]{2,1,0:T(8,128)(2,1)S(1)} %collective-permute-done.5.refs_5_), channel_id=1, source_target_pairs={{0,3},{1,2},{2,1},{3,0},{4,7},{5,6},{6,5},{7,4},{8,11},{9,10},{10,... | collective-permute-start | bytes 1327112 | tf_op jit(solution)/shard_map/ppermute | solution.py:365
  174.3 1.4 copy-start
